TPU v7x, 128 devices: a whole 4x4x4 slice. The times are simulated.
128 devices in a mesh: dp: 32 (over x, z, core), tensor: 4 (over y).
Axes of the slice: x: 4, y: 4, z: 4, core: 2. Of those that a mesh axis runs over, the one named last changes fastest.
Arguments:
- hidden: bfloat16 [32768, 2560], P('dp', 'tensor'), may hold values from -6 to 6
- out_grad: bfloat16 [32768, 2560], P('dp', 'tensor'), may hold values from -6 to 6
- memory: bfloat16 [32768, 1280], P('dp'), may hold values from -6 to 6
- w_key: bfloat16 [1280, 2560], P(None, 'tensor'), may hold values from -0.15625 to 0.15625
- w_value: bfloat16 [1280, 2560], P(None, 'tensor'), may hold values from -0.15625 to 0.15625
- row_owner: int32 [32768, 8], P('dp'), may hold values from 0 to 127, all different within a row; in each aligned block of 256 rows (0 to 255, 256 to 511, ...) at most 32 rows name the same one
- row_slot: int32 [32768, 8], P('dp'), may hold values from 0 to 511
- mem_table: float32 [65536, 160], P(('dp', 'tensor')), may hold values from -6 to 6
- adagrad_sum: float32 [65536, 160], P(('dp', 'tensor')), may hold values from 0.05 to 2
Outputs:
- hidden_grad: bfloat16 [32768, 2560], P('dp', 'tensor')
- key_weight_grad: float32 [1280, 2560], P('dp', 'tensor')
- value_weight_grad: float32 [1280, 2560], P('dp', 'tensor')
- new_table: float32 [65536, 160], P(('dp', 'tensor'))
- new_sum: float32 [65536, 160], P(('dp', 'tensor'))
Inputs may be any that keep to these rules, and one draw needn't show every extreme that they name: `row_owner`: each token's 8 owners are distinct. Within a dp shard, take the tokens in order in aligned blocks of 256: in each block no owner is named more than 32 times, a bound that some owner reaches in some or all blocks. `row_slot`: A few row indices are retrieved very often.
All inputs are finite; a program needn't handle non-finite values.
Results may differ from a plain program's by a relative error of at most 0.0034.
Values sent between devices are 32-bit elements; how exact they have to be, the bound alone decides.
No kernel may reach another device: no remote copies, remote signals or barrier semaphores. Data moves between devices by JAX's collectives and lax.ppermute only.
A program may use at most 128 MiB of HBM per device.

v0:
```python
import math

import jax
import jax.numpy as jnp
from jax import lax
from jax.sharding import PartitionSpec as P

D = 2560


LEARN_RATE = 0.5
EPSILON = 1e-06


def sent_to_all(value, axis):
    copies = jnp.broadcast_to(value, (lax.axis_size(axis), *value.shape))
    return lax.all_to_all(copies, axis, split_axis=0, concat_axis=0, tiled=True)


def of_everyone(value, axis):
    return sent_to_all(value, axis).sum(axis=0)


def in_one(arrays, axis):
    vector, at, outs = (jnp.concatenate([a.reshape(-1) for a in arrays]), 0, [])
    total = of_everyone(vector, axis)
    for a in arrays:
        outs.append(total[at : at + a.size].reshape(a.shape))
        at += a.size
    return tuple(outs)


def body(hidden, out_grad, memory, w_key, w_value, row_owner, row_slot, mem_table, adagrad_sum):
    highest = lax.Precision.HIGHEST
    scale_root = jnp.sqrt(jnp.asarray(D, jnp.float32))
    local_width = w_key.shape[1]
    proj_key = jnp.dot(memory, w_key, preferred_element_type=jnp.float32)
    proj_value = jnp.dot(memory, w_value, preferred_element_type=jnp.float32)
    part_score = jnp.sum(hidden.astype(jnp.float32) * proj_key, axis=1)
    part_gate = jnp.sum(out_grad.astype(jnp.float32) * proj_value, axis=1)
    scores, gate_grad = in_one((part_score, part_gate), "tensor")
    gate_value = jax.nn.sigmoid(scores / scale_root)
    score_grad = gate_grad * gate_value * (1.0 - gate_value) / scale_root
    value_grad = (gate_value[:, None] * out_grad.astype(jnp.float32)).astype(jnp.bfloat16)
    key_grad = (score_grad[:, None] * hidden.astype(jnp.float32)).astype(jnp.bfloat16)
    hidden_grad = (score_grad[:, None] * proj_key).astype(jnp.bfloat16)
    joined = jnp.concatenate([key_grad, value_grad], axis=1)
    over_tokens = (((0,), (0,)), ((), ()))
    both_grads = lax.psum_scatter(
        lax.dot_general(memory, joined, over_tokens, preferred_element_type=jnp.float32),
        "dp",
        scatter_dimension=0,
        tiled=True,
    )
    key_weight_grad = both_grads[:, :local_width]
    value_weight_grad = both_grads[:, local_width:]
    over_features = (((1,), (1,)), ((), ()))
    tensor_count = lax.axis_size("tensor")
    quarter = memory.shape[0] // tensor_count
    total = lax.dot_general(value_grad, w_value, over_features, preferred_element_type=jnp.float32)
    memory_grad = lax.psum_scatter(
        total + lax.dot_general(key_grad, w_key, over_features, preferred_element_type=jnp.float32),
        "tensor",
        scatter_dimension=0,
        tiled=True,
    )
    heads = row_owner.shape[1]
    row_width = memory_grad.shape[1] // heads
    first_row = lax.axis_index("tensor") * quarter
    owners = lax.dynamic_slice_in_dim(row_owner, first_row, quarter, 0)
    slots = lax.dynamic_slice_in_dim(row_slot, first_row, quarter, 0)
    grads = memory_grad.reshape(-1, row_width)
    dp_count = lax.axis_size("dp")
    owner_count = dp_count * tensor_count
    capacity = max(2, 2 * quarter * heads // owner_count)
    owner_ids = jnp.arange(owner_count, dtype=jnp.int32)
    matches = (owners[:, :, None] == owner_ids[None, None, :]).astype(jnp.float32)
    token_hits = jnp.sum(matches, axis=1)
    token_ids = jnp.arange(quarter, dtype=jnp.int32)
    earlier = (token_ids[:, None] > token_ids[None, :]).astype(jnp.float32)
    before = jnp.dot(earlier, token_hits, precision=highest, preferred_element_type=jnp.float32)
    ranks = jnp.sum(matches * before[:, None, :], axis=2).astype(jnp.int32)
    placed = (owners * capacity + ranks).reshape(-1)
    slot_plus = (slots.reshape(-1) + 1).astype(jnp.float32)
    total_slots = owner_count * capacity
    pack_block = math.gcd(total_slots, 512)
    pack_starts = jnp.arange(total_slots // pack_block, dtype=jnp.int32) * pack_block
    block_ids = jnp.arange(pack_block, dtype=jnp.int32)

    def pack_block_fn(first):
        select = (placed[:, None] == first + block_ids[None, :]).astype(jnp.float32)
        block_grads = lax.dot_general(
            select, grads, over_tokens, precision=highest, preferred_element_type=jnp.float32
        )
        block_slots = jnp.dot(
            slot_plus, select, precision=highest, preferred_element_type=jnp.float32
        )
        return (block_grads, block_slots)

    packed_grads, packed_slots = lax.map(pack_block_fn, pack_starts)
    send_grads = packed_grads.reshape(total_slots, row_width)
    send_slots = packed_slots.reshape(total_slots).astype(jnp.int32) - 1
    direct_grads = send_grads.reshape(owner_count, capacity, row_width)
    direct_slots = send_slots.reshape(owner_count, capacity)
    recv_grads, recv_slots = (
        lax.all_to_all(direct_grads, ("dp", "tensor"), split_axis=0, concat_axis=0, tiled=True),
        lax.all_to_all(direct_slots, ("dp", "tensor"), split_axis=0, concat_axis=0, tiled=True),
    )
    recv_grads = recv_grads.reshape(-1, row_width)
    recv_slots = recv_slots.reshape(-1)
    table_rows = mem_table.shape[0]
    sum_block = math.gcd(table_rows, 512)
    sum_starts = jnp.arange(table_rows // sum_block, dtype=jnp.int32) * sum_block
    row_ids = jnp.arange(sum_block, dtype=jnp.int32)

    def sum_block_fn(first):
        select = (recv_slots[:, None] == first + row_ids[None, :]).astype(jnp.float32)
        return lax.dot_general(
            select, recv_grads, over_tokens, precision=highest, preferred_element_type=jnp.float32
        )

    row_sum = lax.map(sum_block_fn, sum_starts).reshape(table_rows, row_width)
    new_sum = adagrad_sum + row_sum * row_sum
    new_table = mem_table - LEARN_RATE * row_sum / (jnp.sqrt(new_sum) + EPSILON)
    return (hidden_grad, key_weight_grad, value_weight_grad, new_table, new_sum)


def solution(mesh):
    return jax.shard_map(
        body,
        mesh=mesh,
        in_specs=(
            P("dp", "tensor"),
            P("dp", "tensor"),
            P("dp", None),
            P(None, "tensor"),
            P(None, "tensor"),
            P("dp", None),
            P("dp", None),
            P(("dp", "tensor"), None),
            P(("dp", "tensor"), None),
        ),
        out_specs=(
            P("dp", "tensor"),
            P("dp", "tensor"),
            P("dp", "tensor"),
            P(("dp", "tensor"), None),
            P(("dp", "tensor"), None),
        ),
        check_vma=False,
    )
```

profile of v0, /device:TPU:1, one launch (start us, length us, event | category | flops | bytes accessed | tf_op | source)
XLA Modules:
  0.0 253.0 jit_solution(13348047730842255768)
XLA Ops:
  7.2 2.6 %copy.46 = bf16[1024,640]{0,1:T(8,128)(2,1)} copy(bf16[1024,640]{1,0:T(8,128)(2,1)} %param.11) | data formatting | bytes 2621440 | tf_op args[0]
  9.8 2.5 copy.47
  12.3 5.4 %fusion.18 = (f32[1024]{0:T(1024)S(1)}, f32[1024,640]{0,1:T(8,128)}) fusion(bf16[1024,640]{0,1:T(8,128)(2,1)} %copy.46, bf16[1024,1280]{1,0:T(8,128)(2,1)S(1)} %copy-done, bf16[1280,640]{1,0:T(8,128)(2,1)} %param.14), kind=kOutput, calls=%fused_computation.21 | convolution fusion | flops 1679686656 | bytes 8196096 | tf_op jit(solution)/shard_map/dot_general | solution.py:37
  17.7 2.0 fusion.20
  19.7 9.1 %all_to_all.17 = f32[4,1,2048]{2,1,0:T(1,128)S(1)} all-to-all(f32[4,1,2048]{2,1,0:T(1,128)S(1)} %broadcast_in_dim.18), channel_id=1, replica_groups=mesh['dp'=32,'tensor'=4] {'tensor'}, dimensions={0} | all-to-all | bytes 65536 | tf_op jit(solution)/shard_map/all_to_all | solution.py:17
  28.9 4.6 %fusion.19 = (bf16[1024,640]{0,1:T(8,128)(2,1)S(1)}, bf16[1024,640]{0,1:T(8,128)(2,1)}, bf16[1024,640]{0,1:T(8,128)(2,1)S(1)}) fusion(bf16[1024,640]{0,1:T(8,128)(2,1)} %copy.46, f32[1024]{0:T(1024)S(1)} %get-tuple-element.125, f32[1024,640]{0,1:T(8,128)} %get-tuple-element.129, bf16[1024,640]{0,1:T(8,128)(2,1)} %copy.47, f32[1024]{0:T(1024)S(1)} %get-tuple-element.124), kind=kLoop, calls=%fused_computation.22 | loop fusion | flops 5242880 | bytes 9183232 | tf_op jit(solution)/shard_map/convert_element_type | solution.py:45
  33.5 2.3 fusion.34
  35.9 4.6 %convolution_add_fusion = f32[1024,1280]{1,0:T(8,128)} fusion(f32[1024,1280]{1,0:T(8,128)S(1)} %fusion.34, bf16[1024,640]{0,1:T(8,128)(2,1)S(1)} %get-tuple-element.126, bf16[1280,640]{1,0:T(8,128)(2,1)S(1)} %copy-done.3), kind=kOutput, calls=%fused_computation.15 | convolution fusion | flops 1679032320 | bytes 13434880 | tf_op jit(solution)/shard_map/dot_general | solution.py:62
  40.5 0.2 reduce-scatter.7.cloned.1.call-start
  40.7 8.0 %convolution_bitcast_fusion = f32[1280,1280]{0,1:T(8,128)} fusion(bf16[1024,1280]{1,0:T(8,128)(2,1)S(1)} %copy-done, bf16[1024,640]{0,1:T(8,128)(2,1)} %copy-done.4, bf16[1024,640]{0,1:T(8,128)(2,1)} %copy-done.1), kind=kOutput, calls=%fused_computation.12 | convolution fusion | flops 3360686080 | bytes 11796480 | tf_op jit(solution)/shard_map/dot_general | solution.py:50
  48.7 8.3 %copy.56 = f32[1280,1280]{1,0:T(8,128)} copy(f32[1280,1280]{0,1:T(8,128)} %convolution_bitcast_fusion) | data formatting | bytes 13107200
  57.1 0.7 add_convert_fusion
  57.8 0.1 copy.63
  57.9 0.4 convert_reduce_fusion
  58.3 0.3 fusion.25
  58.6 0.9 select_reduce_fusion
  59.6 0.1 copy.50
  59.8 0.1 convert_element_type.53
  59.9 38.0 %reduce-scatter.5.cloned.1.call-done = f32[256,1280]{1,0:T(8,128)} async-done(((f32[1024,1280]{1,0:T(8,128)}), f32[256,1280]{1,0:T(8,128)}) %reduce-scatter.5.cloned.1.call-update) | async-done | bytes 1310736 | tf_op jit(solution)/shard_map/reduce_scatter | solution.py:61
  97.9 3.3 %reshape.60 = f32[2048,160]{1,0:T(8,128)} reshape(f32[256,1280]{1,0:T(8,128)} %reduce-scatter.5.cloned.1.call-done) | data formatting | bytes 2621440 | tf_op jit(solution)/shard_map/reshape | solution.py:72
  101.2 59.9 %while.18 = (s32[]{:T(128)}, f32[8,512,160]{1,2,0:T(8,128)}, f32[8,512]{1,0:T(8,128)S(1)}, s32[256,8]{1,0:T(8,128)}, s32[8]{0:T(128)S(1)}, /*index=5*/f32[2048,1...) while((s32[]{:T(128)}, f32[8,512,160]{1,2,0:T(8,128)}, ...), condition=%wide.wide.region_8.9_spmd.clone, body=%wide.wide.region_7.8_spmd.clone.sunk | while | flops 2027946496 | bytes 2462329 | solution.py:100
  101.2 0.6 dynamic_slice.20
  101.8 0.6 iota_add_fusion.3
  102.4 4.8 %fusion.64 = f32[8,512,160]{1,2,0:T(8,128)} fusion(f32[8,512,160]{1,2,0:T(8,128)} %get-tuple-element.221, s32[]{:T(128)} %get-tuple-element.220, f32[2048,160]{1,0:T(8,128)} %get-tuple-element.235, s32[512]{0:T(512)S(1)} %iota_add_fusion.3, s32[2048]{0:T(1024)S(1)} %get-tuple-element.237), kind=kOutput, calls=%fused_computation.10.clone.clone.1 | convolution fusion | flops 2014314496 | bytes 2435584 | tf_op jit(solution)/shard_map/while/body/eval_jaxpr/dot_general | solution.py:92
  107.2 1.3 fusion.65
  108.6 0.6 dynamic_slice.20
  109.2 0.6 iota_add_fusion.3
  109.9 4.8 %fusion.64 = f32[8,512,160]{1,2,0:T(8,128)} fusion(f32[8,512,160]{1,2,0:T(8,128)} %get-tuple-element.221, s32[]{:T(128)} %get-tuple-element.220, f32[2048,160]{1,0:T(8,128)} %get-tuple-element.235, s32[512]{0:T(512)S(1)} %iota_add_fusion.3, s32[2048]{0:T(1024)S(1)} %get-tuple-element.237), kind=kOutput, calls=%fused_computation.10.clone.clone.1 | convolution fusion | flops 2014314496 | bytes 2435584 | tf_op jit(solution)/shard_map/while/body/eval_jaxpr/dot_general | solution.py:92
  114.7 1.3 fusion.65
  116.1 0.6 dynamic_slice.20
  116.7 0.6 iota_add_fusion.3
  117.3 4.9 %fusion.64 = f32[8,512,160]{1,2,0:T(8,128)} fusion(f32[8,512,160]{1,2,0:T(8,128)} %get-tuple-element.221, s32[]{:T(128)} %get-tuple-element.220, f32[2048,160]{1,0:T(8,128)} %get-tuple-element.235, s32[512]{0:T(512)S(1)} %iota_add_fusion.3, s32[2048]{0:T(1024)S(1)} %get-tuple-element.237), kind=kOutput, calls=%fused_computation.10.clone.clone.1 | convolution fusion | flops 2014314496 | bytes 2435584 | tf_op jit(solution)/shard_map/while/body/eval_jaxpr/dot_general | solution.py:92
  122.2 1.3 fusion.65
  123.6 0.6 dynamic_slice.20
  124.2 0.6 iota_add_fusion.3
  124.9 4.9 %fusion.64 = f32[8,512,160]{1,2,0:T(8,128)} fusion(f32[8,512,160]{1,2,0:T(8,128)} %get-tuple-element.221, s32[]{:T(128)} %get-tuple-element.220, f32[2048,160]{1,0:T(8,128)} %get-tuple-element.235, s32[512]{0:T(512)S(1)} %iota_add_fusion.3, s32[2048]{0:T(1024)S(1)} %get-tuple-element.237), kind=kOutput, calls=%fused_computation.10.clone.clone.1 | convolution fusion | flops 2014314496 | bytes 2435584 | tf_op jit(solution)/shard_map/while/body/eval_jaxpr/dot_general | solution.py:92
  129.8 1.3 fusion.65
  131.2 0.6 dynamic_slice.20
  131.8 0.7 iota_add_fusion.3
  132.4 4.9 %fusion.64 = f32[8,512,160]{1,2,0:T(8,128)} fusion(f32[8,512,160]{1,2,0:T(8,128)} %get-tuple-element.221, s32[]{:T(128)} %get-tuple-element.220, f32[2048,160]{1,0:T(8,128)} %get-tuple-element.235, s32[512]{0:T(512)S(1)} %iota_add_fusion.3, s32[2048]{0:T(1024)S(1)} %get-tuple-element.237), kind=kOutput, calls=%fused_computation.10.clone.clone.1 | convolution fusion | flops 2014314496 | bytes 2435584 | tf_op jit(solution)/shard_map/while/body/eval_jaxpr/dot_general | solution.py:92
  137.4 1.3 fusion.65
  138.8 0.6 dynamic_slice.20
  139.3 0.6 iota_add_fusion.3
  140.0 4.8 %fusion.64 = f32[8,512,160]{1,2,0:T(8,128)} fusion(f32[8,512,160]{1,2,0:T(8,128)} %get-tuple-element.221, s32[]{:T(128)} %get-tuple-element.220, f32[2048,160]{1,0:T(8,128)} %get-tuple-element.235, s32[512]{0:T(512)S(1)} %iota_add_fusion.3, s32[2048]{0:T(1024)S(1)} %get-tuple-element.237), kind=kOutput, calls=%fused_computation.10.clone.clone.1 | convolution fusion | flops 2014314496 | bytes 2435584 | tf_op jit(solution)/shard_map/while/body/eval_jaxpr/dot_general | solution.py:92
  144.8 1.3 fusion.65
  146.2 0.6 dynamic_slice.20
  146.8 0.6 iota_add_fusion.3
  147.4 4.8 %fusion.64 = f32[8,512,160]{1,2,0:T(8,128)} fusion(f32[8,512,160]{1,2,0:T(8,128)} %get-tuple-element.221, s32[]{:T(128)} %get-tuple-element.220, f32[2048,160]{1,0:T(8,128)} %get-tuple-element.235, s32[512]{0:T(512)S(1)} %iota_add_fusion.3, s32[2048]{0:T(1024)S(1)} %get-tuple-element.237), kind=kOutput, calls=%fused_computation.10.clone.clone.1 | convolution fusion | flops 2014314496 | bytes 2435584 | tf_op jit(solution)/shard_map/while/body/eval_jaxpr/dot_general | solution.py:92
  152.3 1.3 fusion.65
  153.7 0.6 dynamic_slice.20
  154.2 0.6 iota_add_fusion.3
  154.9 4.8 %fusion.64 = f32[8,512,160]{1,2,0:T(8,128)} fusion(f32[8,512,160]{1,2,0:T(8,128)} %get-tuple-element.221, s32[]{:T(128)} %get-tuple-element.220, f32[2048,160]{1,0:T(8,128)} %get-tuple-element.235, s32[512]{0:T(512)S(1)} %iota_add_fusion.3, s32[2048]{0:T(1024)S(1)} %get-tuple-element.237), kind=kOutput, calls=%fused_computation.10.clone.clone.1 | convolution fusion | flops 2014314496 | bytes 2435584 | tf_op jit(solution)/shard_map/while/body/eval_jaxpr/dot_general | solution.py:92
  159.7 1.3 fusion.65
  161.2 0.7 sub.14
  161.9 8.0 %all-to-all-start.1 = ((s32[128,1,32]{2,1,0:T(1,128)}), s32[128,1,32]{2,1,0:T(1,128)S(1)}, u32[]{:S(2)}, u32[]{:S(2)}) async-start(s32[128,1,32]{2,1,0:T(1,128)} %bitcast.1), calls=%async_computation.2 | async-start | bytes 131072 | tf_op jit(solution)/shard_map/all_to_all | solution.py:107
  169.9 4.7 %copy.52 = f32[8,512,160]{2,1,0:T(8,128)} copy(f32[8,512,160]{1,2,0:T(8,128)} %get-tuple-element.64) | data formatting | bytes 5242880 | tf_op jit(solution)/shard_map/while | solution.py:100
  174.6 5.1 %all-to-all-done.1 = s32[128,1,32]{2,1,0:T(1,128)S(1)} async-done(((s32[128,1,32]{2,1,0:T(1,128)}), s32[128,1,32]{2,1,0:T(1,128)S(1)}, u32[]{:S(2)}, u32[]{:S(2)}) %all-to-all-start.1) | async-done | bytes 16416 | tf_op jit(solution)/shard_map/all_to_all | solution.py:107
  179.7 5.1 %all-to-all-start.2 = ((f32[128,32,160]{2,1,0:T(8,128)}), f32[128,32,160]{2,1,0:T(8,128)}, u32[]{:S(2)}, u32[]{:S(2)}) async-start(f32[128,32,160]{2,1,0:T(8,128)} %bitcast.41), calls=%async_computation.3 | async-start | bytes 8388608 | tf_op jit(solution)/shard_map/all_to_all | solution.py:106
  184.8 2.5 copy.53
  187.4 1.6 fusion.33
  189.0 0.5 broadcast.62
  189.5 0.8 reduce.4
  190.4 47.5 %all-to-all-done.2 = f32[128,32,160]{2,1,0:T(8,128)} async-done(((f32[128,32,160]{2,1,0:T(8,128)}), f32[128,32,160]{2,1,0:T(8,128)}, u32[]{:S(2)}, u32[]{:S(2)}) %all-to-all-start.2) | async-done | bytes 2621472 | tf_op jit(solution)/shard_map/all_to_all | solution.py:106
  237.9 8.2 %divide_subtract_fusion = (f32[512,160]{0,1:T(8,128)}, f32[512,160]{0,1:T(8,128)}) fusion(f32[512,160]{0,1:T(8,128)S(1)} %copy-done.8, f32[512,160]{0,1:T(8,128)S(1)} %copy-done.9, f32[4096,160]{1,0:T(8,128)} %bitcast.3, s32[4096]{0:T(1024)S(1)} %eq.53), kind=kOutput, calls=%fused_computation.32 | convolution fusion | flops 4029120512 | bytes 3948544 | tf_op jit(solution)/shard_map/while/body/eval_jaxpr/dot_general | solution.py:118
  (43 shorter events, 0.8 us)
Async XLA Ops:
  7.2 5.2 %copy-start = (bf16[1024,1280]{1,0:T(8,128)(2,1)S(1)}, bf16[1024,1280]{1,0:T(8,128)(2,1)}, u32[]{:S(2)}) copy-start(bf16[1024,1280]{1,0:T(8,128)(2,1)} %param.13) | copy-start | bytes 7864324
  7.2 90.7 %reduce-scatter.5.cloned.1.call-start = ((), (), s32[]{:S(2)}) async-start(), calls=%async_computation.5 | async-start | bytes 6553600 | tf_op jit(solution)/shard_map/reduce_scatter | solution.py:61
  12.3 5.4 %copy-start.2 = (bf16[1024,640]{0,1:T(8,128)(2,1)S(1)}, bf16[1024,640]{0,1:T(8,128)(2,1)}, u32[]{:S(2)}) copy-start(bf16[1024,640]{0,1:T(8,128)(2,1)} %copy.47) | copy-start | bytes 3932164
  12.3 5.4 %copy-start.6 = (bf16[1280,640]{1,0:T(8,128)(2,1)S(1)}, bf16[1280,640]{1,0:T(8,128)(2,1)}, u32[]{:S(2)}) copy-start(bf16[1280,640]{1,0:T(8,128)(2,1)} %param.15) | copy-start | bytes 4915204
  28.9 4.6 %copy-start.7 = (bf16[1280,640]{1,0:T(8,128)(2,1)S(1)}, bf16[1280,640]{1,0:T(8,128)(2,1)}, u32[]{:S(2)}) copy-start(bf16[1280,640]{1,0:T(8,128)(2,1)} %param.15) | copy-start | bytes 4915204
  33.5 2.3 copy-start.4
  33.5 2.3 copy-start.1
  33.5 2.4 copy-start.3
  40.5 146.9 %reduce-scatter.7.cloned.1.call-start = ((), (), s32[]{:S(2)}) async-start(), calls=%async_computation.6 | async-start | bytes 6758400
  59.5 41.7 %copy-start.5 = (s32[256,8]{1,0:T(8,128)}, s32[256,8]{1,0:T(8,128)S(1)}, u32[]{:S(2)}) copy-start(s32[256,8]{1,0:T(8,128)S(1)} %convert_add_fusion) | copy-start | bytes 24580
  161.9 17.8 %all-to-all-start.1 = ((s32[128,1,32]{2,1,0:T(1,128)}), s32[128,1,32]{2,1,0:T(1,128)S(1)}, u32[]{:S(2)}, u32[]{:S(2)}) async-start(s32[128,1,32]{2,1,0:T(1,128)} %bitcast.1), calls=%async_computation.2 | async-start | bytes 131072 | tf_op jit(solution)/shard_map/all_to_all | solution.py:107
  179.7 58.2 %all-to-all-start.2 = ((f32[128,32,160]{2,1,0:T(8,128)}), f32[128,32,160]{2,1,0:T(8,128)}, u32[]{:S(2)}, u32[]{:S(2)}) async-start(f32[128,32,160]{2,1,0:T(8,128)} %bitcast.41), calls=%async_computation.3 | async-start | bytes 8388608 | tf_op jit(solution)/shard_map/all_to_all | solution.py:106
  184.8 53.1 %copy-start.8 = (f32[512,160]{0,1:T(8,128)S(1)}, f32[512,160]{0,1:T(8,128)}, u32[]{:S(2)}) copy-start(f32[512,160]{0,1:T(8,128)} %param.18) | copy-start | bytes 983044
  184.8 53.1 %copy-start.9 = (f32[512,160]{0,1:T(8,128)S(1)}, f32[512,160]{0,1:T(8,128)}, u32[]{:S(2)}) copy-start(f32[512,160]{0,1:T(8,128)} %param.19) | copy-start | bytes 983044
Sparse Core Ops, SparseCore 0:
  40.6 57.2 reduce-scatter.4
  101.6 84.7 reduce-scatter.6
where the time goes:
time: 254 us; the launch traced here: 253 us
  waiting for transfers between devices  90.7 us (36%)
  matrix products  80.1 us (32%)
  local copies, waits for them, and re-layouts  32.5 us (13%)
  between operations  14.3 us (6%)
  starting transfers between devices  13.4 us (5%)
  other arithmetic  12.6 us (5%)
  blocking collectives  9.11 us (4%)
    all_to_all x1, waiting for transfers between devices, body(): lax.all_to_all(direct_grads, ('dp', 'tensor'), split_axis=0, concat_axis=...  47.5 us
    dot_general x8, matrix products, pack_block_fn(): lax.dot_general(select, grads, over_tokens, precision=highest, preferred_...  38.8 us
    reduce_scatter x1, waiting for transfers between devices, body(): lax.psum_scatter(total + lax.dot_general(key_grad, w_key, over_features,...  38 us
    unnamed x25, local copies, waits for them, and re-layouts  16.2 us
    dot_general x8, matrix products, pack_block_fn(): jnp.dot(slot_plus, select, precision=highest, preferred_element_type=jnp....  10.7 us
    all_to_all x1, blocking collectives, sent_to_all(): return lax.all_to_all(copies, axis, split_axis=0, concat_axis=0, tiled=True)  9.11 us
    dot_general x1, matrix products, sum_block_fn(): lax.dot_general(select, recv_grads, over_tokens, precision=highest, prefe...  8.2 us
    all_to_all x1, starting transfers between devices, body(): lax.all_to_all(direct_slots, ('dp', 'tensor'), split_axis=0, concat_axis=...  8 us
  transfers between devices with their start and end apart: 4, of which 3 were waited for; matrix products, arithmetic and copies ran while one was open for 37% of the time, Pallas kernels for 0%

commit v1 on v0

v1 whole, which is shorter than its diff:
```python
import functools

import jax
import jax.numpy as jnp
from jax import lax
from jax.experimental import pallas as pl
from jax.experimental.pallas import tpu as pltpu
from jax.sharding import PartitionSpec as P

D = 2560
HEADS = 8
EH = 160
MAIN = 128
TAIL = EH - MAIN
CAP = 32
GROUP = CAP // 4
CHUNK = CAP + GROUP + 1
LEARN_RATE = 0.5
EPSILON = 1e-06
F32 = jnp.float32
BF16 = jnp.bfloat16
OVER_ROWS = (((0,), (0,)), ((), ()))
OVER_LANES = (((1,), (1,)), ((), ()))


def params(mib):
    return pltpu.CompilerParams(vmem_limit_bytes=mib << 20)


def cost(flops, moved):
    return pl.CostEstimate(flops=flops, bytes_accessed=moved, transcendentals=0)


def row_sums(x):
    lanes = x[:, :128]
    for at in range(128, x.shape[1], 128):
        lanes = lanes + x[:, at : at + 128]
    return jnp.sum(lanes.T, axis=0, keepdims=True)


def as_columns(row, width):
    column = jnp.broadcast_to(row, (128, row.shape[1])).T
    return jnp.concatenate([column] * (width // 128), axis=1)


def ranks_kernel(at_ref, owners_ref, slots_ref, ranks_ref, sent_ref):
    count = owners_ref.shape[1]
    owners = owners_ref[...]
    slot_plus = slots_ref[...] + 1
    ids = lax.broadcasted_iota(jnp.int32, (128, count), 0)
    hits = jnp.zeros((128, count), F32)
    for h in range(HEADS):
        hits = hits + jnp.where(owners[h : h + 1] == ids, 1.0, 0.0)
    earlier = lax.broadcasted_iota(jnp.int32, (count, count), 0) < lax.broadcasted_iota(
        jnp.int32, (count, count), 1
    )
    before = jnp.dot(
        hits.astype(BF16), jnp.where(earlier, 1.0, 0.0).astype(BF16), preferred_element_type=F32
    )
    high = jnp.zeros((128, 128), F32)
    low = jnp.zeros((128, 128), F32)
    for h in range(HEADS):
        match = owners[h : h + 1] == ids
        rank = jnp.sum(jnp.where(match, before, 0.0), axis=0, keepdims=True).astype(jnp.int32)
        ranks_ref[h : h + 1, :] = rank
        place = jnp.where(rank == ids, 1.0, 0.0).astype(BF16)
        slot = slot_plus[h : h + 1]
        upper = jnp.where(match, (slot // 16).astype(F32), 0.0).astype(BF16)
        lower = jnp.where(match, (slot % 16).astype(F32), 0.0).astype(BF16)
        high = high + lax.dot_general(upper, place, OVER_LANES, preferred_element_type=F32)
        low = low + lax.dot_general(lower, place, OVER_LANES, preferred_element_type=F32)
    sent_ref[...] = 16.0 * high + low


def forward_kernel(memory_ref, hidden_ref, grad_ref, wk_ref, wv_ref, key_ref, part_ref):
    memory = memory_ref[...]
    proj_key = jnp.dot(memory, wk_ref[...], preferred_element_type=F32)
    key_ref[...] = proj_key
    part_ref[0:1, :] = row_sums(hidden_ref[...].astype(F32) * proj_key)
    proj_value = jnp.dot(memory, wv_ref[...], preferred_element_type=F32)
    part_ref[1:2, :] = row_sums(grad_ref[...].astype(F32) * proj_value)


def gate_kernel(p0, p1, p2, p3, hidden_ref, grad_ref, key_ref, both_ref, hidden_grad_ref):
    width = hidden_ref.shape[1]
    total = (p0[...] + p1[...]) + (p2[...] + p3[...])
    root = jnp.sqrt(jnp.full((1, 1), D, F32))
    gate = jax.nn.sigmoid(total[0:1] / root)
    score = total[1:2] * gate * (1.0 - gate) / root
    gates = as_columns(gate, width)
    scores = as_columns(score, width)
    both_ref[:, :width] = (scores * hidden_ref[...].astype(F32)).astype(BF16)
    both_ref[:, width:] = (gates * grad_ref[...].astype(F32)).astype(BF16)
    hidden_grad_ref[...] = (scores * key_ref[...]).astype(BF16)


def memory_grad_kernel(at_ref, left_ref, right_ref, wk_ref, wv_ref, out_left, out_right):
    width = wk_ref.shape[1]
    half = HEADS // 2

    def product(both, first, rows):
        return lax.dot_general(
            both[:, :width], wk_ref[first : first + rows, :], OVER_LANES, preferred_element_type=F32
        ) + lax.dot_general(
            both[:, width:], wv_ref[first : first + rows, :], OVER_LANES, preferred_element_type=F32
        )

    for both_ref, out_ref, base in ((left_ref, out_left, 0), (right_ref, out_right, half)):
        both = both_ref[...]
        for h in range(half):
            head = product(both, (base + h) * EH, EH)
            out_ref[0, :, h * MAIN : (h + 1) * MAIN] = head[:, :MAIN]
            out_ref[0, :, half * MAIN + h * TAIL : half * MAIN + (h + 1) * TAIL] = head[:, MAIN:]


def weight_grad_kernel(memory_ref, both_ref, out_ref):
    out_ref[...] = lax.dot_general(
        memory_ref[...], both_ref[...], OVER_ROWS, preferred_element_type=F32
    )


def pack_kernel(left_ref, right_ref, owners_ref, ranks_ref, sent_ref, out_ref, select, rows, tails):
    j = pl.program_id(0)
    count = owners_ref.shape[1]
    half = HEADS // 2
    lane_group = lax.broadcasted_iota(jnp.int32, (count, 128), 1) // TAIL
    ids = lax.broadcasted_iota(jnp.int32, (128, count), 0)
    for h in range(HEADS):
        source = (left_ref, right_ref)[h // half]
        at = h % half

        @pl.when(j == 0)
        def _():
            main = source[:, at * MAIN : (at + 1) * MAIN]
            top = main.astype(BF16)
            rows[h * count : (h + 1) * count, :MAIN] = top
            rows[h * count : (h + 1) * count, 256 : 256 + MAIN] = (main - top.astype(F32)).astype(
                BF16
            )

        tail = source[:, half * MAIN : half * MAIN + 128]
        tail = pltpu.roll(tail, (j - at + 4) % 4 * TAIL, 1)
        tail = jnp.where(lane_group == j, tail, 0.0)
        top = tail.astype(BF16)
        rows[h * count : (h + 1) * count, MAIN:256] = top
        rows[h * count : (h + 1) * count, 256 + MAIN :] = (tail - top.astype(F32)).astype(BF16)
        match = jnp.where(owners_ref[h : h + 1, :] == ids, 1.0, 0.0).astype(BF16)
        rank = ranks_ref[h : h + 1, :]
        for k in range(GROUP):
            here = jnp.where(rank == j * GROUP + k, 1.0, 0.0)
            here = jnp.broadcast_to(here, (128, count)).astype(BF16)
            select[k * 128 : (k + 1) * 128, h * count : (h + 1) * count] = match * here
    found = jnp.dot(select[...], rows[...], preferred_element_type=F32)
    found = found[:, :256] + found[:, 256:]

    @pl.when(j == 0)
    def _():
        tails[...] = found[:, MAIN:]

    @pl.when(j > 0)
    def _():
        tails[...] += found[:, MAIN:]

    for k in range(GROUP):
        out_ref[pl.ds(j * GROUP + k, 128, stride=CHUNK), :] = found[k * 128 : (k + 1) * 128, :MAIN]

    @pl.when(j == pl.num_programs(0) - 1)
    def _():
        for k in range(GROUP):
            out_ref[pl.ds(CAP + k, 128, stride=CHUNK), :] = tails[k * 128 : (k + 1) * 128, :]
        out_ref[pl.ds(CAP + GROUP, 128, stride=CHUNK), :] = sent_ref[...]


def update_kernel(got_ref, table_ref, sums_ref, new_table_ref, new_sum_ref, values, select):
    owned = table_ref.shape[1]
    slots = got_ref[pl.ds(CAP + GROUP, 128, stride=CHUNK), :]
    ids = (lax.broadcasted_iota(jnp.int32, (128, owned), 1) + 1).astype(F32)
    for k in range(CAP):
        at = slice(k * 128, (k + 1) * 128)
        select[at, :] = jnp.where(slots[:, k : k + 1] == ids, 1.0, 0.0).astype(BF16)
        main = got_ref[pl.ds(k, 128, stride=CHUNK), :].T
        top = main.astype(BF16)
        values[:MAIN, at] = top
        values[EH : EH + MAIN, at] = (main - top.astype(F32)).astype(BF16)
    for k in range(GROUP):
        tail = got_ref[pl.ds(CAP + k, 128, stride=CHUNK), :].T
        top = tail.astype(BF16)
        rest = (tail - top.astype(F32)).astype(BF16)
        for j in range(4):
            at = slice((j * GROUP + k) * 128, (j * GROUP + k + 1) * 128)
            values[MAIN:EH, at] = top[j * TAIL : (j + 1) * TAIL]
            values[EH + MAIN :, at] = rest[j * TAIL : (j + 1) * TAIL]
    both = jnp.dot(values[...], select[...], preferred_element_type=F32)
    row_sum = both[:EH] + both[EH:]
    new_sum = sums_ref[...] + row_sum * row_sum
    new_sum_ref[...] = new_sum
    new_table_ref[...] = table_ref[...] - LEARN_RATE * row_sum / (jnp.sqrt(new_sum) + EPSILON)


def whole(shape):
    return pl.BlockSpec(shape, lambda *_: (0,) * len(shape))


def body(hidden, out_grad, memory, w_key, w_value, row_owner, row_slot, mem_table, adagrad_sum):
    tokens, width = hidden.shape
    depth = memory.shape[1]
    quarter = tokens // 4
    me = lax.axis_index("tensor").astype(jnp.int32)
    at = me.reshape(1)
    tile = 256
    tiles = tokens // tile

    def by_rows(cols):
        return pl.BlockSpec((tile, cols), lambda i: (i, 0))

    part_spec = pl.BlockSpec((2, tile), lambda i: (0, i))
    proj_key, part = pl.pallas_call(
        forward_kernel,
        grid=(tiles,),
        in_specs=[
            by_rows(depth),
            by_rows(width),
            by_rows(width),
            whole((depth, width)),
            whole((depth, width)),
        ],
        out_specs=[by_rows(width), part_spec],
        out_shape=[
            jax.ShapeDtypeStruct((tokens, width), F32),
            jax.ShapeDtypeStruct((2, tokens), F32),
        ],
        compiler_params=params(40),
        cost_estimate=cost(4 * tokens * depth * width, 12 << 20),
        name="forward",
    )(memory, hidden, out_grad, w_key, w_value)
    parts = [part] + [
        lax.ppermute(part, "tensor", [(i, (i + step) % 4) for i in range(4)]) for step in (1, 2, 3)
    ]

    ranks, sent = pl.pallas_call(
        ranks_kernel,
        grid_spec=pltpu.PrefetchScalarGridSpec(
            num_scalar_prefetch=1,
            grid=(1,),
            in_specs=[pl.BlockSpec((HEADS, quarter), lambda i, s: (0, s[0]))] * 2,
            out_specs=[whole((HEADS, quarter)), whole((128, 128))],
        ),
        out_shape=[
            jax.ShapeDtypeStruct((HEADS, quarter), jnp.int32),
            jax.ShapeDtypeStruct((128, 128), F32),
        ],
        compiler_params=params(16),
        cost_estimate=cost(200 << 20, 1 << 20),
        name="ranks",
    )(at, row_owner.T, row_slot.T)

    both, hidden_grad = pl.pallas_call(
        gate_kernel,
        grid=(tiles,),
        in_specs=[part_spec] * 4 + [by_rows(width)] * 3,
        out_specs=[by_rows(2 * width), by_rows(width)],
        out_shape=[
            jax.ShapeDtypeStruct((tokens, 2 * width), BF16),
            jax.ShapeDtypeStruct((tokens, width), BF16),
        ],
        compiler_params=params(32),
        cost_estimate=cost(8 * tokens * width, 9 << 20),
        name="gate",
    )(*parts, hidden, out_grad, proj_key)

    def memory_grad(first, steps, name):
        out = pl.BlockSpec((1, quarter, width), lambda p, s: (p, 0, 0))
        return pl.pallas_call(
            memory_grad_kernel,
            grid_spec=pltpu.PrefetchScalarGridSpec(
                num_scalar_prefetch=1,
                grid=(steps,),
                in_specs=[
                    pl.BlockSpec((quarter, 2 * width), lambda p, s: ((s[0] + 7 - first - p) % 4, 0)),
                    pl.BlockSpec((quarter, 2 * width), lambda p, s: ((s[0] + 1 + first + p) % 4, 0)),
                    whole((depth, width)),
                    whole((depth, width)),
                ],
                out_specs=[out, out],
            ),
            out_shape=[jax.ShapeDtypeStruct((steps, quarter, width), F32)] * 2,
            compiler_params=params(40),
            cost_estimate=cost(
                4 * steps * quarter * depth * width, (4 << 20) + steps * (2 << 20)
            ),
            name=name,
        )(at, both, both, w_key, w_value)

    first_left, first_right = memory_grad(0, 1, "memory_grad_first")
    left = [first_left[0, :128], first_left[0, 128:]]
    right = [first_right[0, :128], first_right[0, 128:]]
    rest_left, rest_right = memory_grad(1, 3, "memory_grad_rest")
    up = [(i, (i + 1) % 4) for i in range(4)]
    down = [(i, (i + 3) % 4) for i in range(4)]
    for step in range(3):
        for piece in range(2):
            rows = slice(piece * 128, (piece + 1) * 128)
            left[piece] = lax.ppermute(left[piece], "tensor", up) + rest_left[step, rows]
            right[piece] = lax.ppermute(right[piece], "tensor", down) + rest_right[step, rows]
    left = jnp.concatenate(left, axis=0)
    right = jnp.concatenate(right, axis=0)

    weight_tile = 256
    both_grads = pl.pallas_call(
        weight_grad_kernel,
        grid=(depth // weight_tile,),
        in_specs=[
            pl.BlockSpec((tokens, weight_tile), lambda i: (0, i)),
            whole((tokens, 2 * width)),
        ],
        out_specs=pl.BlockSpec((weight_tile, 2 * width), lambda i: (i, 0)),
        out_shape=jax.ShapeDtypeStruct((depth, 2 * width), F32),
        compiler_params=params(40),
        cost_estimate=cost(4 * tokens * depth * width, 12 << 20),
        name="weight_grad",
    )(memory, both)
    both_grads = lax.psum_scatter(both_grads, "dp", scatter_dimension=0, tiled=True)
    key_weight_grad = both_grads[:, :width]
    value_weight_grad = both_grads[:, width:]

    packed = pl.pallas_call(
        pack_kernel,
        grid=(4,),
        in_specs=[
            whole((quarter, width)),
            whole((quarter, width)),
            whole((HEADS, quarter)),
            whole((HEADS, quarter)),
            whole((128, 128)),
        ],
        out_specs=whole((128 * CHUNK, 128)),
        out_shape=jax.ShapeDtypeStruct((128 * CHUNK, 128), F32),
        scratch_shapes=[
            pltpu.VMEM((GROUP * 128, HEADS * quarter), BF16),
            pltpu.VMEM((HEADS * quarter, 512), BF16),
            pltpu.VMEM((GROUP * 128, 128), F32),
        ],
        compiler_params=params(48),
        cost_estimate=cost(2 * 4096 * 2048 * 512, 6 << 20),
        name="pack",
    )(left, right, ranks_owner(row_owner, me, quarter), ranks, sent)
    received = lax.all_to_all(
        packed.reshape(128, 1, CHUNK * 128),
        ("dp", "tensor"),
        split_axis=0,
        concat_axis=0,
        tiled=True,
    ).reshape(128 * CHUNK, 128)
    owned = mem_table.shape[0]
    table_spec = whole((EH, owned))
    new_table, new_sum = pl.pallas_call(
        update_kernel,
        grid=(1,),
        in_specs=[whole((128 * CHUNK, 128)), table_spec, table_spec],
        out_specs=[table_spec, table_spec],
        out_shape=[jax.ShapeDtypeStruct((EH, owned), F32)] * 2,
        scratch_shapes=[
            pltpu.VMEM((2 * EH, CAP * 128), BF16),
            pltpu.VMEM((CAP * 128, owned), BF16),
        ],
        compiler_params=params(48),
        cost_estimate=cost(4 * EH * 4096 * 512, 5 << 20),
        name="update",
    )(received, mem_table.T, adagrad_sum.T)
    return (hidden_grad, key_weight_grad, value_weight_grad, new_table.T, new_sum.T)


def ranks_owner(row_owner, me, quarter):
    return lax.dynamic_slice_in_dim(row_owner, me * quarter, quarter, 0).T


def solution(mesh):
    return jax.shard_map(
        body,
        mesh=mesh,
        in_specs=(
            P("dp", "tensor"),
            P("dp", "tensor"),
            P("dp", None),
            P(None, "tensor"),
            P(None, "tensor"),
            P("dp", None),
            P("dp", None),
            P(("dp", "tensor"), None),
            P(("dp", "tensor"), None),
        ),
        out_specs=(
            P("dp", "tensor"),
            P("dp", "tensor"),
            P("dp", "tensor"),
            P(("dp", "tensor"), None),
            P(("dp", "tensor"), None),
        ),
        check_vma=False,
    )
```

time: 254 us -> 168 us (0.66)
  matrix products: 80.1 us -> 0 us
  waiting for transfers between devices: 90.7 us -> 24.2 us
  blocking collectives: 9.11 us -> 53.7 us
  Pallas kernels: 0 us -> 37.1 us
  local copies, waits for them, and re-layouts: 32.5 us -> 14.6 us
  other arithmetic: 12.6 us -> 5.29 us
  starting transfers between devices: 13.4 us -> 18.6 us
    dot_general x23 -> x0, matrix products: 80.1 us -> none  [the longest x8 38.8 us: pack_block_fn(): lax.dot_general(select, grads, over_tokens, precision=highest, preferred_...]
    all_to_all x2 -> x0, waiting for transfers between devices: 52.6 us -> none  [the longest x1 47.5 us: body(): lax.all_to_all(direct_grads, ('dp', 'tensor'), split_axis=0, concat_axis=...]
    all_to_all x1, blocking collectives: 9.11 us -> 53.7 us  [body(): lax.all_to_all(packed.reshape(128, 1, CHUNK * 128), ('dp', 'tensor'), spl...]
    reduce_scatter x1, waiting for transfers between devices: 38 us -> 0.01 us  [body(): lax.psum_scatter(both_grads, 'dp', scatter_dimension=0, tiled=True)]
    pallas_call x0 -> x8, Pallas kernels: none -> 37.1 us  [the longest x1 13.9 us: body(): pl.pallas_call(pack_kernel, grid=(4,), in_specs=[whole((quarter, width)),...]
    ppermute x0 -> x15, waiting for transfers between devices: none -> 24.2 us  [the longest x6 22.5 us: body(): lax.ppermute(left[piece], 'tensor', up) + rest_left[step, rows]]
    ppermute x0 -> x15, starting transfers between devices: none -> 18.5 us  [the longest x6 11.5 us: body(): lax.ppermute(right[piece], 'tensor', down) + rest_right[step, rows]]
    all_to_all x2 -> x0, starting transfers between devices: 13.1 us -> none  [the longest x1 8 us: body(): lax.all_to_all(direct_slots, ('dp', 'tensor'), split_axis=0, concat_axis=...]
  transfers between devices with their start and end apart: 4 -> 16, of which waited for: 3 -> 7; matrix products, arithmetic and copies ran while one was open for 37% -> 3% of each run, Pallas kernels for 0% -> 15%
where the time goes in v1:
time: 168 us
  blocking collectives  53.7 us (32%)
  Pallas kernels  37.1 us (22%)
  waiting for transfers between devices  24.2 us (14%)
  starting transfers between devices  18.6 us (11%)
  local copies, waits for them, and re-layouts  14.6 us (9%)
  between operations  14.3 us (9%)
  other arithmetic  5.29 us (3%)
    all_to_all x1, blocking collectives, body(): lax.all_to_all(packed.reshape(128, 1, CHUNK * 128), ('dp', 'tensor'), spl...  53.7 us
    ppermute x6, waiting for transfers between devices, body(): lax.ppermute(left[piece], 'tensor', up) + rest_left[step, rows]  22.5 us
    pallas_call x1, Pallas kernels, body(): pl.pallas_call(pack_kernel, grid=(4,), in_specs=[whole((quarter, width)),...  13.9 us
    unnamed x36, local copies, waits for them, and re-layouts  12.8 us
    ppermute x6, starting transfers between devices, body(): lax.ppermute(right[piece], 'tensor', down) + rest_right[step, rows]  11.5 us
    pallas_call x2, Pallas kernels, memory_grad(): pl.pallas_call(memory_grad_kernel, grid_spec=pltpu.PrefetchScalarGridSpec...  7.46 us
    ppermute x3, starting transfers between devices, body(): lax.ppermute(part, 'tensor', [(i, (i + step) % 4) for i in range(4)])  5.88 us
    pallas_call x1, Pallas kernels, body(): pl.pallas_call(forward_kernel, grid=(tiles,), in_specs=[by_rows(depth), b...  5.16 us
  transfers between devices with their start and end apart: 16, of which 7 were waited for; matrix products, arithmetic and copies ran while one was open for 3% of the time, Pallas kernels for 15%

profile of v1, /device:TPU:1, one launch (start us, length us, event | category | flops | bytes accessed | tf_op | source)
XLA Modules:
  0.0 167.8 jit_solution(10223529799647517098)
XLA Ops:
  7.2 0.0 reduce-scatter.2.cloned.1.call-start
  7.2 0.0 copy-start.4
  7.2 1.4 copy-done.4
  8.6 1.4 copy-done.7
  10.1 1.3 copy-done.10
  11.4 1.3 copy-done.11
  12.7 1.7 %copy-done.13 = bf16[1024,1280]{1,0:T(8,128)(2,1)S(1)} copy-done((bf16[1024,1280]{1,0:T(8,128)(2,1)S(1)}, bf16[1024,1280]{1,0:T(8,128)(2,1)}, u32[]{:S(2)}) %copy-start.13) | copy-done | bytes 2621464
  14.4 5.2 %forward.1 = (f32[1024,640]{1,0:T(8,128)S(1)}, f32[2,1024]{1,0:T(2,128)S(1)}) custom-call(bf16[1024,1280]{1,0:T(8,128)(2,1)S(1)} %copy-done.13, bf16[1024,640]{1,0:T(8,128)(2,1)S(1)} %copy-done.10, bf16[1024,640]{1,0:T(8,128)(2,1)S(1)} %copy-done.11, bf16[1280,640]{1,0:T(8,128)(2,1)S(1)} %copy-done.4, bf16[1280,640]{1,0:T(8,128)(2,1)S(1)} %copy-done.7), custom_call_target="tpu_custom_call" | custom-call | flops 3355443200 | bytes 12582912 | tf_op jit(solution)/shard_map/forward/pallas_call | solution.py:217
  19.6 2.2 %collective-permute-start = (f32[2,1024]{1,0:T(2,128)S(1)}, f32[2,1024]{1,0:T(2,128)S(1)}, u32[]{:S(2)}, u32[]{:S(2)}) collective-permute-start(f32[2,1024]{1,0:T(2,128)S(1)} %get-tuple-element.17.p0), channel_id=1, source_target_pairs={{0,1},{1,2},{2,3},{3,0},{4,5},{5,6},{6,7},{7,4},{8,9},{9,10},{10,1... | collective-permute-start | bytes 24584 | tf_op jit(solution)/shard_map/ppermute | solution.py:237
  21.8 2.6 %collective-permute-start.1 = (f32[2,1024]{1,0:T(2,128)S(1)}, f32[2,1024]{1,0:T(2,128)S(1)}, u32[]{:S(2)}, u32[]{:S(2)}) collective-permute-start(f32[2,1024]{1,0:T(2,128)S(1)} %get-tuple-element.17.p0), channel_id=1, source_target_pairs={{0,2},{1,3},{2,0},{3,1},{4,6},{5,7},{6,4},{7,5},{8,10},{9,11},{10,... | collective-permute-start | bytes 24584 | tf_op jit(solution)/shard_map/ppermute | solution.py:237
  24.4 1.1 collective-permute-start.2
  25.5 0.0 collective-permute-done.p1
  25.5 0.3 collective-permute-done.1.p2
  25.8 1.4 collective-permute-done.2.p3
  27.2 2.1 %gate.1 = (bf16[1024,1280]{1,0:T(8,128)(2,1)S(1)}, bf16[1024,640]{1,0:T(8,128)(2,1)}) custom-call(f32[2,1024]{1,0:T(2,128)S(1)} %get-tuple-element.17.p0, f32[2,1024]{1,0:T(2,128)S(1)} %collective-permute-done.p1, f32[2,1024]{1,0:T(2,128)S(1)} %collective-permute-done.1.p2, f32[2,1024]{1,0:T(2,128)S(1)} %collective-permute-done.2.p3, ...), custom_call_target="tpu_custom_call" | custom-call | flops 5242880 | bytes 9437184 | tf_op jit(solution)/shard_map/gate/pallas_call | solution.py:257
  29.4 0.0 copy-done.14
  29.4 4.7 %weight_grad.1 = f32[1280,1280]{1,0:T(8,128)S(1)} custom-call(bf16[1024,1280]{1,0:T(8,128)(2,1)S(1)} %copy-done.14, bf16[1024,1280]{1,0:T(8,128)(2,1)S(1)} %get-tuple-element.20.both_ref.left_ref.right_ref), custom_call_target="tpu_custom_call" | custom-call | flops 3355443200 | bytes 12582912 | tf_op jit(solution)/shard_map/weight_grad/pallas_call | solution.py:309
  34.1 0.0 copy-start
  34.1 2.7 %copy-done = f32[1280,1280]{1,0:T(8,128)} copy-done((f32[1280,1280]{1,0:T(8,128)}, f32[1280,1280]{1,0:T(8,128)S(1)}, u32[]{:S(2)}) %copy-start) | copy-done | bytes 6553624
  36.8 0.0 reduce-scatter.2.cloned.1.call-update
  36.8 0.0 copy-start.5
  36.8 1.4 copy-done.5
  38.3 1.4 copy-done.8
  39.7 1.9 %memory_grad_first.1 = (f32[1,256,640]{2,1,0:T(8,128)S(1)}, f32[1,256,640]{2,1,0:T(8,128)S(1)}) custom-call(s32[1]{0:T(128)} %bitcast.at_ref, bf16[1024,1280]{1,0:T(8,128)(2,1)S(1)} %get-tuple-element.20.both_ref.left_ref.right_ref, bf16[1024,1280]{1,0:T(8,128)(2,1)S(1)} %get-tuple-element.20.both_ref.left_ref.right_ref, bf16[1280,640]{1,0:T(8,128)(2,1)S(1)} %copy-done.5, ...), custom_call_target="tpu_custom_call" | custom-call | flops 838860800 | bytes 6291456 | tf_op jit(solution)/shard_map/memory_grad_first/pallas_call | solution.py:273
  41.5 0.0 copy-start.6
  41.6 0.1 collective-permute-start.3
  41.7 0.9 collective-permute-start.6
  42.6 1.9 %collective-permute-start.9 = (f32[128,640]{1,0:T(8,128)S(1)}, f32[128,640]{1,0:T(8,128)S(1)}, u32[]{:S(2)}, u32[]{:S(2)}) collective-permute-start(f32[128,640]{1,0:T(8,128)S(1)} %get-tuple-element.41), channel_id=1, source_target_pairs={{0,3},{1,0},{2,1},{3,2},{4,7},{5,4},{6,5},{7,6},{8,11},{9,8},{10,9... | collective-permute-start | bytes 983048 | tf_op jit(solution)/shard_map/ppermute | solution.py:304
  44.6 1.4 collective-permute-start.12
  45.9 5.6 %memory_grad_rest.1 = (f32[3,256,640]{2,1,0:T(8,128)S(1)}, f32[3,256,640]{2,1,0:T(8,128)S(1)}) custom-call(s32[1]{0:T(128)} %bitcast.at_ref, bf16[1024,1280]{1,0:T(8,128)(2,1)S(1)} %get-tuple-element.20.both_ref.left_ref.right_ref, bf16[1024,1280]{1,0:T(8,128)(2,1)S(1)} %get-tuple-element.20.both_ref.left_ref.right_ref, bf16[1280,640]{1,0:T(8,128)(2,1)S(1)} %copy-done.6, ...), custom_call_target="tpu_custom_call" | custom-call | flops 2516582400 | bytes 10485760 | tf_op jit(solution)/shard_map/memory_grad_rest/pallas_call | solution.py:273
  51.6 0.0 collective-permute-done.3
  51.6 5.4 %collective-permute-done.6 = f32[128,640]{1,0:T(8,128)S(1)} collective-permute-done((f32[128,640]{1,0:T(8,128)S(1)}, f32[128,640]{1,0:T(8,128)S(1)}, u32[]{:S(2)}, u32[]{:S(2)}) %collective-permute-start.6) | collective-permute-done | bytes 327712 | tf_op jit(solution)/shard_map/ppermute | solution.py:303
  57.0 0.8 bitcast_add_fusion.11
  57.8 0.0 collective-permute-start.4
  57.8 0.0 collective-permute-start.7
  57.8 0.0 collective-permute-done.9
  57.8 0.0 collective-permute-done.12
  57.8 0.8 bitcast_add_fusion.5
  58.6 2.7 %collective-permute-start.10 = (f32[128,640]{1,0:T(8,128)}, f32[128,640]{1,0:T(8,128)S(1)}, u32[]{:S(2)}, u32[]{:S(2)}) collective-permute-start(f32[128,640]{1,0:T(8,128)} %get-tuple-element.33), channel_id=1, source_target_pairs={{0,3},{1,0},{2,1},{3,2},{4,7},{5,4},{6,5},{7,6},{8,11},{9,8},{10,9... | collective-permute-start | bytes 983048 | tf_op jit(solution)/shard_map/ppermute | solution.py:304
  61.3 1.4 collective-permute-start.13
  62.8 2.4 %collective-permute-done.4 = f32[128,640]{1,0:T(8,128)S(1)} collective-permute-done((f32[128,640]{1,0:T(8,128)}, f32[128,640]{1,0:T(8,128)S(1)}, u32[]{:S(2)}, u32[]{:S(2)}) %collective-permute-start.4) | collective-permute-done | bytes 327712 | tf_op jit(solution)/shard_map/ppermute | solution.py:303
  65.2 7.3 %collective-permute-done.7 = f32[128,640]{1,0:T(8,128)} collective-permute-done((f32[128,640]{1,0:T(8,128)S(1)}, f32[128,640]{1,0:T(8,128)}, u32[]{:S(2)}, u32[]{:S(2)}) %collective-permute-start.7) | collective-permute-done | bytes 327712 | tf_op jit(solution)/shard_map/ppermute | solution.py:303
  72.5 1.3 bitcast_add_fusion.10
  73.7 0.1 collective-permute-start.5
  73.8 0.1 collective-permute-start.8
  73.9 0.0 collective-permute-done.10
  73.9 0.0 collective-permute-done.13
  73.9 1.1 bitcast_add_fusion.4
  75.0 2.7 %collective-permute-start.11 = (f32[128,640]{1,0:T(8,128)S(1)}, f32[128,640]{1,0:T(8,128)S(1)}, u32[]{:S(2)}, u32[]{:S(2)}) collective-permute-start(f32[128,640]{1,0:T(8,128)S(1)} %get-tuple-element.31), channel_id=1, source_target_pairs={{0,3},{1,0},{2,1},{3,2},{4,7},{5,4},{6,5},{7,6},{8,11},{9,8},{10,9... | collective-permute-start | bytes 983048 | tf_op jit(solution)/shard_map/ppermute | solution.py:304
  77.7 1.4 collective-permute-start.14
  79.1 0.8 ranks.1
  79.9 1.0 collective-permute-done.5
  80.9 6.3 %collective-permute-done.8 = f32[128,640]{1,0:T(8,128)S(1)} collective-permute-done((f32[128,640]{1,0:T(8,128)S(1)}, f32[128,640]{1,0:T(8,128)S(1)}, u32[]{:S(2)}, u32[]{:S(2)}) %collective-permute-start.8) | collective-permute-done | bytes 327712 | tf_op jit(solution)/shard_map/ppermute | solution.py:303
  87.2 1.2 bitcast_add_fusion.9
  88.5 0.0 collective-permute-done.11
  88.5 0.0 collective-permute-done.14
  88.5 0.1 bitcast_add_fusion.3
  88.5 0.1 pad_maximum_fusion
  88.6 13.9 %pack.1 = f32[5248,128]{1,0:T(8,128)S(1)} custom-call(f32[256,640]{1,0:T(8,128)S(1)} %get-tuple-element.47.left_ref, f32[256,640]{1,0:T(8,128)S(1)} %get-tuple-element.48.right_ref, s32[8,256]{1,0:T(8,128)S(1)} %dynamic-slice_bitcast_fusion.owners_ref, s32[8,256]{1,0:T(8,128)S(1)} %get-tuple-element.25.ranks_ref, f32[128,128]{1,0:T(8,128)S(1)} %get-tuple-element.26.sent_ref), custom_call_target="tpu_custom_call" | custom-call | flops 8589934592 | bytes 6291456 | tf_op jit(solution)/shard_map/pack/pallas_call | solution.py:326
  102.5 0.0 copy-start.15
  102.5 0.0 copy-start.16
  102.6 53.7 %all_to_all.5 = f32[128,1,5248]{2,1,0:T(1,128)S(1)} all-to-all(f32[128,1,5248]{2,1,0:T(1,128)S(1)} %bitcast.43), channel_id=1, replica_groups=mesh['dp'=32,'tensor'=4] {'dp','tensor'}, dimensions={0} | all-to-all | bytes 5373952 | tf_op jit(solution)/shard_map/all_to_all | solution.py:347
  156.3 3.0 %update.1 = (f32[160,512]{1,0:T(8,128)}, f32[160,512]{1,0:T(8,128)}) custom-call(f32[5248,128]{1,0:T(8,128)S(1)} %bitcast.44, f32[160,512]{1,0:T(8,128)S(1)} %bitcast.46, f32[160,512]{1,0:T(8,128)S(1)} %bitcast.47), custom_call_target="tpu_custom_call" | custom-call | flops 1342177280 | bytes 5242880 | tf_op jit(solution)/shard_map/update/pallas_call | solution.py:356
  159.3 1.6 fusion
  (25 shorter events, 0.1 us)
Async XLA Ops:
  7.2 152.1 %reduce-scatter.2.cloned.1.call-start = ((), (), s32[]{:S(2)}) async-start(), calls=%async_computation.2 | async-start | bytes 6758400 | tf_op jit(solution)/shard_map/reduce_scatter | solution.py:322
  7.2 1.4 copy-start.4
  8.6 1.4 copy-start.7
  10.1 1.3 copy-start.10
  11.4 1.3 copy-start.11
  12.7 1.7 %copy-start.13 = (bf16[1024,1280]{1,0:T(8,128)(2,1)S(1)}, bf16[1024,1280]{1,0:T(8,128)(2,1)}, u32[]{:S(2)}) copy-start(bf16[1024,1280]{1,0:T(8,128)(2,1)} %memory_ref.3) | copy-start | bytes 7864324
  19.6 5.9 %collective-permute-start = (f32[2,1024]{1,0:T(2,128)S(1)}, f32[2,1024]{1,0:T(2,128)S(1)}, u32[]{:S(2)}, u32[]{:S(2)}) collective-permute-start(f32[2,1024]{1,0:T(2,128)S(1)} %get-tuple-element.17.p0), channel_id=1, source_target_pairs={{0,1},{1,2},{2,3},{3,0},{4,5},{5,6},{6,7},{7,4},{8,9},{9,10},{10,1... | collective-permute-start | bytes 24584 | tf_op jit(solution)/shard_map/ppermute | solution.py:237
  21.8 4.0 %collective-permute-start.1 = (f32[2,1024]{1,0:T(2,128)S(1)}, f32[2,1024]{1,0:T(2,128)S(1)}, u32[]{:S(2)}, u32[]{:S(2)}) collective-permute-start(f32[2,1024]{1,0:T(2,128)S(1)} %get-tuple-element.17.p0), channel_id=1, source_target_pairs={{0,2},{1,3},{2,0},{3,1},{4,6},{5,7},{6,4},{7,5},{8,10},{9,11},{10,... | collective-permute-start | bytes 24584 | tf_op jit(solution)/shard_map/ppermute | solution.py:237
  24.4 2.8 %collective-permute-start.2 = (f32[2,1024]{1,0:T(2,128)S(1)}, f32[2,1024]{1,0:T(2,128)S(1)}, u32[]{:S(2)}, u32[]{:S(2)}) collective-permute-start(f32[2,1024]{1,0:T(2,128)S(1)} %get-tuple-element.17.p0), channel_id=1, source_target_pairs={{0,3},{1,0},{2,1},{3,2},{4,7},{5,4},{6,5},{7,6},{8,11},{9,8},{10,9... | collective-permute-start | bytes 24584 | tf_op jit(solution)/shard_map/ppermute | solution.py:237
  27.2 2.1 %copy-start.14 = (bf16[1024,1280]{1,0:T(8,128)(2,1)S(1)}, bf16[1024,1280]{1,0:T(8,128)(2,1)}, u32[]{:S(2)}) copy-start(bf16[1024,1280]{1,0:T(8,128)(2,1)} %memory_ref.3) | copy-start | bytes 7864324
  34.1 2.7 %copy-start = (f32[1280,1280]{1,0:T(8,128)}, f32[1280,1280]{1,0:T(8,128)S(1)}, u32[]{:S(2)}) copy-start(f32[1280,1280]{1,0:T(8,128)S(1)} %weight_grad.1) | copy-start | bytes 19660804
  36.8 1.4 copy-start.5
  38.3 1.4 copy-start.8
  39.7 6.3 %copy-start.9 = (bf16[1280,640]{1,0:T(8,128)(2,1)S(1)}, bf16[1280,640]{1,0:T(8,128)(2,1)}, u32[]{:S(2)}) copy-start(bf16[1280,640]{1,0:T(8,128)(2,1)} %wv_ref.5) | copy-start | bytes 4915204
  41.5 4.4 %copy-start.6 = (bf16[1280,640]{1,0:T(8,128)(2,1)S(1)}, bf16[1280,640]{1,0:T(8,128)(2,1)}, u32[]{:S(2)}) copy-start(bf16[1280,640]{1,0:T(8,128)(2,1)} %wk_ref.5) | copy-start | bytes 4915204
  41.6 10.0 %collective-permute-start.3 = (f32[128,640]{1,0:T(8,128)S(1)}, f32[128,640]{1,0:T(8,128)S(1)}, u32[]{:S(2)}, u32[]{:S(2)}) collective-permute-start(f32[128,640]{1,0:T(8,128)S(1)} %get-tuple-element.43), channel_id=1, source_target_pairs={{0,1},{1,2},{2,3},{3,0},{4,5},{5,6},{6,7},{7,4},{8,9},{9,10},{10,1... | collective-permute-start | bytes 983048 | tf_op jit(solution)/shard_map/ppermute | solution.py:303
  41.7 15.3 %collective-permute-start.6 = (f32[128,640]{1,0:T(8,128)S(1)}, f32[128,640]{1,0:T(8,128)S(1)}, u32[]{:S(2)}, u32[]{:S(2)}) collective-permute-start(f32[128,640]{1,0:T(8,128)S(1)} %get-tuple-element.44), channel_id=1, source_target_pairs={{0,1},{1,2},{2,3},{3,0},{4,5},{5,6},{6,7},{7,4},{8,9},{9,10},{10,1... | collective-permute-start | bytes 983048 | tf_op jit(solution)/shard_map/ppermute | solution.py:303
  42.6 15.2 %collective-permute-start.9 = (f32[128,640]{1,0:T(8,128)S(1)}, f32[128,640]{1,0:T(8,128)S(1)}, u32[]{:S(2)}, u32[]{:S(2)}) collective-permute-start(f32[128,640]{1,0:T(8,128)S(1)} %get-tuple-element.41), channel_id=1, source_target_pairs={{0,3},{1,0},{2,1},{3,2},{4,7},{5,4},{6,5},{7,6},{8,11},{9,8},{10,9... | collective-permute-start | bytes 983048 | tf_op jit(solution)/shard_map/ppermute | solution.py:304
  44.6 13.3 %collective-permute-start.12 = (f32[128,640]{1,0:T(8,128)S(1)}, f32[128,640]{1,0:T(8,128)S(1)}, u32[]{:S(2)}, u32[]{:S(2)}) collective-permute-start(f32[128,640]{1,0:T(8,128)S(1)} %get-tuple-element.42), channel_id=1, source_target_pairs={{0,3},{1,0},{2,1},{3,2},{4,7},{5,4},{6,5},{7,6},{8,11},{9,8},{10,9... | collective-permute-start | bytes 983048 | tf_op jit(solution)/shard_map/ppermute | solution.py:304
  51.6 7.1 %copy-start.1 = (f32[3,256,640]{2,1,0:T(8,128)}, f32[3,256,640]{2,1,0:T(8,128)S(1)}, u32[]{:S(2)}) copy-start(f32[3,256,640]{2,1,0:T(8,128)S(1)} %get-tuple-element.24) | copy-start | bytes 5898244
  51.6 7.1 %copy-start.3 = (f32[3,256,640]{2,1,0:T(8,128)}, f32[3,256,640]{2,1,0:T(8,128)S(1)}, u32[]{:S(2)}) copy-start(f32[3,256,640]{2,1,0:T(8,128)S(1)} %get-tuple-element.22) | copy-start | bytes 5898244
  57.8 7.3 %collective-permute-start.4 = (f32[128,640]{1,0:T(8,128)}, f32[128,640]{1,0:T(8,128)S(1)}, u32[]{:S(2)}, u32[]{:S(2)}) collective-permute-start(f32[128,640]{1,0:T(8,128)} %get-tuple-element.39), channel_id=1, source_target_pairs={{0,1},{1,2},{2,3},{3,0},{4,5},{5,6},{6,7},{7,4},{8,9},{9,10},{10,1... | collective-permute-start | bytes 983048 | tf_op jit(solution)/shard_map/ppermute | solution.py:303
  57.8 14.6 %collective-permute-start.7 = (f32[128,640]{1,0:T(8,128)S(1)}, f32[128,640]{1,0:T(8,128)}, u32[]{:S(2)}, u32[]{:S(2)}) collective-permute-start(f32[128,640]{1,0:T(8,128)S(1)} %get-tuple-element.40), channel_id=1, source_target_pairs={{0,1},{1,2},{2,3},{3,0},{4,5},{5,6},{6,7},{7,4},{8,9},{9,10},{10,1... | collective-permute-start | bytes 983048 | tf_op jit(solution)/shard_map/ppermute | solution.py:303
  58.6 15.3 %copy-start.2 = (f32[3,256,640]{2,1,0:T(8,128)S(1)}, f32[3,256,640]{2,1,0:T(8,128)}, u32[]{:S(2)}) copy-start(f32[3,256,640]{2,1,0:T(8,128)} %copy-done.1) | copy-start | bytes 5898244
  58.6 15.3 %collective-permute-start.10 = (f32[128,640]{1,0:T(8,128)}, f32[128,640]{1,0:T(8,128)S(1)}, u32[]{:S(2)}, u32[]{:S(2)}) collective-permute-start(f32[128,640]{1,0:T(8,128)} %get-tuple-element.33), channel_id=1, source_target_pairs={{0,3},{1,0},{2,1},{3,2},{4,7},{5,4},{6,5},{7,6},{8,11},{9,8},{10,9... | collective-permute-start | bytes 983048 | tf_op jit(solution)/shard_map/ppermute | solution.py:304
  61.3 12.6 %collective-permute-start.13 = (f32[128,640]{1,0:T(8,128)S(1)}, f32[128,640]{1,0:T(8,128)}, u32[]{:S(2)}, u32[]{:S(2)}) collective-permute-start(f32[128,640]{1,0:T(8,128)S(1)} %get-tuple-element.34), channel_id=1, source_target_pairs={{0,3},{1,0},{2,1},{3,2},{4,7},{5,4},{6,5},{7,6},{8,11},{9,8},{10,9... | collective-permute-start | bytes 983048 | tf_op jit(solution)/shard_map/ppermute | solution.py:304
  62.8 16.3 %copy-start.12 = (s32[1024,8]{0,1:T(8,128)S(1)}, s32[1024,8]{0,1:T(8,128)}, u32[]{:S(2)}) copy-start(s32[1024,8]{0,1:T(8,128)} %param.14) | copy-start | bytes 98308
  62.8 16.3 %copy-start.17 = (s32[1024,8]{0,1:T(8,128)S(1)}, s32[1024,8]{0,1:T(8,128)}, u32[]{:S(2)}) copy-start(s32[1024,8]{0,1:T(8,128)} %param.15) | copy-start | bytes 98308
  73.7 7.2 %collective-permute-start.5 = (f32[128,640]{1,0:T(8,128)S(1)}, f32[128,640]{1,0:T(8,128)S(1)}, u32[]{:S(2)}, u32[]{:S(2)}) collective-permute-start(f32[128,640]{1,0:T(8,128)S(1)} %get-tuple-element.37), channel_id=1, source_target_pairs={{0,1},{1,2},{2,3},{3,0},{4,5},{5,6},{6,7},{7,4},{8,9},{9,10},{10,1... | collective-permute-start | bytes 983048 | tf_op jit(solution)/shard_map/ppermute | solution.py:303
  73.8 13.4 %collective-permute-start.8 = (f32[128,640]{1,0:T(8,128)S(1)}, f32[128,640]{1,0:T(8,128)S(1)}, u32[]{:S(2)}, u32[]{:S(2)}) collective-permute-start(f32[128,640]{1,0:T(8,128)S(1)} %get-tuple-element.38), channel_id=1, source_target_pairs={{0,1},{1,2},{2,3},{3,0},{4,5},{5,6},{6,7},{7,4},{8,9},{9,10},{10,1... | collective-permute-start | bytes 983048 | tf_op jit(solution)/shard_map/ppermute | solution.py:303
  75.0 13.5 %collective-permute-start.11 = (f32[128,640]{1,0:T(8,128)S(1)}, f32[128,640]{1,0:T(8,128)S(1)}, u32[]{:S(2)}, u32[]{:S(2)}) collective-permute-start(f32[128,640]{1,0:T(8,128)S(1)} %get-tuple-element.31), channel_id=1, source_target_pairs={{0,3},{1,0},{2,1},{3,2},{4,7},{5,4},{6,5},{7,6},{8,11},{9,8},{10,9... | collective-permute-start | bytes 983048 | tf_op jit(solution)/shard_map/ppermute | solution.py:304
  77.7 10.7 %collective-permute-start.14 = (f32[128,640]{1,0:T(8,128)S(1)}, f32[128,640]{1,0:T(8,128)S(1)}, u32[]{:S(2)}, u32[]{:S(2)}) collective-permute-start(f32[128,640]{1,0:T(8,128)S(1)} %get-tuple-element.32), channel_id=1, source_target_pairs={{0,3},{1,0},{2,1},{3,2},{4,7},{5,4},{6,5},{7,6},{8,11},{9,8},{10,9... | collective-permute-start | bytes 983048 | tf_op jit(solution)/shard_map/ppermute | solution.py:304
  102.5 53.7 %copy-start.15 = (f32[512,160]{0,1:T(8,128)S(1)}, f32[512,160]{0,1:T(8,128)}, u32[]{:S(2)}) copy-start(f32[512,160]{0,1:T(8,128)} %param.16) | copy-start | bytes 983044
  102.5 53.7 %copy-start.16 = (f32[512,160]{0,1:T(8,128)S(1)}, f32[512,160]{0,1:T(8,128)}, u32[]{:S(2)}) copy-start(f32[512,160]{0,1:T(8,128)} %param.17) | copy-start | bytes 983044
Sparse Core Ops, SparseCore 0:
  36.9 103.9 reduce-scatter.1

commit v2 on v1

v2 whole, which is shorter than its diff:
```python
import functools

import jax
import jax.numpy as jnp
from jax import lax
from jax.experimental import pallas as pl
from jax.experimental.pallas import tpu as pltpu
from jax.sharding import PartitionSpec as P

D = 2560
HEADS = 8
EH = 160
MAIN = 128
TAIL = EH - MAIN
CAP = 32
GROUP = CAP // 4
CHUNK = CAP + GROUP + 1
LEARN_RATE = 0.5
EPSILON = 1e-06
F32 = jnp.float32
BF16 = jnp.bfloat16
OVER_ROWS = (((0,), (0,)), ((), ()))
OVER_LANES = (((1,), (1,)), ((), ()))


def params(mib):
    return pltpu.CompilerParams(vmem_limit_bytes=mib << 20)


def cost(flops, moved):
    return pl.CostEstimate(flops=flops, bytes_accessed=moved, transcendentals=0)


def row_sums(x):
    lanes = x[:, :128]
    for at in range(128, x.shape[1], 128):
        lanes = lanes + x[:, at : at + 128]
    return jnp.sum(lanes.T, axis=0, keepdims=True)


def as_columns(row, width):
    column = jnp.broadcast_to(row, (128, row.shape[1])).T
    return jnp.concatenate([column] * (width // 128), axis=1)


def ranks_kernel(at_ref, owners_ref, slots_ref, select_ref, group_ref, sent_ref):
    count = owners_ref.shape[1]
    owners = owners_ref[...]
    slot_plus = slots_ref[...] + 1
    ids = lax.broadcasted_iota(jnp.int32, (128, count), 0)
    hits = jnp.zeros((128, count), F32)
    for h in range(HEADS):
        hits = hits + jnp.where(owners[h : h + 1] == ids, 1.0, 0.0)
    earlier = lax.broadcasted_iota(jnp.int32, (count, count), 0) < lax.broadcasted_iota(
        jnp.int32, (count, count), 1
    )
    before = jnp.dot(
        hits.astype(BF16), jnp.where(earlier, 1.0, 0.0).astype(BF16), preferred_element_type=F32
    )
    high = jnp.zeros((128, 128), F32)
    low = jnp.zeros((128, 128), F32)
    for h in range(HEADS):
        match = owners[h : h + 1] == ids
        rank = jnp.sum(jnp.where(match, before, 0.0), axis=0, keepdims=True).astype(jnp.int32)
        place = jnp.where(rank == ids, 1.0, 0.0).astype(BF16)
        slot = slot_plus[h : h + 1]
        upper = jnp.where(match, (slot // 16).astype(F32), 0.0).astype(BF16)
        lower = jnp.where(match, (slot % 16).astype(F32), 0.0).astype(BF16)
        high = high + lax.dot_general(upper, place, OVER_LANES, preferred_element_type=F32)
        low = low + lax.dot_general(lower, place, OVER_LANES, preferred_element_type=F32)
        columns = slice(h * count, (h + 1) * count)
        group_ref[columns, :] = jnp.broadcast_to((rank // GROUP).astype(F32), (128, count)).T
        within = jnp.where(match, rank % GROUP, -1)
        for k in range(GROUP):
            select_ref[k * 128 : (k + 1) * 128, columns] = jnp.where(within == k, 1.0, 0.0).astype(
                BF16
            )
    sent_ref[...] = 16.0 * high + low


def forward_kernel(
    at_ref, memory_ref, hidden_ref, grad_ref, wk_ref, wv_ref, key_ref, part_ref, first_ref
):
    @pl.when(pl.program_id(0) == at_ref[0])
    def _():
        width = hidden_ref.shape[1]
        first_ref[:, :width] = hidden_ref[...]
        first_ref[:, width:] = grad_ref[...]

    memory = memory_ref[...]
    proj_key = jnp.dot(memory, wk_ref[...], preferred_element_type=F32)
    key_ref[...] = proj_key
    part_ref[0:1, :] = row_sums(hidden_ref[...].astype(F32) * proj_key)
    proj_value = jnp.dot(memory, wv_ref[...], preferred_element_type=F32)
    part_ref[1:2, :] = row_sums(grad_ref[...].astype(F32) * proj_value)


def gate_columns(total, width):
    root = jnp.sqrt(jnp.full((1, 1), D, F32))
    gate = jax.nn.sigmoid(total[0:1] / root)
    score = total[1:2] * gate * (1.0 - gate) / root
    return as_columns(gate, width), as_columns(score, width)


def backward_tile(total, hidden_ref, grad_ref):
    gates, scores = gate_columns(total, hidden_ref.shape[1])
    key_grad = (scores * hidden_ref[...].astype(F32)).astype(BF16)
    value_grad = (gates * grad_ref[...].astype(F32)).astype(BF16)
    return key_grad, value_grad, scores


def memory_grad_tile(key_grad, value_grad, wk_ref, wv_ref, top_ref, low_ref):
    top = top_ref.shape[0]
    for h in range(HEADS):
        rows = slice(h * EH, (h + 1) * EH)
        head = lax.dot_general(
            key_grad, wk_ref[rows, :], OVER_LANES, preferred_element_type=F32
        ) + lax.dot_general(value_grad, wv_ref[rows, :], OVER_LANES, preferred_element_type=F32)
        main = slice(h * MAIN, (h + 1) * MAIN)
        tail = slice(HEADS * MAIN + h * TAIL, HEADS * MAIN + (h + 1) * TAIL)
        top_ref[:, main] = head[:top, :MAIN]
        top_ref[:, tail] = head[:top, MAIN:]
        low_ref[:, main] = head[top:, :MAIN]
        low_ref[:, tail] = head[top:, MAIN:]


def first_kernel(
    at_ref, p0, p1, p2, p3, first_ref, wk_ref, wv_ref, top_ref, low_ref, total_ref
):
    total_ref[...] = (p0[...] + p1[...]) + (p2[...] + p3[...])
    count, width = first_ref.shape[0], first_ref.shape[1] // 2
    total = total_ref[:, pl.ds(pl.multiple_of(at_ref[0] * count, count), count)]
    key_grad, value_grad, _ = backward_tile(
        total, first_ref.at[:, :width], first_ref.at[:, width:]
    )
    memory_grad_tile(key_grad, value_grad, wk_ref, wv_ref, top_ref, low_ref)


def gate_kernel(total_ref, hidden_ref, grad_ref, both_ref):
    width = hidden_ref.shape[1]
    key_grad, value_grad, _ = backward_tile(total_ref[...], hidden_ref, grad_ref)
    both_ref[:, :width] = key_grad
    both_ref[:, width:] = value_grad


def hidden_grad_kernel(total_ref, key_ref, out_ref):
    _, scores = gate_columns(total_ref[...], key_ref.shape[1])
    out_ref[...] = (scores * key_ref[...]).astype(BF16)


def rest_kernel(at_ref, both_ref, wk_ref, wv_ref, top_ref, low_ref):
    width = wk_ref.shape[1]
    memory_grad_tile(
        both_ref[:, :width], both_ref[:, width:], wk_ref, wv_ref, top_ref.at[0], low_ref.at[0]
    )


def weight_grad_kernel(at_ref, memory_ref, both_ref, mine_ref, other_ref):
    i = pl.program_id(0)
    block = mine_ref.shape[0] // 16
    rows = memory_ref.shape[1]
    me_x, me_z, me_core = at_ref[0], at_ref[1], at_ref[2]

    def order(r):
        return jnp.where(r == 0, 0, jnp.where(r == 3, 1, r + 1))

    found = lax.dot_general(
        memory_ref[...], both_ref[...], OVER_ROWS, preferred_element_type=F32
    )
    for p in range(rows // block):
        x = order((i * 2 + p // 8) ^ me_x)
        z = order((p % 8 // 2) ^ me_z)
        place = x * 4 + z if p % 2 == 0 else z * 4 + x
        to = pl.ds(pl.multiple_of(place * block, 8), block)
        value = found[p * block : (p + 1) * block]

        @pl.when(me_core == p % 2)
        def _():
            mine_ref[to, :] = value

        @pl.when(me_core != p % 2)
        def _():
            other_ref[to, :] = value


def pack_kernel(top_ref, low_ref, select_ref, group_ref, sent_ref, out_ref, rows):
    count = top_ref.shape[0] + low_ref.shape[0]

    def summed(cols):
        return jnp.concatenate([top_ref[:, cols], low_ref[:, cols]], axis=0)

    lane_group = lax.broadcasted_iota(jnp.int32, (count, 128), 1) // TAIL
    for j in range(5):
        for h in range(HEADS):
            group = group_ref[h * count : (h + 1) * count, :]
            if j < 4:
                value = jnp.where(group == j, summed(slice(h * MAIN, (h + 1) * MAIN)), 0.0)
            else:
                at = HEADS * MAIN + h * TAIL
                tail = summed(slice(at, at + TAIL))
                tail = jnp.concatenate([tail] * 4, axis=1)
                value = jnp.where(group == lane_group.astype(F32), tail, 0.0)
            top = value.astype(BF16)
            rows[j, h * count : (h + 1) * count, :MAIN] = top
            rows[j, h * count : (h + 1) * count, MAIN:] = (value - top.astype(F32)).astype(BF16)
        found = jnp.dot(select_ref[...], rows[j], preferred_element_type=F32)
        found = found[:, :MAIN] + found[:, MAIN:]
        for k in range(GROUP):
            out_ref[pl.ds(j * GROUP + k, 128, stride=CHUNK), :] = found[k * 128 : (k + 1) * 128]
    out_ref[pl.ds(CAP + GROUP, 128, stride=CHUNK), :] = sent_ref[...]


def update_kernel(got_ref, table_ref, sums_ref, new_table_ref, new_sum_ref, values, select):
    owned = table_ref.shape[1]
    slots = got_ref[pl.ds(CAP + GROUP, 128, stride=CHUNK), :]
    ids = (lax.broadcasted_iota(jnp.int32, (128, owned), 1) + 1).astype(F32)
    for k in range(CAP):
        at = slice(k * 128, (k + 1) * 128)
        select[at, :] = jnp.where(slots[:, k : k + 1] == ids, 1.0, 0.0).astype(BF16)
        main = got_ref[pl.ds(k, 128, stride=CHUNK), :].T
        top = main.astype(BF16)
        values[:MAIN, at] = top
        values[EH : EH + MAIN, at] = (main - top.astype(F32)).astype(BF16)
    for k in range(GROUP):
        tail = got_ref[pl.ds(CAP + k, 128, stride=CHUNK), :].T
        top = tail.astype(BF16)
        rest = (tail - top.astype(F32)).astype(BF16)
        for j in range(4):
            at = slice((j * GROUP + k) * 128, (j * GROUP + k + 1) * 128)
            values[MAIN:EH, at] = top[j * TAIL : (j + 1) * TAIL]
            values[EH + MAIN :, at] = rest[j * TAIL : (j + 1) * TAIL]
    both = jnp.dot(values[...], select[...], preferred_element_type=F32)
    row_sum = both[:EH] + both[EH:]
    new_sum = sums_ref[...] + row_sum * row_sum
    new_sum_ref[...] = new_sum
    new_table_ref[...] = table_ref[...] - LEARN_RATE * row_sum / (jnp.sqrt(new_sum) + EPSILON)


def whole(shape):
    return pl.BlockSpec(shape, lambda *_: (0,) * len(shape))


def body(hidden, out_grad, memory, w_key, w_value, row_owner, row_slot, mem_table, adagrad_sum):
    tokens, width = hidden.shape
    depth = memory.shape[1]
    quarter = tokens // 4
    tile = 256
    tiles = tokens // tile

    position = lax.axis_index("dp").astype(jnp.int32)
    core = position & 1
    place = jnp.stack([position >> 3, (position >> 1) & 3, core])
    at = jnp.stack([lax.axis_index("tensor").astype(jnp.int32), core])

    def quarter_at(p, s):
        return (s[0] + 4 + (1 + p) * (2 * s[1] - 1)) & 3

    start = quarter_at(0, at).reshape(1)

    def by_rows(cols):
        return pl.BlockSpec((tile, cols), lambda i, s: (i, 0))

    chunk = whole((quarter, 2 * width))
    proj_key, part, first_both = pl.pallas_call(
        forward_kernel,
        grid_spec=pltpu.PrefetchScalarGridSpec(
            num_scalar_prefetch=1,
            grid=(tiles,),
            in_specs=[
                by_rows(depth),
                by_rows(width),
                by_rows(width),
                whole((depth, width)),
                whole((depth, width)),
            ],
            out_specs=[
                by_rows(width),
                pl.BlockSpec((2, tile), lambda i, s: (0, i)),
                chunk,
            ],
        ),
        out_shape=[
            jax.ShapeDtypeStruct((tokens, width), F32),
            jax.ShapeDtypeStruct((2, tokens), F32),
            jax.ShapeDtypeStruct((quarter, 2 * width), BF16),
        ],
        compiler_params=params(58),
        cost_estimate=cost(4 * tokens * depth * width, 12 << 20),
        name="forward",
    )(start, memory, hidden, out_grad, w_key, w_value)
    parts = [part] + [
        lax.ppermute(part, "tensor", [(i, (i + step) % 4) for i in range(4)]) for step in (1, 2, 3)
    ]

    def swapped(value, bits):
        def goal(i):
            dp, tensor = i // 4, i % 4
            by = bits[dp % 2]
            return (dp ^ by[0]) * 4 + (tensor ^ by[1])

        return lax.ppermute(value, ("dp", "tensor"), [(i, goal(i)) for i in range(128)])

    def turned(value):
        def goal(i):
            return i // 4 * 4 + (i + (1, 3)[i // 4 % 2]) % 4

        return lax.ppermute(value, ("dp", "tensor"), [(i, goal(i)) for i in range(128)])

    def tile_spec(cols):
        return pl.BlockSpec((quarter, cols), lambda p, s: (quarter_at(p, s), 0))

    weights = [whole((depth, width))] * 2
    part_whole = whole((2, tokens))
    top = 136
    low = quarter - top
    first_top, first_low, total = pl.pallas_call(
        first_kernel,
        grid_spec=pltpu.PrefetchScalarGridSpec(
            num_scalar_prefetch=1,
            grid=(1,),
            in_specs=[part_whole] * 4 + [chunk] + weights,
            out_specs=[whole((top, depth)), whole((low, depth)), part_whole],
        ),
        out_shape=[
            jax.ShapeDtypeStruct((top, depth), F32),
            jax.ShapeDtypeStruct((low, depth), F32),
            jax.ShapeDtypeStruct((2, tokens), F32),
        ],
        compiler_params=params(20),
        cost_estimate=cost(4 * quarter * depth * width, 6 << 20),
        name="first",
    )(start, *parts, first_both, w_key, w_value)

    def by_rows(cols):
        return pl.BlockSpec((quarter, cols), lambda i: (i, 0))

    total_spec = pl.BlockSpec((2, quarter), lambda i: (0, i))
    both = pl.pallas_call(
        gate_kernel,
        grid=(4,),
        in_specs=[total_spec] + [by_rows(width)] * 2,
        out_specs=by_rows(2 * width),
        out_shape=jax.ShapeDtypeStruct((tokens, 2 * width), BF16),
        compiler_params=params(24),
        cost_estimate=cost(1, 1),
        name="gate",
    )(total, hidden, out_grad)

    grad_spec = whole((depth // 2, 2 * width))
    mine, other = pl.pallas_call(
        weight_grad_kernel,
        grid_spec=pltpu.PrefetchScalarGridSpec(
            num_scalar_prefetch=1,
            grid=(2,),
            in_specs=[
                pl.BlockSpec((tokens, depth // 2), lambda i, s: (0, i)),
                whole((tokens, 2 * width)),
            ],
            out_specs=[grad_spec, grad_spec],
        ),
        out_shape=[jax.ShapeDtypeStruct((depth // 2, 2 * width), F32)] * 2,
        compiler_params=params(32),
        cost_estimate=cost(1, 1),
        name="weight_grad",
    )(place, memory, both)
    late, _ = lax.optimization_barrier((both, other))
    rest_top, rest_low = pl.pallas_call(
        rest_kernel,
        grid_spec=pltpu.PrefetchScalarGridSpec(
            num_scalar_prefetch=1,
            grid=(3,),
            in_specs=[
                pl.BlockSpec((quarter, 2 * width), lambda p, s: (quarter_at(p + 1, s), 0)),
                *weights,
            ],
            out_specs=[
                pl.BlockSpec((1, top, depth), lambda p, s: (p, 0, 0)),
                pl.BlockSpec((1, low, depth), lambda p, s: (p, 0, 0)),
            ],
        ),
        out_shape=[
            jax.ShapeDtypeStruct((3, top, depth), F32),
            jax.ShapeDtypeStruct((3, low, depth), F32),
        ],
        compiler_params=params(24),
        cost_estimate=cost(1, 1),
        name="rest",
    )(at, late, w_key, w_value)

    def folded(value, bits):
        half = value.shape[0] // 2
        return value[:half] + swapped(value[half:], bits)

    moved_top = turned(first_top) + rest_top[0]
    moved_low = turned(first_low) + rest_low[0]
    moved_top, owners, slots = lax.optimization_barrier((moved_top, row_owner.T, row_slot.T))
    passed_top = turned(moved_top)
    passed_low = turned(moved_low)
    select, group, sent = pl.pallas_call(
        ranks_kernel,
        grid_spec=pltpu.PrefetchScalarGridSpec(
            num_scalar_prefetch=1,
            grid=(1,),
            in_specs=[pl.BlockSpec((HEADS, quarter), lambda i, s: (0, s[0]))] * 2,
            out_specs=[
                whole((GROUP * 128, HEADS * quarter)),
                whole((HEADS * quarter, 128)),
                whole((128, 128)),
            ],
        ),
        out_shape=[
            jax.ShapeDtypeStruct((GROUP * 128, HEADS * quarter), BF16),
            jax.ShapeDtypeStruct((HEADS * quarter, 128), F32),
            jax.ShapeDtypeStruct((128, 128), F32),
        ],
        compiler_params=params(32),
        cost_estimate=cost(1 << 36, 1 << 27),
        name="ranks",
    )(at, owners, slots)
    mine, select = lax.optimization_barrier((mine, select))
    pair = mine + swapped(other, ((1, 0), (1, 0)))
    rest_low, pair = lax.optimization_barrier((rest_low, pair))
    moved_top = turned(passed_top + rest_top[1])
    moved_low = turned(passed_low + rest_low[1])
    grads = folded(pair, ((8, 0), (2, 0)))
    rest_low, grads = lax.optimization_barrier((rest_low, grads))
    sum_top = moved_top + rest_top[2]
    sum_low = moved_low + rest_low[2]
    grads = folded(grads, ((24, 0), (6, 0)))
    sum_low, grads = lax.optimization_barrier((sum_low, grads))
    grads = folded(grads, ((2, 0), (8, 0)))

    packed = pl.pallas_call(
        pack_kernel,
        grid=(1,),
        in_specs=[
            whole((top, depth)),
            whole((low, depth)),
            whole((GROUP * 128, HEADS * quarter)),
            whole((HEADS * quarter, 128)),
            whole((128, 128)),
        ],
        out_specs=whole((128 * CHUNK, 128)),
        out_shape=jax.ShapeDtypeStruct((128 * CHUNK, 128), F32),
        scratch_shapes=[pltpu.VMEM((5, HEADS * quarter, 256), BF16)],
        compiler_params=params(32),
        cost_estimate=cost(2 * 1024 * 2048 * 1280, 12 << 20),
        name="pack",
    )(sum_top, sum_low, select, group, sent)
    packed, grads, total = lax.optimization_barrier((packed, grads, total))
    hidden_grad = pl.pallas_call(
        hidden_grad_kernel,
        grid=(4,),
        in_specs=[total_spec, by_rows(width)],
        out_specs=by_rows(width),
        out_shape=jax.ShapeDtypeStruct((tokens, width), BF16),
        compiler_params=params(24),
        cost_estimate=cost(2 * tokens * width, 4 << 20),
        name="hidden_grad",
    )(total, proj_key)
    received = lax.all_to_all(
        packed.reshape(128, 1, CHUNK * 128),
        ("dp", "tensor"),
        split_axis=0,
        concat_axis=0,
        tiled=True,
    ).reshape(128 * CHUNK, 128)
    received, hidden_grad = lax.optimization_barrier((received, hidden_grad))
    owned = mem_table.shape[0]
    table_spec = whole((EH, owned))
    new_table, new_sum = pl.pallas_call(
        update_kernel,
        grid=(1,),
        in_specs=[whole((128 * CHUNK, 128)), table_spec, table_spec],
        out_specs=[table_spec, table_spec],
        out_shape=[jax.ShapeDtypeStruct((EH, owned), F32)] * 2,
        scratch_shapes=[
            pltpu.VMEM((2 * EH, CAP * 128), BF16),
            pltpu.VMEM((CAP * 128, owned), BF16),
        ],
        compiler_params=params(48),
        cost_estimate=cost(4 * EH * 4096 * 512, 5 << 20),
        name="update",
    )(received, mem_table.T, adagrad_sum.T)
    half = grads.shape[0] // 2
    last = swapped(grads[half:], ((6, 0), (24, 0)))
    kept, new_table = lax.optimization_barrier((grads[:half], new_table))
    key_weight_grad = kept[:, :width] + last[:, :width]
    value_weight_grad = kept[:, width:] + last[:, width:]
    return (hidden_grad, key_weight_grad, value_weight_grad, new_table.T, new_sum.T)


def solution(mesh):
    return jax.shard_map(
        body,
        mesh=mesh,
        in_specs=(
            P("dp", "tensor"),
            P("dp", "tensor"),
            P("dp", None),
            P(None, "tensor"),
            P(None, "tensor"),
            P("dp", None),
            P("dp", None),
            P(("dp", "tensor"), None),
            P(("dp", "tensor"), None),
        ),
        out_specs=(
            P("dp", "tensor"),
            P("dp", "tensor"),
            P("dp", "tensor"),
            P(("dp", "tensor"), None),
            P(("dp", "tensor"), None),
        ),
        check_vma=False,
    )
```

time: 168 us -> 144 us (0.86)
  blocking collectives: 53.7 us -> 0 us
  waiting for transfers between devices: 24.2 us -> 59.1 us
  between operations: 14.3 us -> 0.83 us
  starting transfers between devices: 18.6 us -> 31.8 us
  local copies, waits for them, and re-layouts: 14.6 us -> 9.77 us
  other arithmetic: 5.29 us -> 3.36 us
    all_to_all x1 -> x0, blocking collectives: 53.7 us -> none  [body(): lax.all_to_all(packed.reshape(128, 1, CHUNK * 128), ('dp', 'tensor'), spl...]
    all_to_all x0 -> x1, waiting for transfers between devices: none -> 30.4 us  [body(): lax.all_to_all(packed.reshape(128, 1, CHUNK * 128), ('dp', 'tensor'), spl...]
    all_to_all x0 -> x1, starting transfers between devices: none -> 9.68 us  [body(): lax.all_to_all(packed.reshape(128, 1, CHUNK * 128), ('dp', 'tensor'), spl...]
    ppermute x12 -> x11, starting transfers between devices: 12.7 us -> 17.4 us  [the longest x5 11.1 us: swapped(): lax.ppermute(value, ('dp', 'tensor'), [(i, goal(i)) for i in range(128)])]
    unnamed x36 -> x28, local copies, waits for them, and re-layouts: 12.8 us -> 8.87 us
    ppermute x12 -> x11, waiting for transfers between devices: 22.5 us -> 25.4 us  [the longest x6 13.5 us: turned(): lax.ppermute(value, ('dp', 'tensor'), [(i, goal(i)) for i in range(128)])]
    add x6 -> x11, other arithmetic: 5.2 us -> 3.21 us  [the longest x1 1.2 us: body(): moved_top = turned(first_top) + rest_top[0]]
    pallas_call x6 -> x7, Pallas kernels: 33.3 us -> 33.3 us  [the longest x1 8.47 us: body(): pl.pallas_call(forward_kernel, grid_spec=pltpu.PrefetchScalarGridSpec(num...]
  transfers between devices with their start and end apart: 16 -> 15, of which waited for: 7 -> 8; matrix products, arithmetic and copies ran while one was open for 3% -> 2% of each run, Pallas kernels for 15% -> 19%
where the time goes in v2:
time: 144 us
  waiting for transfers between devices  59.1 us (41%)
  Pallas kernels  38.7 us (27%)
  starting transfers between devices  31.8 us (22%)
  local copies, waits for them, and re-layouts  9.77 us (7%)
  other arithmetic  3.36 us (2%)
    all_to_all x1, waiting for transfers between devices, body(): lax.all_to_all(packed.reshape(128, 1, CHUNK * 128), ('dp', 'tensor'), spl...  30.4 us
    ppermute x6, waiting for transfers between devices, turned(): lax.ppermute(value, ('dp', 'tensor'), [(i, goal(i)) for i in range(128)])  13.5 us
    ppermute x5, waiting for transfers between devices, swapped(): lax.ppermute(value, ('dp', 'tensor'), [(i, goal(i)) for i in range(128)])  11.9 us
    ppermute x5, starting transfers between devices, swapped(): lax.ppermute(value, ('dp', 'tensor'), [(i, goal(i)) for i in range(128)])  11.1 us
    all_to_all x1, starting transfers between devices, body(): lax.all_to_all(packed.reshape(128, 1, CHUNK * 128), ('dp', 'tensor'), spl...  9.68 us
    unnamed x28, local copies, waits for them, and re-layouts  8.87 us
    pallas_call x1, Pallas kernels, body(): pl.pallas_call(forward_kernel, grid_spec=pltpu.PrefetchScalarGridSpec(num...  8.47 us
    pallas_call x1, Pallas kernels, body(): pl.pallas_call(pack_kernel, grid=(1,), in_specs=[whole((top, depth)), who...  8.02 us
  transfers between devices with their start and end apart: 15, of which 8 were waited for; matrix products, arithmetic and copies ran while one was open for 2% of the time, Pallas kernels for 19%

profile of v2, /device:TPU:1, one launch (start us, length us, event | category | flops | bytes accessed | tf_op | source)
XLA Modules:
  0.0 143.5 jit_solution(15919887937883666884)
XLA Ops:
  0.7 8.5 %forward.1 = (f32[1024,640]{1,0:T(8,128)}, f32[2,1024]{1,0:T(2,128)}, bf16[256,1280]{1,0:T(8,128)(2,1)}) custom-call(s32[1]{0:T(128)} %bitcast.at_ref, bf16[1024,1280]{1,0:T(8,128)(2,1)} %memory_ref.3, bf16[1024,640]{1,0:T(8,128)(2,1)} %hidden_ref.3, bf16[1024,640]{1,0:T(8,128)(2,1)} %grad_ref.3, bf16[1280,640]{1,0:T(8,128)(2,1)} %wk_ref.5, ...), custom_call_target="tpu_custom_call" | custom-call | flops 3355443200 | bytes 12582912 | tf_op jit(solution)/shard_map/forward/pallas_call | solution.py:264
  9.1 3.6 %collective-permute-start.2 = (f32[2,1024]{1,0:T(2,128)}, f32[2,1024]{1,0:T(2,128)S(1)}, u32[]{:S(2)}, u32[]{:S(2)}) collective-permute-start(f32[2,1024]{1,0:T(2,128)} %get-tuple-element.39.p0), channel_id=1, source_target_pairs={{0,3},{1,0},{2,1},{3,2},{4,7},{5,4},{6,5},{7,6},{8,11},{9,8},{10,9... | collective-permute-start | bytes 24584 | tf_op jit(solution)/shard_map/ppermute | solution.py:292
  12.8 0.3 collective-permute-start.1
  13.1 0.7 collective-permute-start
  13.8 0.0 collective-permute-done.2.p3
  13.8 3.2 %collective-permute-done.1.p2 = f32[2,1024]{1,0:T(2,128)S(1)} collective-permute-done((f32[2,1024]{1,0:T(2,128)}, f32[2,1024]{1,0:T(2,128)S(1)}, u32[]{:S(2)}, u32[]{:S(2)}) %collective-permute-start.1) | collective-permute-done | bytes 8224 | tf_op jit(solution)/shard_map/ppermute | solution.py:292
  17.0 0.1 collective-permute-done.p1
  17.1 1.1 copy-done.6
  18.2 0.7 copy-done.7
  18.9 2.7 %first.1 = (f32[136,1280]{1,0:T(8,128)}, f32[120,1280]{1,0:T(8,128)S(1)}, f32[2,1024]{1,0:T(2,128)S(1)}) custom-call(s32[1]{0:T(128)} %bitcast.at_ref, f32[2,1024]{1,0:T(2,128)S(1)} %copy-done.7, f32[2,1024]{1,0:T(2,128)S(1)} %collective-permute-done.p1, f32[2,1024]{1,0:T(2,128)S(1)} %collective-permute-done.1.p2, f32[2,1024]{1,0:T(2,128)S(1)} %collective-permute-done.2.p3, ...), custom_call_target="tpu_custom_call" | custom-call | flops 838860800 | bytes 6291456 | tf_op jit(solution)/shard_map/first/pallas_call | solution.py:316
  21.6 0.8 copy-done.8
  22.5 0.6 collective-permute-start.3
  23.0 0.1 pad_add_fusion.1.at_ref
  23.1 1.3 copy-done.4
  24.4 1.3 copy-done.5
  25.8 0.8 gate.1.both_ref
  26.5 0.1 pad_add_fusion.at_ref
  26.6 0.9 copy-done.2
  27.5 5.3 %weight_grad.1 = (f32[640,1280]{1,0:T(8,128)S(1)}, f32[640,1280]{1,0:T(8,128)S(1)}) custom-call(s32[3]{0:T(128)S(1)} %pad_add_fusion.1.at_ref, bf16[1024,1280]{1,0:T(8,128)(2,1)S(1)} %copy-done.2, bf16[1024,1280]{1,0:T(8,128)(2,1)S(1)} %gate.1.both_ref), custom_call_target="tpu_custom_call" | custom-call | flops 1 | bytes 1 | tf_op jit(solution)/shard_map/weight_grad/pallas_call | solution.py:350
  32.8 1.9 %collective-permute-start.8 = (f32[640,1280]{1,0:T(8,128)S(1)}, f32[640,1280]{1,0:T(8,128)S(1)}, u32[]{:S(2)}, u32[]{:S(2)}) collective-permute-start(f32[640,1280]{1,0:T(8,128)S(1)} %get-tuple-element.43), channel_id=1, source_target_pairs={{0,4},{1,5},{2,6},{3,7},{4,0},{5,1},{6,2},{7,3},{8,12},{9,13},{10,... | collective-permute-start | bytes 9830408 | tf_op jit(solution)/shard_map/ppermute | solution.py:301
  34.6 3.0 %collective-permute-start.6 = (f32[120,1280]{1,0:T(8,128)S(1)}, f32[120,1280]{1,0:T(8,128)S(1)}, u32[]{:S(2)}, u32[]{:S(2)}) collective-permute-start(f32[120,1280]{1,0:T(8,128)S(1)} %copy-done.9), channel_id=1, source_target_pairs={{0,1},{1,2},{2,3},{3,0},{4,7},{5,4},{6,5},{7,6},{8,9},{9,10},{10,1... | collective-permute-start | bytes 1843208 | tf_op jit(solution)/shard_map/ppermute | solution.py:307
  37.6 6.2 %rest.1 = (f32[3,136,1280]{2,1,0:T(8,128)S(1)}, f32[3,120,1280]{2,1,0:T(8,128)S(1)}) custom-call(s32[2]{0:T(128)S(1)} %pad_add_fusion.at_ref, bf16[1024,1280]{1,0:T(8,128)(2,1)S(1)} %gate.1.both_ref, bf16[1280,640]{1,0:T(8,128)(2,1)S(1)} %copy-done, bf16[1280,640]{1,0:T(8,128)(2,1)S(1)} %copy-done.1), custom_call_target="tpu_custom_call" | custom-call | flops 1 | bytes 1 | tf_op jit(solution)/shard_map/rest/pallas_call | solution.py:367
  43.8 0.0 copy-start.12
  43.8 0.0 copy-start.13
  43.8 0.0 collective-permute-done.3
  43.8 1.2 bitcast_add_fusion.2
  45.0 0.1 collective-permute-start.4
  45.1 2.4 %ranks.1 = (bf16[1024,2048]{1,0:T(8,128)(2,1)S(1)}, f32[2048,128]{1,0:T(8,128)S(1)}, f32[128,128]{1,0:T(8,128)S(1)}) custom-call(s32[2]{0:T(128)S(1)} %pad_add_fusion.at_ref, s32[8,1024]{1,0:T(8,128)S(1)} %bitcast.28, s32[8,1024]{1,0:T(8,128)S(1)} %bitcast.29), custom_call_target="tpu_custom_call" | custom-call | flops 68719476736 | bytes 134217728 | tf_op jit(solution)/shard_map/ranks/pallas_call | solution.py:399
  47.5 0.0 collective-permute-done.8
  47.5 0.4 add.49
  47.9 0.1 slice.60
  48.0 1.7 %collective-permute-start.10 = (f32[320,1280]{1,0:T(8,128)S(1)}, f32[320,1280]{1,0:T(8,128)S(1)}, u32[]{:S(2)}, u32[]{:S(2)}) collective-permute-start(f32[320,1280]{1,0:T(8,128)S(1)} %slice.60), channel_id=1, source_target_pairs={{0,32},{1,33},{2,34},{3,35},{4,12},{5,13},{6,14},{7,15},{8,40},{9,... | collective-permute-start | bytes 4915208 | tf_op jit(solution)/shard_map/ppermute | solution.py:301
  49.8 0.0 collective-permute-done.6
  49.8 0.1 bitcast_add_fusion.5
  49.9 0.5 collective-permute-start.7
  50.4 4.9 %collective-permute-done.4 = f32[136,1280]{1,0:T(8,128)S(1)} collective-permute-done((f32[136,1280]{1,0:T(8,128)S(1)}, f32[136,1280]{1,0:T(8,128)S(1)}, u32[]{:S(2)}, u32[]{:S(2)}) %collective-permute-start.4) | collective-permute-done | bytes 696352 | tf_op jit(solution)/shard_map/ppermute | solution.py:307
  55.2 0.1 bitcast_add_fusion.1
  55.3 1.0 collective-permute-start.5
  56.3 5.5 %collective-permute-done.7 = f32[120,1280]{1,0:T(8,128)S(1)} collective-permute-done((f32[120,1280]{1,0:T(8,128)S(1)}, f32[120,1280]{1,0:T(8,128)S(1)}, u32[]{:S(2)}, u32[]{:S(2)}) %collective-permute-start.7) | collective-permute-done | bytes 614432 | tf_op jit(solution)/shard_map/ppermute | solution.py:307
  61.8 0.1 bitcast_add_fusion.4
  61.9 1.2 collective-permute-start.9
  63.1 5.5 %collective-permute-done.10 = f32[320,1280]{1,0:T(8,128)S(1)} collective-permute-done((f32[320,1280]{1,0:T(8,128)S(1)}, f32[320,1280]{1,0:T(8,128)S(1)}, u32[]{:S(2)}, u32[]{:S(2)}) %collective-permute-start.10) | collective-permute-done | bytes 1638432 | tf_op jit(solution)/shard_map/ppermute | solution.py:301
  68.6 0.3 slice_add_fusion
  68.9 0.1 slice.63
  68.9 3.7 %collective-permute-start.11 = (f32[160,1280]{1,0:T(8,128)S(1)}, f32[160,1280]{1,0:T(8,128)S(1)}, u32[]{:S(2)}, u32[]{:S(2)}) collective-permute-start(f32[160,1280]{1,0:T(8,128)S(1)} %slice.63), channel_id=1, source_target_pairs={{0,96},{1,97},{2,98},{3,99},{4,28},{5,29},{6,30},{7,31},{8,104},{9... | collective-permute-start | bytes 2457608 | tf_op jit(solution)/shard_map/ppermute | solution.py:301
  72.6 0.0 collective-permute-done.5
  72.6 0.1 bitcast_add_fusion.top_ref
  72.7 3.2 %collective-permute-done.9 = f32[120,1280]{1,0:T(8,128)S(1)} collective-permute-done((f32[120,1280]{1,0:T(8,128)S(1)}, f32[120,1280]{1,0:T(8,128)S(1)}, u32[]{:S(2)}, u32[]{:S(2)}) %collective-permute-start.9) | collective-permute-done | bytes 614432 | tf_op jit(solution)/shard_map/ppermute | solution.py:307
  75.9 0.1 bitcast_add_fusion.3.low_ref
  75.9 6.4 %collective-permute-done.11 = f32[160,1280]{1,0:T(8,128)S(1)} collective-permute-done((f32[160,1280]{1,0:T(8,128)S(1)}, f32[160,1280]{1,0:T(8,128)S(1)}, u32[]{:S(2)}, u32[]{:S(2)}) %collective-permute-start.11) | collective-permute-done | bytes 819232 | tf_op jit(solution)/shard_map/ppermute | solution.py:301
  82.3 0.1 slice_add_fusion.1
  82.5 1.3 collective-permute-start.12
  83.8 8.0 %pack.1 = f32[5248,128]{1,0:T(8,128)} custom-call(f32[136,1280]{1,0:T(8,128)S(1)} %bitcast_add_fusion.top_ref, f32[120,1280]{1,0:T(8,128)S(1)} %bitcast_add_fusion.3.low_ref, bf16[1024,2048]{1,0:T(8,128)(2,1)S(1)} %get-tuple-element.59.select_ref, f32[2048,128]{1,0:T(8,128)S(1)} %get-tuple-element.60.group_ref, f32[128,128]{1,0:T(8,128)S(1)} %get-tuple-element.61.sent_ref), custom_call_target="tpu_custom_call" | custom-call | flops 5368709120 | bytes 12582912 | tf_op jit(solution)/shard_map/pack/pallas_call | solution.py:433
  91.8 0.0 collective-permute-done.12
  91.8 0.1 slice_add_fusion.2
  91.8 9.7 %all-to-all-start = ((f32[128,1,5248]{2,1,0:T(1,128)}), f32[128,1,5248]{2,1,0:T(1,128)S(1)}, u32[]{:S(2)}, u32[]{:S(2)}) async-start(f32[128,1,5248]{2,1,0:T(1,128)} %bitcast.13), calls=%async_computation | async-start | bytes 5373952 | tf_op jit(solution)/shard_map/all_to_all | solution.py:461
  101.5 0.7 fusion
  102.2 2.6 %collective-permute-start.13 = (f32[40,1280]{1,0:T(8,128)}, f32[40,1280]{1,0:T(8,128)S(1)}, u32[]{:S(2)}, u32[]{:S(2)}) collective-permute-start(f32[40,1280]{1,0:T(8,128)} %get-tuple-element.76), channel_id=1, source_target_pairs={{0,24},{1,25},{2,26},{3,27},{4,100},{5,101},{6,102},{7,103},{8,16}... | collective-permute-start | bytes 614408 | tf_op jit(solution)/shard_map/ppermute | solution.py:301
  104.8 1.7 %copy-done.3 = f32[1024,640]{1,0:T(8,128)S(1)} copy-done((f32[1024,640]{1,0:T(8,128)S(1)}, f32[1024,640]{1,0:T(8,128)}, u32[]{:S(2)}) %copy-start.3) | copy-done | bytes 2621464
  106.6 1.8 %hidden_grad.1 = bf16[1024,640]{1,0:T(8,128)(2,1)} custom-call(f32[2,1024]{1,0:T(2,128)S(1)} %get-tuple-element.64.total_ref, f32[1024,640]{1,0:T(8,128)S(1)} %copy-done.3), custom_call_target="tpu_custom_call" | custom-call | flops 1310720 | bytes 4194304 | tf_op jit(solution)/shard_map/hidden_grad/pallas_call | solution.py:451
  108.4 30.4 %all-to-all-done = f32[128,1,5248]{2,1,0:T(1,128)S(1)} async-done(((f32[128,1,5248]{2,1,0:T(1,128)}), f32[128,1,5248]{2,1,0:T(1,128)S(1)}, u32[]{:S(2)}, u32[]{:S(2)}) %all-to-all-start) | async-done | bytes 2687008 | tf_op jit(solution)/shard_map/all_to_all | solution.py:461
  138.9 1.0 copy-done.11
  139.8 3.0 %update.1 = (f32[160,512]{1,0:T(8,128)}, f32[160,512]{1,0:T(8,128)}) custom-call(f32[5248,128]{1,0:T(8,128)S(1)} %bitcast.25, f32[160,512]{1,0:T(8,128)S(1)} %bitcast.26, f32[160,512]{1,0:T(8,128)S(1)} %bitcast.27), custom_call_target="tpu_custom_call" | custom-call | flops 1342177280 | bytes 5242880 | tf_op jit(solution)/shard_map/update/pallas_call | solution.py:471
  142.8 0.7 slice_add_fusion.3
  (20 shorter events, 0.1 us)
Async XLA Ops:
  0.6 16.4 %copy-start = (bf16[1280,640]{1,0:T(8,128)(2,1)S(1)}, bf16[1280,640]{1,0:T(8,128)(2,1)}, u32[]{:S(2)}) copy-start(bf16[1280,640]{1,0:T(8,128)(2,1)} %wk_ref.5) | copy-start | bytes 4915204
  0.7 16.4 %copy-start.1 = (bf16[1280,640]{1,0:T(8,128)(2,1)S(1)}, bf16[1280,640]{1,0:T(8,128)(2,1)}, u32[]{:S(2)}) copy-start(bf16[1280,640]{1,0:T(8,128)(2,1)} %wv_ref.5) | copy-start | bytes 4915204
  9.1 4.7 %collective-permute-start.2 = (f32[2,1024]{1,0:T(2,128)}, f32[2,1024]{1,0:T(2,128)S(1)}, u32[]{:S(2)}, u32[]{:S(2)}) collective-permute-start(f32[2,1024]{1,0:T(2,128)} %get-tuple-element.39.p0), channel_id=1, source_target_pairs={{0,3},{1,0},{2,1},{3,2},{4,7},{5,4},{6,5},{7,6},{8,11},{9,8},{10,9... | collective-permute-start | bytes 24584 | tf_op jit(solution)/shard_map/ppermute | solution.py:292
  12.8 4.2 %collective-permute-start.1 = (f32[2,1024]{1,0:T(2,128)}, f32[2,1024]{1,0:T(2,128)S(1)}, u32[]{:S(2)}, u32[]{:S(2)}) collective-permute-start(f32[2,1024]{1,0:T(2,128)} %get-tuple-element.39.p0), channel_id=1, source_target_pairs={{0,2},{1,3},{2,0},{3,1},{4,6},{5,7},{6,4},{7,5},{8,10},{9,11},{10,... | collective-permute-start | bytes 24584 | tf_op jit(solution)/shard_map/ppermute | solution.py:292
  13.1 4.0 %collective-permute-start = (f32[2,1024]{1,0:T(2,128)}, f32[2,1024]{1,0:T(2,128)S(1)}, u32[]{:S(2)}, u32[]{:S(2)}) collective-permute-start(f32[2,1024]{1,0:T(2,128)} %get-tuple-element.39.p0), channel_id=1, source_target_pairs={{0,1},{1,2},{2,3},{3,0},{4,5},{5,6},{6,7},{7,4},{8,9},{9,10},{10,1... | collective-permute-start | bytes 24584 | tf_op jit(solution)/shard_map/ppermute | solution.py:292
  17.1 1.1 copy-start.6
  18.2 0.7 copy-start.7
  21.6 0.8 copy-start.8
  22.5 21.3 %collective-permute-start.3 = (f32[136,1280]{1,0:T(8,128)}, f32[136,1280]{1,0:T(8,128)}, u32[]{:S(2)}, u32[]{:S(2)}) collective-permute-start(f32[136,1280]{1,0:T(8,128)} %get-tuple-element.41), channel_id=1, source_target_pairs={{0,1},{1,2},{2,3},{3,0},{4,7},{5,4},{6,5},{7,6},{8,9},{9,10},{10,1... | collective-permute-start | bytes 2088968 | tf_op jit(solution)/shard_map/ppermute | solution.py:307
  23.1 1.3 copy-start.4
  24.4 1.3 copy-start.5
  25.7 1.7 %copy-start.2 = (bf16[1024,1280]{1,0:T(8,128)(2,1)S(1)}, bf16[1024,1280]{1,0:T(8,128)(2,1)}, u32[]{:S(2)}) copy-start(bf16[1024,1280]{1,0:T(8,128)(2,1)} %memory_ref.3) | copy-start | bytes 7864324
  27.5 7.1 %copy-start.9 = (f32[120,1280]{1,0:T(8,128)S(1)}, f32[120,1280]{1,0:T(8,128)}, u32[]{:S(2)}) copy-start(f32[120,1280]{1,0:T(8,128)} %copy-done.8) | copy-start | bytes 1843204
  32.8 14.7 %collective-permute-start.8 = (f32[640,1280]{1,0:T(8,128)S(1)}, f32[640,1280]{1,0:T(8,128)S(1)}, u32[]{:S(2)}, u32[]{:S(2)}) collective-permute-start(f32[640,1280]{1,0:T(8,128)S(1)} %get-tuple-element.43), channel_id=1, source_target_pairs={{0,4},{1,5},{2,6},{3,7},{4,0},{5,1},{6,2},{7,3},{8,12},{9,13},{10,... | collective-permute-start | bytes 9830408 | tf_op jit(solution)/shard_map/ppermute | solution.py:301
  34.6 15.1 %collective-permute-start.6 = (f32[120,1280]{1,0:T(8,128)S(1)}, f32[120,1280]{1,0:T(8,128)S(1)}, u32[]{:S(2)}, u32[]{:S(2)}) collective-permute-start(f32[120,1280]{1,0:T(8,128)S(1)} %copy-done.9), channel_id=1, source_target_pairs={{0,1},{1,2},{2,3},{3,0},{4,7},{5,4},{6,5},{7,6},{8,9},{9,10},{10,1... | collective-permute-start | bytes 1843208 | tf_op jit(solution)/shard_map/ppermute | solution.py:307
  43.8 1.3 copy-start.12
  43.8 1.3 copy-start.13
  45.0 10.2 %collective-permute-start.4 = (f32[136,1280]{1,0:T(8,128)S(1)}, f32[136,1280]{1,0:T(8,128)S(1)}, u32[]{:S(2)}, u32[]{:S(2)}) collective-permute-start(f32[136,1280]{1,0:T(8,128)S(1)} %bitcast_add_fusion.2), channel_id=1, source_target_pairs={{0,1},{1,2},{2,3},{3,0},{4,7},{5,4},{6,5},{7,6},{8,9},{9,10},{10,1... | collective-permute-start | bytes 2088968 | tf_op jit(solution)/shard_map/ppermute | solution.py:307
  48.0 20.5 %collective-permute-start.10 = (f32[320,1280]{1,0:T(8,128)S(1)}, f32[320,1280]{1,0:T(8,128)S(1)}, u32[]{:S(2)}, u32[]{:S(2)}) collective-permute-start(f32[320,1280]{1,0:T(8,128)S(1)} %slice.60), channel_id=1, source_target_pairs={{0,32},{1,33},{2,34},{3,35},{4,12},{5,13},{6,14},{7,15},{8,40},{9,... | collective-permute-start | bytes 4915208 | tf_op jit(solution)/shard_map/ppermute | solution.py:301
  49.9 12.0 %collective-permute-start.7 = (f32[120,1280]{1,0:T(8,128)S(1)}, f32[120,1280]{1,0:T(8,128)S(1)}, u32[]{:S(2)}, u32[]{:S(2)}) collective-permute-start(f32[120,1280]{1,0:T(8,128)S(1)} %bitcast_add_fusion.5), channel_id=1, source_target_pairs={{0,1},{1,2},{2,3},{3,0},{4,7},{5,4},{6,5},{7,6},{8,9},{9,10},{10,1... | collective-permute-start | bytes 1843208 | tf_op jit(solution)/shard_map/ppermute | solution.py:307
  55.3 17.3 %collective-permute-start.5 = (f32[136,1280]{1,0:T(8,128)S(1)}, f32[136,1280]{1,0:T(8,128)S(1)}, u32[]{:S(2)}, u32[]{:S(2)}) collective-permute-start(f32[136,1280]{1,0:T(8,128)S(1)} %bitcast_add_fusion.1), channel_id=1, source_target_pairs={{0,1},{1,2},{2,3},{3,0},{4,7},{5,4},{6,5},{7,6},{8,9},{9,10},{10,1... | collective-permute-start | bytes 2088968 | tf_op jit(solution)/shard_map/ppermute | solution.py:307
  61.9 14.0 %collective-permute-start.9 = (f32[120,1280]{1,0:T(8,128)S(1)}, f32[120,1280]{1,0:T(8,128)S(1)}, u32[]{:S(2)}, u32[]{:S(2)}) collective-permute-start(f32[120,1280]{1,0:T(8,128)S(1)} %bitcast_add_fusion.4), channel_id=1, source_target_pairs={{0,1},{1,2},{2,3},{3,0},{4,7},{5,4},{6,5},{7,6},{8,9},{9,10},{10,1... | collective-permute-start | bytes 1843208 | tf_op jit(solution)/shard_map/ppermute | solution.py:307
  68.9 13.4 %collective-permute-start.11 = (f32[160,1280]{1,0:T(8,128)S(1)}, f32[160,1280]{1,0:T(8,128)S(1)}, u32[]{:S(2)}, u32[]{:S(2)}) collective-permute-start(f32[160,1280]{1,0:T(8,128)S(1)} %slice.63), channel_id=1, source_target_pairs={{0,96},{1,97},{2,98},{3,99},{4,28},{5,29},{6,30},{7,31},{8,104},{9... | collective-permute-start | bytes 2457608 | tf_op jit(solution)/shard_map/ppermute | solution.py:301
  82.5 9.3 %collective-permute-start.12 = (f32[80,1280]{1,0:T(8,128)S(1)}, f32[80,1280]{1,0:T(8,128)S(1)}, u32[]{:S(2)}, u32[]{:S(2)}) collective-permute-start(f32[80,1280]{1,0:T(8,128)S(1)} %slice.65), channel_id=1, source_target_pairs={{0,8},{1,9},{2,10},{3,11},{4,36},{5,37},{6,38},{7,39},{8,0},{9,1},... | collective-permute-start | bytes 1228808 | tf_op jit(solution)/shard_map/ppermute | solution.py:301
  91.8 47.0 %all-to-all-start = ((f32[128,1,5248]{2,1,0:T(1,128)}), f32[128,1,5248]{2,1,0:T(1,128)S(1)}, u32[]{:S(2)}, u32[]{:S(2)}) async-start(f32[128,1,5248]{2,1,0:T(1,128)} %bitcast.13), calls=%async_computation | async-start | bytes 5373952 | tf_op jit(solution)/shard_map/all_to_all | solution.py:461
  102.2 40.6 %collective-permute-start.13 = (f32[40,1280]{1,0:T(8,128)}, f32[40,1280]{1,0:T(8,128)S(1)}, u32[]{:S(2)}, u32[]{:S(2)}) collective-permute-start(f32[40,1280]{1,0:T(8,128)} %get-tuple-element.76), channel_id=1, source_target_pairs={{0,24},{1,25},{2,26},{3,27},{4,100},{5,101},{6,102},{7,103},{8,16}... | collective-permute-start | bytes 614408 | tf_op jit(solution)/shard_map/ppermute | solution.py:301
  104.8 1.7 %copy-start.3 = (f32[1024,640]{1,0:T(8,128)S(1)}, f32[1024,640]{1,0:T(8,128)}, u32[]{:S(2)}) copy-start(f32[1024,640]{1,0:T(8,128)} %get-tuple-element.65.key_ref) | copy-start | bytes 7864324
  106.6 32.3 %copy-start.10 = (f32[512,160]{0,1:T(8,128)S(1)}, f32[512,160]{0,1:T(8,128)}, u32[]{:S(2)}) copy-start(f32[512,160]{0,1:T(8,128)} %param.16) | copy-start | bytes 983044
  138.9 1.0 copy-start.11

commit v3 on v2

--- a/solution.py
+++ b/solution.py
@@ -79,7 +79,7 @@
 
 
 def forward_kernel(
-    at_ref, memory_ref, hidden_ref, grad_ref, wk_ref, wv_ref, key_ref, part_ref, first_ref
+    at_ref, memory_ref, hidden_ref, grad_ref, wk_ref, wv_ref, part_ref, first_ref
 ):
     @pl.when(pl.program_id(0) == at_ref[0])
     def _():
@@ -89,7 +89,6 @@
 
     memory = memory_ref[...]
     proj_key = jnp.dot(memory, wk_ref[...], preferred_element_type=F32)
-    key_ref[...] = proj_key
     part_ref[0:1, :] = row_sums(hidden_ref[...].astype(F32) * proj_key)
     proj_value = jnp.dot(memory, wv_ref[...], preferred_element_type=F32)
     part_ref[1:2, :] = row_sums(grad_ref[...].astype(F32) * proj_value)
@@ -102,50 +101,46 @@
     return as_columns(gate, width), as_columns(score, width)
 
 
-def backward_tile(total, hidden_ref, grad_ref):
-    gates, scores = gate_columns(total, hidden_ref.shape[1])
-    key_grad = (scores * hidden_ref[...].astype(F32)).astype(BF16)
-    value_grad = (gates * grad_ref[...].astype(F32)).astype(BF16)
-    return key_grad, value_grad, scores
-
-
-def memory_grad_tile(key_grad, value_grad, wk_ref, wv_ref, top_ref, low_ref):
-    top = top_ref.shape[0]
+def summed_parts(part_refs, at=slice(None)):
+    p0, p1, p2, p3 = (ref[:, at] for ref in part_refs)
+    return (p0 + p1) + (p2 + p3)
+
+
+def memory_grad_tile(key_grad, value_grad, wk_ref, wv_ref, *out_refs):
     for h in range(HEADS):
         rows = slice(h * EH, (h + 1) * EH)
         head = lax.dot_general(
             key_grad, wk_ref[rows, :], OVER_LANES, preferred_element_type=F32
         ) + lax.dot_general(value_grad, wv_ref[rows, :], OVER_LANES, preferred_element_type=F32)
-        main = slice(h * MAIN, (h + 1) * MAIN)
         tail = slice(HEADS * MAIN + h * TAIL, HEADS * MAIN + (h + 1) * TAIL)
-        top_ref[:, main] = head[:top, :MAIN]
-        top_ref[:, tail] = head[:top, MAIN:]
-        low_ref[:, main] = head[top:, :MAIN]
-        low_ref[:, tail] = head[top:, MAIN:]
-
-
-def first_kernel(
-    at_ref, p0, p1, p2, p3, first_ref, wk_ref, wv_ref, top_ref, low_ref, total_ref
-):
-    total_ref[...] = (p0[...] + p1[...]) + (p2[...] + p3[...])
+        at = 0
+        for out_ref in out_refs:
+            here = slice(at, at + out_ref.shape[0])
+            out_ref[:, h * MAIN : (h + 1) * MAIN] = head[here, :MAIN]
+            out_ref[:, tail] = head[here, MAIN:]
+            at += out_ref.shape[0]
+
+
+def first_kernel(at_ref, p0, p1, p2, p3, first_ref, wk_ref, wv_ref, top_ref, low_ref):
     count, width = first_ref.shape[0], first_ref.shape[1] // 2
-    total = total_ref[:, pl.ds(pl.multiple_of(at_ref[0] * count, count), count)]
-    key_grad, value_grad, _ = backward_tile(
-        total, first_ref.at[:, :width], first_ref.at[:, width:]
-    )
+    tile = pl.ds(pl.multiple_of(at_ref[0] * count, count), count)
+    gates, scores = gate_columns(summed_parts((p0, p1, p2, p3), tile), width)
+    key_grad = (scores * first_ref[:, :width].astype(F32)).astype(BF16)
+    value_grad = (gates * first_ref[:, width:].astype(F32)).astype(BF16)
     memory_grad_tile(key_grad, value_grad, wk_ref, wv_ref, top_ref, low_ref)
 
 
-def gate_kernel(total_ref, hidden_ref, grad_ref, both_ref):
+def gate_kernel(p0, p1, p2, p3, hidden_ref, grad_ref, both_ref):
     width = hidden_ref.shape[1]
-    key_grad, value_grad, _ = backward_tile(total_ref[...], hidden_ref, grad_ref)
-    both_ref[:, :width] = key_grad
-    both_ref[:, width:] = value_grad
-
-
-def hidden_grad_kernel(total_ref, key_ref, out_ref):
-    _, scores = gate_columns(total_ref[...], key_ref.shape[1])
-    out_ref[...] = (scores * key_ref[...]).astype(BF16)
+    gates, scores = gate_columns(summed_parts((p0, p1, p2, p3)), width)
+    both_ref[:, :width] = (scores * hidden_ref[...].astype(F32)).astype(BF16)
+    both_ref[:, width:] = (gates * grad_ref[...].astype(F32)).astype(BF16)
+
+
+def hidden_grad_kernel(p0, p1, p2, p3, memory_ref, wk_ref, out_ref):
+    _, scores = gate_columns(summed_parts((p0, p1, p2, p3)), out_ref.shape[1])
+    proj_key = jnp.dot(memory_ref[...], wk_ref[...], preferred_element_type=F32)
+    out_ref[...] = (scores * proj_key).astype(BF16)
 
 
 def rest_kernel(at_ref, both_ref, wk_ref, wv_ref, top_ref, low_ref):
@@ -261,7 +256,7 @@
         return pl.BlockSpec((tile, cols), lambda i, s: (i, 0))
 
     chunk = whole((quarter, 2 * width))
-    proj_key, part, first_both = pl.pallas_call(
+    part, first_both = pl.pallas_call(
         forward_kernel,
         grid_spec=pltpu.PrefetchScalarGridSpec(
             num_scalar_prefetch=1,
@@ -274,17 +269,15 @@
                 whole((depth, width)),
             ],
             out_specs=[
-                by_rows(width),
                 pl.BlockSpec((2, tile), lambda i, s: (0, i)),
                 chunk,
             ],
         ),
         out_shape=[
-            jax.ShapeDtypeStruct((tokens, width), F32),
             jax.ShapeDtypeStruct((2, tokens), F32),
             jax.ShapeDtypeStruct((quarter, 2 * width), BF16),
         ],
-        compiler_params=params(58),
+        compiler_params=params(53),
         cost_estimate=cost(4 * tokens * depth * width, 12 << 20),
         name="forward",
     )(start, memory, hidden, out_grad, w_key, w_value)
@@ -311,25 +304,26 @@
 
     weights = [whole((depth, width))] * 2
     part_whole = whole((2, tokens))
-    top = 136
+    top = 144
     low = quarter - top
-    first_top, first_low, total = pl.pallas_call(
+
+    first_top, first_low = pl.pallas_call(
         first_kernel,
         grid_spec=pltpu.PrefetchScalarGridSpec(
             num_scalar_prefetch=1,
             grid=(1,),
             in_specs=[part_whole] * 4 + [chunk] + weights,
-            out_specs=[whole((top, depth)), whole((low, depth)), part_whole],
+            out_specs=[whole((top, depth)), whole((low, depth))],
         ),
         out_shape=[
             jax.ShapeDtypeStruct((top, depth), F32),
             jax.ShapeDtypeStruct((low, depth), F32),
-            jax.ShapeDtypeStruct((2, tokens), F32),
         ],
         compiler_params=params(20),
         cost_estimate=cost(4 * quarter * depth * width, 6 << 20),
         name="first",
     )(start, *parts, first_both, w_key, w_value)
+    parts, _ = lax.optimization_barrier((parts, first_low))
 
     def by_rows(cols):
         return pl.BlockSpec((quarter, cols), lambda i: (i, 0))
@@ -338,13 +332,13 @@
     both = pl.pallas_call(
         gate_kernel,
         grid=(4,),
-        in_specs=[total_spec] + [by_rows(width)] * 2,
+        in_specs=[total_spec] * 4 + [by_rows(width)] * 2,
         out_specs=by_rows(2 * width),
         out_shape=jax.ShapeDtypeStruct((tokens, 2 * width), BF16),
         compiler_params=params(24),
         cost_estimate=cost(1, 1),
         name="gate",
-    )(total, hidden, out_grad)
+    )(*parts, hidden, out_grad)
 
     grad_spec = whole((depth // 2, 2 * width))
     mine, other = pl.pallas_call(
@@ -393,7 +387,9 @@
 
     moved_top = turned(first_top) + rest_top[0]
     moved_low = turned(first_low) + rest_low[0]
-    moved_top, owners, slots = lax.optimization_barrier((moved_top, row_owner.T, row_slot.T))
+    moved_top, moved_low, owners, slots = lax.optimization_barrier(
+        (moved_top, moved_low, row_owner.T, row_slot.T)
+    )
     passed_top = turned(moved_top)
     passed_low = turned(moved_low)
     select, group, sent = pl.pallas_call(
@@ -419,16 +415,17 @@
     )(at, owners, slots)
     mine, select = lax.optimization_barrier((mine, select))
     pair = mine + swapped(other, ((1, 0), (1, 0)))
-    rest_low, pair = lax.optimization_barrier((rest_low, pair))
-    moved_top = turned(passed_top + rest_top[1])
-    moved_low = turned(passed_low + rest_low[1])
+    rest_top, rest_low, pair = lax.optimization_barrier((rest_top, rest_low, pair))
+    moved_top, moved_low = lax.optimization_barrier(
+        (passed_top + rest_top[1], passed_low + rest_low[1])
+    )
+    moved_top = turned(moved_top)
+    moved_low = turned(moved_low)
     grads = folded(pair, ((8, 0), (2, 0)))
     rest_low, grads = lax.optimization_barrier((rest_low, grads))
     sum_top = moved_top + rest_top[2]
     sum_low = moved_low + rest_low[2]
     grads = folded(grads, ((24, 0), (6, 0)))
-    sum_low, grads = lax.optimization_barrier((sum_low, grads))
-    grads = folded(grads, ((2, 0), (8, 0)))
 
     packed = pl.pallas_call(
         pack_kernel,
@@ -447,17 +444,17 @@
         cost_estimate=cost(2 * 1024 * 2048 * 1280, 12 << 20),
         name="pack",
     )(sum_top, sum_low, select, group, sent)
-    packed, grads, total = lax.optimization_barrier((packed, grads, total))
+    packed, grads, parts = lax.optimization_barrier((packed, grads, parts))
     hidden_grad = pl.pallas_call(
         hidden_grad_kernel,
         grid=(4,),
-        in_specs=[total_spec, by_rows(width)],
+        in_specs=[total_spec] * 4 + [by_rows(depth), whole((depth, width))],
         out_specs=by_rows(width),
         out_shape=jax.ShapeDtypeStruct((tokens, width), BF16),
         compiler_params=params(24),
-        cost_estimate=cost(2 * tokens * width, 4 << 20),
+        cost_estimate=cost(2 * tokens * depth * width, 6 << 20),
         name="hidden_grad",
-    )(total, proj_key)
+    )(*parts, memory, w_key)
     received = lax.all_to_all(
         packed.reshape(128, 1, CHUNK * 128),
         ("dp", "tensor"),
@@ -465,7 +462,8 @@
         concat_axis=0,
         tiled=True,
     ).reshape(128 * CHUNK, 128)
-    received, hidden_grad = lax.optimization_barrier((received, hidden_grad))
+    grads = folded(grads, ((2, 0), (8, 0)))
+    received, hidden_grad, grads = lax.optimization_barrier((received, hidden_grad, grads))
     owned = mem_table.shape[0]
     table_spec = whole((EH, owned))
     new_table, new_sum = pl.pallas_call(

time: 144 us -> 140 us (0.972)
  waiting for transfers between devices: 59.1 us -> 52.8 us
  starting transfers between devices: 31.8 us -> 35 us
  local copies, waits for them, and re-layouts: 9.77 us -> 7.86 us
    all_to_all x1, waiting for transfers between devices: 30.4 us -> 2.59 us  [body(): lax.all_to_all(packed.reshape(128, 1, CHUNK * 128), ('dp', 'tensor'), spl...]
    ppermute x5, waiting for transfers between devices: 11.9 us -> 28.6 us  [swapped(): lax.ppermute(value, ('dp', 'tensor'), [(i, goal(i)) for i in range(128)])]
    ppermute x6, waiting for transfers between devices: 13.5 us -> 18.6 us  [turned(): lax.ppermute(value, ('dp', 'tensor'), [(i, goal(i)) for i in range(128)])]
    all_to_all x1, starting transfers between devices: 9.68 us -> 12 us  [body(): lax.all_to_all(packed.reshape(128, 1, CHUNK * 128), ('dp', 'tensor'), spl...]
    ppermute x6, starting transfers between devices: 6.31 us -> 8.22 us  [turned(): lax.ppermute(value, ('dp', 'tensor'), [(i, goal(i)) for i in range(128)])]
    pallas_call x1, Pallas kernels: 3 us -> 4.72 us  [body(): pl.pallas_call(update_kernel, grid=(1,), in_specs=[whole((128 * CHUNK, 12...]
    pallas_call x2, Pallas kernels: 2.61 us -> 4.32 us  [the longest x1 3.52 us: body(): pl.pallas_call(hidden_grad_kernel, grid=(4,), in_specs=[total_spec] * 4 +...]
    pallas_call x1, Pallas kernels: 8.02 us -> 6.5 us  [body(): pl.pallas_call(pack_kernel, grid=(1,), in_specs=[whole((top, depth)), who...]
  transfers between devices with their start and end apart: 15 -> 15, of which waited for: 8 -> 8; matrix products, arithmetic and copies ran while one was open for 2% -> 2% of each run, Pallas kernels for 19% -> 21%
where the time goes in v3:
time: 140 us
  waiting for transfers between devices  52.8 us (38%)
  Pallas kernels  40 us (29%)
  starting transfers between devices  35 us (25%)
  local copies, waits for them, and re-layouts  7.86 us (6%)
  other arithmetic  3.14 us (2%)
    ppermute x5, waiting for transfers between devices, swapped(): lax.ppermute(value, ('dp', 'tensor'), [(i, goal(i)) for i in range(128)])  28.6 us
    ppermute x6, waiting for transfers between devices, turned(): lax.ppermute(value, ('dp', 'tensor'), [(i, goal(i)) for i in range(128)])  18.6 us
    all_to_all x1, starting transfers between devices, body(): lax.all_to_all(packed.reshape(128, 1, CHUNK * 128), ('dp', 'tensor'), spl...  12 us
    ppermute x5, starting transfers between devices, swapped(): lax.ppermute(value, ('dp', 'tensor'), [(i, goal(i)) for i in range(128)])  10.1 us
    ppermute x6, starting transfers between devices, turned(): lax.ppermute(value, ('dp', 'tensor'), [(i, goal(i)) for i in range(128)])  8.22 us
    pallas_call x1, Pallas kernels, body(): pl.pallas_call(forward_kernel, grid_spec=pltpu.PrefetchScalarGridSpec(num...  7.81 us
    unnamed x24, local copies, waits for them, and re-layouts  7.64 us
    pallas_call x1, Pallas kernels, body(): pl.pallas_call(pack_kernel, grid=(1,), in_specs=[whole((top, depth)), who...  6.5 us
  transfers between devices with their start and end apart: 15, of which 8 were waited for; matrix products, arithmetic and copies ran while one was open for 2% of the time, Pallas kernels for 21%

profile of v3, /device:TPU:1, one launch (start us, length us, event | category | flops | bytes accessed | tf_op | source)
XLA Modules:
  0.0 139.6 jit_solution(17643922102787406688)
XLA Ops:
  0.6 0.0 copy-start
  0.7 0.0 copy-start.1
  0.7 7.8 %forward.1 = (f32[2,1024]{1,0:T(2,128)S(1)}, bf16[256,1280]{1,0:T(8,128)(2,1)S(1)}) custom-call(s32[1]{0:T(128)} %bitcast.at_ref, bf16[1024,1280]{1,0:T(8,128)(2,1)} %memory_ref.5, bf16[1024,640]{1,0:T(8,128)(2,1)} %hidden_ref.3, bf16[1024,640]{1,0:T(8,128)(2,1)} %grad_ref.3, bf16[1280,640]{1,0:T(8,128)(2,1)} %wk_ref.7, bf16[1280,640]{1,0:T(8,128)(2,1)} %wv_ref.5), custom_call_target="tpu_custom_call" | custom-call | flops 3355443200 | bytes 12582912 | tf_op jit(solution)/shard_map/forward/pallas_call | solution.py:259
  8.5 3.6 %collective-permute-start.2 = (f32[2,1024]{1,0:T(2,128)S(1)}, f32[2,1024]{1,0:T(2,128)S(1)}, u32[]{:S(2)}, u32[]{:S(2)}) collective-permute-start(f32[2,1024]{1,0:T(2,128)S(1)} %get-tuple-element.77.p0), channel_id=1, source_target_pairs={{0,3},{1,0},{2,1},{3,2},{4,7},{5,4},{6,5},{7,6},{8,11},{9,8},{10,9... | collective-permute-start | bytes 24584 | tf_op jit(solution)/shard_map/ppermute | solution.py:285
  12.1 0.3 collective-permute-start.1
  12.5 0.7 collective-permute-start
  13.2 0.0 collective-permute-done.2.p3
  13.2 3.0 %collective-permute-done.1.p2 = f32[2,1024]{1,0:T(2,128)S(1)} collective-permute-done((f32[2,1024]{1,0:T(2,128)S(1)}, f32[2,1024]{1,0:T(2,128)S(1)}, u32[]{:S(2)}, u32[]{:S(2)}) %collective-permute-start.1) | collective-permute-done | bytes 8224 | tf_op jit(solution)/shard_map/ppermute | solution.py:285
  16.1 0.1 collective-permute-done.p1
  16.2 0.0 copy-done
  16.2 2.7 %first.1 = (f32[144,1280]{1,0:T(8,128)S(1)}, f32[112,1280]{1,0:T(8,128)}) custom-call(s32[1]{0:T(128)} %bitcast.at_ref, f32[2,1024]{1,0:T(2,128)S(1)} %get-tuple-element.77.p0, f32[2,1024]{1,0:T(2,128)S(1)} %collective-permute-done.p1, f32[2,1024]{1,0:T(2,128)S(1)} %collective-permute-done.1.p2, f32[2,1024]{1,0:T(2,128)S(1)} %collective-permute-done.2.p3, ...), custom_call_target="tpu_custom_call" | custom-call | flops 838860800 | bytes 6291456 | tf_op jit(solution)/shard_map/first/pallas_call | solution.py:310
  19.0 0.9 copy-done.7
  19.8 0.6 collective-permute-start.4
  20.4 1.4 collective-permute-start.3
  21.8 0.1 pad_add_fusion.1.at_ref
  21.9 1.3 copy-done.5
  23.2 1.3 copy-done.6
  24.5 0.8 gate.1.both_ref
  25.3 0.1 pad_add_fusion.at_ref
  25.4 0.8 copy-done.3
  26.2 5.3 %weight_grad.1 = (f32[640,1280]{1,0:T(8,128)S(1)}, f32[640,1280]{1,0:T(8,128)S(1)}) custom-call(s32[3]{0:T(128)S(1)} %pad_add_fusion.1.at_ref, bf16[1024,1280]{1,0:T(8,128)(2,1)S(1)} %copy-done.3, bf16[1024,1280]{1,0:T(8,128)(2,1)S(1)} %gate.1.both_ref), custom_call_target="tpu_custom_call" | custom-call | flops 1 | bytes 1 | tf_op jit(solution)/shard_map/weight_grad/pallas_call | solution.py:344
  31.5 2.1 %collective-permute-start.6 = (f32[640,1280]{1,0:T(8,128)S(1)}, f32[640,1280]{1,0:T(8,128)S(1)}, u32[]{:S(2)}, u32[]{:S(2)}) collective-permute-start(f32[640,1280]{1,0:T(8,128)S(1)} %get-tuple-element.55), channel_id=1, source_target_pairs={{0,4},{1,5},{2,6},{3,7},{4,0},{5,1},{6,2},{7,3},{8,12},{9,13},{10,... | collective-permute-start | bytes 9830408 | tf_op jit(solution)/shard_map/ppermute | solution.py:294
  33.7 6.2 %rest.1 = (f32[3,144,1280]{2,1,0:T(8,128)S(1)}, f32[3,112,1280]{2,1,0:T(8,128)S(1)}) custom-call(s32[2]{0:T(128)S(1)} %pad_add_fusion.at_ref, bf16[1024,1280]{1,0:T(8,128)(2,1)S(1)} %gate.1.both_ref, bf16[1280,640]{1,0:T(8,128)(2,1)S(1)} %copy-done.1, bf16[1280,640]{1,0:T(8,128)(2,1)S(1)} %copy-done), custom_call_target="tpu_custom_call" | custom-call | flops 1 | bytes 1 | tf_op jit(solution)/shard_map/rest/pallas_call | solution.py:361
  39.9 0.0 collective-permute-done.4
  39.9 0.0 copy-start.10
  39.9 0.0 copy-start.11
  39.9 1.1 bitcast_add_fusion.5
  41.0 0.0 collective-permute-done.3
  41.0 0.1 bitcast_add_fusion.2
  41.1 1.4 %collective-permute-start.7 = (f32[112,1280]{1,0:T(8,128)S(1)}, f32[112,1280]{1,0:T(8,128)S(1)}, u32[]{:S(2)}, u32[]{:S(2)}) collective-permute-start(f32[112,1280]{1,0:T(8,128)S(1)} %bitcast_add_fusion.5), channel_id=1, source_target_pairs={{0,1},{1,2},{2,3},{3,0},{4,7},{5,4},{6,5},{7,6},{8,9},{9,10},{10,1... | collective-permute-start | bytes 1720328 | tf_op jit(solution)/shard_map/ppermute | solution.py:300
  42.6 1.7 %collective-permute-start.5 = (f32[144,1280]{1,0:T(8,128)S(1)}, f32[144,1280]{1,0:T(8,128)S(1)}, u32[]{:S(2)}, u32[]{:S(2)}) collective-permute-start(f32[144,1280]{1,0:T(8,128)S(1)} %bitcast_add_fusion.2), channel_id=1, source_target_pairs={{0,1},{1,2},{2,3},{3,0},{4,7},{5,4},{6,5},{7,6},{8,9},{9,10},{10,1... | collective-permute-start | bytes 2211848 | tf_op jit(solution)/shard_map/ppermute | solution.py:300
  44.3 2.4 %ranks.1 = (bf16[1024,2048]{1,0:T(8,128)(2,1)S(1)}, f32[2048,128]{1,0:T(8,128)S(1)}, f32[128,128]{1,0:T(8,128)S(1)}) custom-call(s32[2]{0:T(128)S(1)} %pad_add_fusion.at_ref, s32[8,1024]{1,0:T(8,128)S(1)} %bitcast.28, s32[8,1024]{1,0:T(8,128)S(1)} %bitcast.29), custom_call_target="tpu_custom_call" | custom-call | flops 68719476736 | bytes 134217728 | tf_op jit(solution)/shard_map/ranks/pallas_call | solution.py:395
  46.7 0.0 collective-permute-done.6
  46.7 0.4 add.47
  47.1 0.1 slice.60
  47.2 1.7 %collective-permute-start.10 = (f32[320,1280]{1,0:T(8,128)S(1)}, f32[320,1280]{1,0:T(8,128)S(1)}, u32[]{:S(2)}, u32[]{:S(2)}) collective-permute-start(f32[320,1280]{1,0:T(8,128)S(1)} %slice.60), channel_id=1, source_target_pairs={{0,32},{1,33},{2,34},{3,35},{4,12},{5,13},{6,14},{7,15},{8,40},{9,... | collective-permute-start | bytes 4915208 | tf_op jit(solution)/shard_map/ppermute | solution.py:294
  48.9 9.0 %collective-permute-done.5 = f32[144,1280]{1,0:T(8,128)S(1)} collective-permute-done((f32[144,1280]{1,0:T(8,128)S(1)}, f32[144,1280]{1,0:T(8,128)S(1)}, u32[]{:S(2)}, u32[]{:S(2)}) %collective-permute-start.5) | collective-permute-done | bytes 737312 | tf_op jit(solution)/shard_map/ppermute | solution.py:300
  58.0 0.1 bitcast_add_fusion.1
  58.0 0.0 collective-permute-done.7
  58.0 0.1 bitcast_add_fusion.4
  58.1 2.3 %collective-permute-start.8 = (f32[144,1280]{1,0:T(8,128)S(1)}, f32[144,1280]{1,0:T(8,128)S(1)}, u32[]{:S(2)}, u32[]{:S(2)}) collective-permute-start(f32[144,1280]{1,0:T(8,128)S(1)} %bitcast_add_fusion.1), channel_id=1, source_target_pairs={{0,1},{1,2},{2,3},{3,0},{4,7},{5,4},{6,5},{7,6},{8,9},{9,10},{10,1... | collective-permute-start | bytes 2211848 | tf_op jit(solution)/shard_map/ppermute | solution.py:300
  60.5 0.8 collective-permute-start.9
  61.3 7.6 %collective-permute-done.8 = f32[144,1280]{1,0:T(8,128)S(1)} collective-permute-done((f32[144,1280]{1,0:T(8,128)S(1)}, f32[144,1280]{1,0:T(8,128)S(1)}, u32[]{:S(2)}, u32[]{:S(2)}) %collective-permute-start.8) | collective-permute-done | bytes 737312 | tf_op jit(solution)/shard_map/ppermute | solution.py:300
  68.9 0.1 bitcast_add_fusion.top_ref
  68.9 0.0 collective-permute-done.10
  69.0 0.2 slice_add_fusion
  69.2 0.1 slice.63
  69.2 3.8 %collective-permute-start.11 = (f32[160,1280]{1,0:T(8,128)S(1)}, f32[160,1280]{1,0:T(8,128)S(1)}, u32[]{:S(2)}, u32[]{:S(2)}) collective-permute-start(f32[160,1280]{1,0:T(8,128)S(1)} %slice.63), channel_id=1, source_target_pairs={{0,96},{1,97},{2,98},{3,99},{4,28},{5,29},{6,30},{7,31},{8,104},{9... | collective-permute-start | bytes 2457608 | tf_op jit(solution)/shard_map/ppermute | solution.py:294
  73.1 1.9 %collective-permute-done.9 = f32[112,1280]{1,0:T(8,128)S(1)} collective-permute-done((f32[112,1280]{1,0:T(8,128)S(1)}, f32[112,1280]{1,0:T(8,128)S(1)}, u32[]{:S(2)}, u32[]{:S(2)}) %collective-permute-start.9) | collective-permute-done | bytes 573472 | tf_op jit(solution)/shard_map/ppermute | solution.py:300
  75.0 0.1 bitcast_add_fusion.3.low_ref
  75.1 6.5 %pack.1 = f32[5248,128]{1,0:T(8,128)S(1)} custom-call(f32[144,1280]{1,0:T(8,128)S(1)} %bitcast_add_fusion.top_ref, f32[112,1280]{1,0:T(8,128)S(1)} %bitcast_add_fusion.3.low_ref, bf16[1024,2048]{1,0:T(8,128)(2,1)S(1)} %get-tuple-element.72.select_ref, f32[2048,128]{1,0:T(8,128)S(1)} %get-tuple-element.73.group_ref, f32[128,128]{1,0:T(8,128)S(1)} %get-tuple-element.74.sent_ref), custom_call_target="tpu_custom_call" | custom-call | flops 5368709120 | bytes 12582912 | tf_op jit(solution)/shard_map/pack/pallas_call | solution.py:430
  81.6 1.5 %copy-done.2 = f32[5248,128]{1,0:T(8,128)} copy-done((f32[5248,128]{1,0:T(8,128)}, f32[5248,128]{1,0:T(8,128)S(1)}, u32[]{:S(2)}) %copy-start.2) | copy-done | bytes 2687000
  83.1 0.0 collective-permute-done.11
  83.1 0.1 slice_add_fusion.1
  83.2 12.0 %all-to-all-start = ((f32[128,1,5248]{2,1,0:T(1,128)}), f32[128,1,5248]{2,1,0:T(1,128)}, u32[]{:S(2)}, u32[]{:S(2)}) async-start(f32[128,1,5248]{2,1,0:T(1,128)} %bitcast.25), calls=%async_computation | async-start | bytes 5373952 | tf_op jit(solution)/shard_map/all_to_all | solution.py:458
  95.3 1.5 %collective-permute-start.12 = (f32[80,1280]{1,0:T(8,128)S(1)}, f32[80,1280]{1,0:T(8,128)S(1)}, u32[]{:S(2)}, u32[]{:S(2)}) collective-permute-start(f32[80,1280]{1,0:T(8,128)S(1)} %slice.65), channel_id=1, source_target_pairs={{0,8},{1,9},{2,10},{3,11},{4,36},{5,37},{6,38},{7,39},{8,0},{9,1},... | collective-permute-start | bytes 1228808 | tf_op jit(solution)/shard_map/ppermute | solution.py:294
  96.7 1.7 %copy-done.4 = bf16[1024,1280]{1,0:T(8,128)(2,1)S(1)} copy-done((bf16[1024,1280]{1,0:T(8,128)(2,1)S(1)}, bf16[1024,1280]{1,0:T(8,128)(2,1)}, u32[]{:S(2)}) %copy-start.4) | copy-done | bytes 2621464
  98.5 3.5 %hidden_grad.1 = bf16[1024,640]{1,0:T(8,128)(2,1)} custom-call(f32[2,1024]{1,0:T(2,128)S(1)} %get-tuple-element.77.p0, f32[2,1024]{1,0:T(2,128)S(1)} %collective-permute-done.p1, f32[2,1024]{1,0:T(2,128)S(1)} %collective-permute-done.1.p2, f32[2,1024]{1,0:T(2,128)S(1)} %collective-permute-done.2.p3, bf16[1024,1280]{1,0:T(8,128)(2,1)S(1)} %copy-done.4, ...), custom_call_target="tpu_custom_call" | custom-call | flops 1677721600 | bytes 6291456 | tf_op jit(solution)/shard_map/hidden_grad/pallas_call | solution.py:448
  102.0 28.1 %collective-permute-done.12 = f32[80,1280]{1,0:T(8,128)S(1)} collective-permute-done((f32[80,1280]{1,0:T(8,128)S(1)}, f32[80,1280]{1,0:T(8,128)S(1)}, u32[]{:S(2)}, u32[]{:S(2)}) %collective-permute-start.12) | collective-permute-done | bytes 409632 | tf_op jit(solution)/shard_map/ppermute | solution.py:294
  130.1 2.6 %all-to-all-done = f32[128,1,5248]{2,1,0:T(1,128)} async-done(((f32[128,1,5248]{2,1,0:T(1,128)}), f32[128,1,5248]{2,1,0:T(1,128)}, u32[]{:S(2)}, u32[]{:S(2)}) %all-to-all-start) | async-done | bytes 2687008 | tf_op jit(solution)/shard_map/all_to_all | solution.py:458
  132.7 1.0 collective-permute-start.13
  133.7 4.7 %update.1 = (f32[160,512]{1,0:T(8,128)}, f32[160,512]{1,0:T(8,128)}) custom-call(f32[5248,128]{1,0:T(8,128)} %bitcast.14.got_ref, f32[160,512]{1,0:T(8,128)S(1)} %bitcast.26, f32[160,512]{1,0:T(8,128)S(1)} %bitcast.27), custom_call_target="tpu_custom_call" | custom-call | flops 1342177280 | bytes 5242880 | tf_op jit(solution)/shard_map/update/pallas_call | solution.py:469
  138.4 0.5 collective-permute-done.13
  138.9 0.7 slice_add_fusion.3
  (16 shorter events, 0.1 us)
Async XLA Ops:
  0.6 15.6 %copy-start = (bf16[1280,640]{1,0:T(8,128)(2,1)S(1)}, bf16[1280,640]{1,0:T(8,128)(2,1)}, u32[]{:S(2)}) copy-start(bf16[1280,640]{1,0:T(8,128)(2,1)} %wv_ref.5) | copy-start | bytes 4915204
  0.7 15.6 %copy-start.1 = (bf16[1280,640]{1,0:T(8,128)(2,1)S(1)}, bf16[1280,640]{1,0:T(8,128)(2,1)}, u32[]{:S(2)}) copy-start(bf16[1280,640]{1,0:T(8,128)(2,1)} %wk_ref.7) | copy-start | bytes 4915204
  8.5 4.7 %collective-permute-start.2 = (f32[2,1024]{1,0:T(2,128)S(1)}, f32[2,1024]{1,0:T(2,128)S(1)}, u32[]{:S(2)}, u32[]{:S(2)}) collective-permute-start(f32[2,1024]{1,0:T(2,128)S(1)} %get-tuple-element.77.p0), channel_id=1, source_target_pairs={{0,3},{1,0},{2,1},{3,2},{4,7},{5,4},{6,5},{7,6},{8,11},{9,8},{10,9... | collective-permute-start | bytes 24584 | tf_op jit(solution)/shard_map/ppermute | solution.py:285
  12.1 4.0 %collective-permute-start.1 = (f32[2,1024]{1,0:T(2,128)S(1)}, f32[2,1024]{1,0:T(2,128)S(1)}, u32[]{:S(2)}, u32[]{:S(2)}) collective-permute-start(f32[2,1024]{1,0:T(2,128)S(1)} %get-tuple-element.77.p0), channel_id=1, source_target_pairs={{0,2},{1,3},{2,0},{3,1},{4,6},{5,7},{6,4},{7,5},{8,10},{9,11},{10,... | collective-permute-start | bytes 24584 | tf_op jit(solution)/shard_map/ppermute | solution.py:285
  12.5 3.7 %collective-permute-start = (f32[2,1024]{1,0:T(2,128)S(1)}, f32[2,1024]{1,0:T(2,128)S(1)}, u32[]{:S(2)}, u32[]{:S(2)}) collective-permute-start(f32[2,1024]{1,0:T(2,128)S(1)} %get-tuple-element.77.p0), channel_id=1, source_target_pairs={{0,1},{1,2},{2,3},{3,0},{4,5},{5,6},{6,7},{7,4},{8,9},{9,10},{10,1... | collective-permute-start | bytes 24584 | tf_op jit(solution)/shard_map/ppermute | solution.py:285
  19.0 0.9 copy-start.7
  19.8 20.0 %collective-permute-start.4 = (f32[112,1280]{1,0:T(8,128)}, f32[112,1280]{1,0:T(8,128)}, u32[]{:S(2)}, u32[]{:S(2)}) collective-permute-start(f32[112,1280]{1,0:T(8,128)} %get-tuple-element.50), channel_id=1, source_target_pairs={{0,1},{1,2},{2,3},{3,0},{4,7},{5,4},{6,5},{7,6},{8,9},{9,10},{10,1... | collective-permute-start | bytes 1720328 | tf_op jit(solution)/shard_map/ppermute | solution.py:300
  20.4 20.6 %collective-permute-start.3 = (f32[144,1280]{1,0:T(8,128)}, f32[144,1280]{1,0:T(8,128)S(1)}, u32[]{:S(2)}, u32[]{:S(2)}) collective-permute-start(f32[144,1280]{1,0:T(8,128)} %copy-done.7), channel_id=1, source_target_pairs={{0,1},{1,2},{2,3},{3,0},{4,7},{5,4},{6,5},{7,6},{8,9},{9,10},{10,1... | collective-permute-start | bytes 2211848 | tf_op jit(solution)/shard_map/ppermute | solution.py:300
  21.9 1.3 copy-start.5
  23.2 1.3 copy-start.6
  24.5 1.7 %copy-start.3 = (bf16[1024,1280]{1,0:T(8,128)(2,1)S(1)}, bf16[1024,1280]{1,0:T(8,128)(2,1)}, u32[]{:S(2)}) copy-start(bf16[1024,1280]{1,0:T(8,128)(2,1)} %memory_ref.5) | copy-start | bytes 7864324
  31.5 15.1 %collective-permute-start.6 = (f32[640,1280]{1,0:T(8,128)S(1)}, f32[640,1280]{1,0:T(8,128)S(1)}, u32[]{:S(2)}, u32[]{:S(2)}) collective-permute-start(f32[640,1280]{1,0:T(8,128)S(1)} %get-tuple-element.55), channel_id=1, source_target_pairs={{0,4},{1,5},{2,6},{3,7},{4,0},{5,1},{6,2},{7,3},{8,12},{9,13},{10,... | collective-permute-start | bytes 9830408 | tf_op jit(solution)/shard_map/ppermute | solution.py:294
  39.9 4.4 %copy-start.10 = (s32[1024,8]{0,1:T(8,128)S(1)}, s32[1024,8]{0,1:T(8,128)}, u32[]{:S(2)}) copy-start(s32[1024,8]{0,1:T(8,128)} %param.14) | copy-start | bytes 98308
  39.9 4.4 %copy-start.11 = (s32[1024,8]{0,1:T(8,128)S(1)}, s32[1024,8]{0,1:T(8,128)}, u32[]{:S(2)}) copy-start(s32[1024,8]{0,1:T(8,128)} %param.15) | copy-start | bytes 98308
  41.1 16.9 %collective-permute-start.7 = (f32[112,1280]{1,0:T(8,128)S(1)}, f32[112,1280]{1,0:T(8,128)S(1)}, u32[]{:S(2)}, u32[]{:S(2)}) collective-permute-start(f32[112,1280]{1,0:T(8,128)S(1)} %bitcast_add_fusion.5), channel_id=1, source_target_pairs={{0,1},{1,2},{2,3},{3,0},{4,7},{5,4},{6,5},{7,6},{8,9},{9,10},{10,1... | collective-permute-start | bytes 1720328 | tf_op jit(solution)/shard_map/ppermute | solution.py:300
  42.6 15.4 %collective-permute-start.5 = (f32[144,1280]{1,0:T(8,128)S(1)}, f32[144,1280]{1,0:T(8,128)S(1)}, u32[]{:S(2)}, u32[]{:S(2)}) collective-permute-start(f32[144,1280]{1,0:T(8,128)S(1)} %bitcast_add_fusion.2), channel_id=1, source_target_pairs={{0,1},{1,2},{2,3},{3,0},{4,7},{5,4},{6,5},{7,6},{8,9},{9,10},{10,1... | collective-permute-start | bytes 2211848 | tf_op jit(solution)/shard_map/ppermute | solution.py:300
  47.2 21.7 %collective-permute-start.10 = (f32[320,1280]{1,0:T(8,128)S(1)}, f32[320,1280]{1,0:T(8,128)S(1)}, u32[]{:S(2)}, u32[]{:S(2)}) collective-permute-start(f32[320,1280]{1,0:T(8,128)S(1)} %slice.60), channel_id=1, source_target_pairs={{0,32},{1,33},{2,34},{3,35},{4,12},{5,13},{6,14},{7,15},{8,40},{9,... | collective-permute-start | bytes 4915208 | tf_op jit(solution)/shard_map/ppermute | solution.py:294
  58.1 10.7 %collective-permute-start.8 = (f32[144,1280]{1,0:T(8,128)S(1)}, f32[144,1280]{1,0:T(8,128)S(1)}, u32[]{:S(2)}, u32[]{:S(2)}) collective-permute-start(f32[144,1280]{1,0:T(8,128)S(1)} %bitcast_add_fusion.1), channel_id=1, source_target_pairs={{0,1},{1,2},{2,3},{3,0},{4,7},{5,4},{6,5},{7,6},{8,9},{9,10},{10,1... | collective-permute-start | bytes 2211848 | tf_op jit(solution)/shard_map/ppermute | solution.py:300
  60.5 14.6 %collective-permute-start.9 = (f32[112,1280]{1,0:T(8,128)S(1)}, f32[112,1280]{1,0:T(8,128)S(1)}, u32[]{:S(2)}, u32[]{:S(2)}) collective-permute-start(f32[112,1280]{1,0:T(8,128)S(1)} %bitcast_add_fusion.4), channel_id=1, source_target_pairs={{0,1},{1,2},{2,3},{3,0},{4,7},{5,4},{6,5},{7,6},{8,9},{9,10},{10,1... | collective-permute-start | bytes 1720328 | tf_op jit(solution)/shard_map/ppermute | solution.py:300
  69.2 13.9 %collective-permute-start.11 = (f32[160,1280]{1,0:T(8,128)S(1)}, f32[160,1280]{1,0:T(8,128)S(1)}, u32[]{:S(2)}, u32[]{:S(2)}) collective-permute-start(f32[160,1280]{1,0:T(8,128)S(1)} %slice.63), channel_id=1, source_target_pairs={{0,96},{1,97},{2,98},{3,99},{4,28},{5,29},{6,30},{7,31},{8,104},{9... | collective-permute-start | bytes 2457608 | tf_op jit(solution)/shard_map/ppermute | solution.py:294
  81.6 1.5 %copy-start.2 = (f32[5248,128]{1,0:T(8,128)}, f32[5248,128]{1,0:T(8,128)S(1)}, u32[]{:S(2)}) copy-start(f32[5248,128]{1,0:T(8,128)S(1)} %pack.1) | copy-start | bytes 8060932
  83.2 49.5 %all-to-all-start = ((f32[128,1,5248]{2,1,0:T(1,128)}), f32[128,1,5248]{2,1,0:T(1,128)}, u32[]{:S(2)}, u32[]{:S(2)}) async-start(f32[128,1,5248]{2,1,0:T(1,128)} %bitcast.25), calls=%async_computation | async-start | bytes 5373952 | tf_op jit(solution)/shard_map/all_to_all | solution.py:458
  95.3 34.8 %collective-permute-start.12 = (f32[80,1280]{1,0:T(8,128)S(1)}, f32[80,1280]{1,0:T(8,128)S(1)}, u32[]{:S(2)}, u32[]{:S(2)}) collective-permute-start(f32[80,1280]{1,0:T(8,128)S(1)} %slice.65), channel_id=1, source_target_pairs={{0,8},{1,9},{2,10},{3,11},{4,36},{5,37},{6,38},{7,39},{8,0},{9,1},... | collective-permute-start | bytes 1228808 | tf_op jit(solution)/shard_map/ppermute | solution.py:294
  96.7 1.7 %copy-start.4 = (bf16[1024,1280]{1,0:T(8,128)(2,1)S(1)}, bf16[1024,1280]{1,0:T(8,128)(2,1)}, u32[]{:S(2)}) copy-start(bf16[1024,1280]{1,0:T(8,128)(2,1)} %memory_ref.5) | copy-start | bytes 7864324
  102.0 31.7 %copy-start.8 = (f32[512,160]{0,1:T(8,128)S(1)}, f32[512,160]{0,1:T(8,128)}, u32[]{:S(2)}) copy-start(f32[512,160]{0,1:T(8,128)} %param.16) | copy-start | bytes 983044
  102.0 31.7 %copy-start.9 = (f32[512,160]{0,1:T(8,128)S(1)}, f32[512,160]{0,1:T(8,128)}, u32[]{:S(2)}) copy-start(f32[512,160]{0,1:T(8,128)} %param.17) | copy-start | bytes 983044
  132.7 6.2 %collective-permute-start.13 = (f32[40,1280]{1,0:T(8,128)S(1)}, f32[40,1280]{1,0:T(8,128)S(1)}, u32[]{:S(2)}, u32[]{:S(2)}) collective-permute-start(f32[40,1280]{1,0:T(8,128)S(1)} %get-tuple-element.92), channel_id=1, source_target_pairs={{0,24},{1,25},{2,26},{3,27},{4,100},{5,101},{6,102},{7,103},{8,16}... | collective-permute-start | bytes 614408 | tf_op jit(solution)/shard_map/ppermute | solution.py:294

commit v4 on v3

--- a/solution.py
+++ b/solution.py
@@ -416,13 +416,10 @@
     mine, select = lax.optimization_barrier((mine, select))
     pair = mine + swapped(other, ((1, 0), (1, 0)))
     rest_top, rest_low, pair = lax.optimization_barrier((rest_top, rest_low, pair))
-    moved_top, moved_low = lax.optimization_barrier(
-        (passed_top + rest_top[1], passed_low + rest_low[1])
-    )
-    moved_top = turned(moved_top)
-    moved_low = turned(moved_low)
+    moved_top = turned(passed_top + rest_top[1])
+    moved_low = turned(passed_low + rest_low[1])
     grads = folded(pair, ((8, 0), (2, 0)))
-    rest_low, grads = lax.optimization_barrier((rest_low, grads))
+    rest_top, rest_low, grads = lax.optimization_barrier((rest_top, rest_low, grads))
     sum_top = moved_top + rest_top[2]
     sum_low = moved_low + rest_low[2]
     grads = folded(grads, ((24, 0), (6, 0)))
@@ -451,7 +448,7 @@
         in_specs=[total_spec] * 4 + [by_rows(depth), whole((depth, width))],
         out_specs=by_rows(width),
         out_shape=jax.ShapeDtypeStruct((tokens, width), BF16),
-        compiler_params=params(24),
+        compiler_params=params(58),
         cost_estimate=cost(2 * tokens * depth * width, 6 << 20),
         name="hidden_grad",
     )(*parts, memory, w_key)
@@ -462,8 +459,11 @@
         concat_axis=0,
         tiled=True,
     ).reshape(128 * CHUNK, 128)
-    grads = folded(grads, ((2, 0), (8, 0)))
-    received, hidden_grad, grads = lax.optimization_barrier((received, hidden_grad, grads))
+    blocks = grads.reshape(4, -1, 2 * width)
+    got = [
+        swapped(blocks[i], ((2 * bits, 0), (8 * bits, 0))) for i, bits in ((1, 3), (2, 1), (3, 2))
+    ]
+    received, hidden_grad = lax.optimization_barrier((received, hidden_grad))
     owned = mem_table.shape[0]
     table_spec = whole((EH, owned))
     new_table, new_sum = pl.pallas_call(
@@ -480,11 +480,10 @@
         cost_estimate=cost(4 * EH * 4096 * 512, 5 << 20),
         name="update",
     )(received, mem_table.T, adagrad_sum.T)
-    half = grads.shape[0] // 2
-    last = swapped(grads[half:], ((6, 0), (24, 0)))
-    kept, new_table = lax.optimization_barrier((grads[:half], new_table))
-    key_weight_grad = kept[:, :width] + last[:, :width]
-    value_weight_grad = kept[:, width:] + last[:, width:]
+    kept, new_table = lax.optimization_barrier((blocks[0], new_table))
+    total = (kept + got[0]) + (got[1] + got[2])
+    key_weight_grad = total[:, :width]
+    value_weight_grad = total[:, width:]
     return (hidden_grad, key_weight_grad, value_weight_grad, new_table.T, new_sum.T)
 
 

time: 140 us -> 134 us (0.957)
  waiting for transfers between devices: 52.8 us -> 44.8 us
  Pallas kernels: 40 us -> 42.1 us
  local copies, waits for them, and re-layouts: 7.86 us -> 6.18 us
    all_to_all x1, waiting for transfers between devices: 2.59 us -> 27.7 us  [body(): lax.all_to_all(packed.reshape(128, 1, CHUNK * 128), ('dp', 'tensor'), spl...]
    ppermute x5 -> x6, waiting for transfers between devices: 28.6 us -> 5.51 us  [swapped(): lax.ppermute(value, ('dp', 'tensor'), [(i, goal(i)) for i in range(128)])]
    ppermute x6, waiting for transfers between devices: 18.6 us -> 8.63 us  [turned(): lax.ppermute(value, ('dp', 'tensor'), [(i, goal(i)) for i in range(128)])]
    unnamed x24 -> x30, local copies, waits for them, and re-layouts: 7.64 us -> 4.39 us
    pallas_call x1, Pallas kernels: 3.52 us -> 5.93 us  [body(): pl.pallas_call(hidden_grad_kernel, grid=(4,), in_specs=[total_spec] * 4 +...]
    pallas_call x1, Pallas kernels: 4.72 us -> 3 us  [body(): pl.pallas_call(update_kernel, grid=(1,), in_specs=[whole((128 * CHUNK, 12...]
    ppermute x6, starting transfers between devices: 8.22 us -> 9.88 us  [turned(): lax.ppermute(value, ('dp', 'tensor'), [(i, goal(i)) for i in range(128)])]
    slice x1 -> x2, local copies, waits for them, and re-layouts: 0.03 us -> 1.62 us  [the longest x1 0.93 us: body(): blocks[i]]
  transfers between devices with their start and end apart: 15 -> 16, of which waited for: 8 -> 7; matrix products, arithmetic and copies ran while one was open for 2% -> 3% of each run, Pallas kernels for 21% -> 24%
where the time goes in v4:
time: 134 us
  waiting for transfers between devices  44.8 us (33%)
  Pallas kernels  42.1 us (31%)
  starting transfers between devices  36 us (27%)
  local copies, waits for them, and re-layouts  6.18 us (5%)
  other arithmetic  3.45 us (3%)
    all_to_all x1, waiting for transfers between devices, body(): lax.all_to_all(packed.reshape(128, 1, CHUNK * 128), ('dp', 'tensor'), spl...  27.7 us
    ppermute x6, starting transfers between devices, swapped(): lax.ppermute(value, ('dp', 'tensor'), [(i, goal(i)) for i in range(128)])  10.8 us
    all_to_all x1, starting transfers between devices, body(): lax.all_to_all(packed.reshape(128, 1, CHUNK * 128), ('dp', 'tensor'), spl...  10.7 us
    ppermute x6, starting transfers between devices, turned(): lax.ppermute(value, ('dp', 'tensor'), [(i, goal(i)) for i in range(128)])  9.88 us
    ppermute x6, waiting for transfers between devices, turned(): lax.ppermute(value, ('dp', 'tensor'), [(i, goal(i)) for i in range(128)])  8.63 us
    pallas_call x1, Pallas kernels, body(): pl.pallas_call(pack_kernel, grid=(1,), in_specs=[whole((top, depth)), who...  8.02 us
    pallas_call x1, Pallas kernels, body(): pl.pallas_call(forward_kernel, grid_spec=pltpu.PrefetchScalarGridSpec(num...  7.81 us
    pallas_call x1, Pallas kernels, body(): pl.pallas_call(rest_kernel, grid_spec=pltpu.PrefetchScalarGridSpec(num_sc...  6.17 us
  transfers between devices with their start and end apart: 16, of which 7 were waited for; matrix products, arithmetic and copies ran while one was open for 3% of the time, Pallas kernels for 24%

profile of v4, /device:TPU:1, one launch (start us, length us, event | category | flops | bytes accessed | tf_op | source)
XLA Modules:
  0.0 133.5 jit_solution(10751814212797719533)
XLA Ops:
  0.7 0.0 copy-start.1
  0.7 7.8 %forward.1 = (f32[2,1024]{1,0:T(2,128)S(1)}, bf16[256,1280]{1,0:T(8,128)(2,1)S(1)}) custom-call(s32[1]{0:T(128)} %bitcast.at_ref, bf16[1024,1280]{1,0:T(8,128)(2,1)} %memory_ref.5, bf16[1024,640]{1,0:T(8,128)(2,1)} %hidden_ref.3, bf16[1024,640]{1,0:T(8,128)(2,1)} %grad_ref.3, bf16[1280,640]{1,0:T(8,128)(2,1)} %wk_ref.7, bf16[1280,640]{1,0:T(8,128)(2,1)} %wv_ref.5), custom_call_target="tpu_custom_call" | custom-call | flops 3355443200 | bytes 12582912 | tf_op jit(solution)/shard_map/forward/pallas_call | solution.py:259
  8.5 0.0 copy-start.5
  8.5 3.6 %collective-permute-start.2 = (f32[2,1024]{1,0:T(2,128)S(1)}, f32[2,1024]{1,0:T(2,128)S(1)}, u32[]{:S(2)}, u32[]{:S(2)}) collective-permute-start(f32[2,1024]{1,0:T(2,128)S(1)} %get-tuple-element.74.p0), channel_id=1, source_target_pairs={{0,3},{1,0},{2,1},{3,2},{4,7},{5,4},{6,5},{7,6},{8,11},{9,8},{10,9... | collective-permute-start | bytes 24584 | tf_op jit(solution)/shard_map/ppermute | solution.py:285
  12.1 0.3 collective-permute-start.1
  12.5 0.7 collective-permute-start
  13.2 0.0 collective-permute-done.2.p3
  13.2 3.0 %collective-permute-done.1.p2 = f32[2,1024]{1,0:T(2,128)S(1)} collective-permute-done((f32[2,1024]{1,0:T(2,128)S(1)}, f32[2,1024]{1,0:T(2,128)S(1)}, u32[]{:S(2)}, u32[]{:S(2)}) %collective-permute-start.1) | collective-permute-done | bytes 8224 | tf_op jit(solution)/shard_map/ppermute | solution.py:285
  16.1 0.1 collective-permute-done.p1
  16.2 2.7 %first.1 = (f32[144,1280]{1,0:T(8,128)S(1)}, f32[112,1280]{1,0:T(8,128)}) custom-call(s32[1]{0:T(128)} %bitcast.at_ref, f32[2,1024]{1,0:T(2,128)S(1)} %get-tuple-element.74.p0, f32[2,1024]{1,0:T(2,128)S(1)} %collective-permute-done.p1, f32[2,1024]{1,0:T(2,128)S(1)} %collective-permute-done.1.p2, f32[2,1024]{1,0:T(2,128)S(1)} %collective-permute-done.2.p3, ...), custom_call_target="tpu_custom_call" | custom-call | flops 838860800 | bytes 6291456 | tf_op jit(solution)/shard_map/first/pallas_call | solution.py:310
  19.0 0.9 copy-done.9
  19.8 0.6 collective-permute-start.4
  20.4 1.4 %collective-permute-start.3 = (f32[144,1280]{1,0:T(8,128)}, f32[144,1280]{1,0:T(8,128)S(1)}, u32[]{:S(2)}, u32[]{:S(2)}) collective-permute-start(f32[144,1280]{1,0:T(8,128)} %copy-done.9), channel_id=1, source_target_pairs={{0,1},{1,2},{2,3},{3,0},{4,7},{5,4},{6,5},{7,6},{8,9},{9,10},{10,1... | collective-permute-start | bytes 2211848 | tf_op jit(solution)/shard_map/ppermute | solution.py:300
  21.8 0.1 pad_add_fusion.1.at_ref
  21.9 0.0 copy-start.3
  21.9 1.3 copy-done.3
  23.2 1.3 copy-done.4
  24.5 0.8 gate.1.both_ref
  25.3 0.1 pad_add_fusion.at_ref
  25.4 0.8 copy-done.2
  26.3 5.3 %weight_grad.1 = (f32[640,1280]{1,0:T(8,128)S(1)}, f32[640,1280]{1,0:T(8,128)S(1)}) custom-call(s32[3]{0:T(128)S(1)} %pad_add_fusion.1.at_ref, bf16[1024,1280]{1,0:T(8,128)(2,1)S(1)} %copy-done.2, bf16[1024,1280]{1,0:T(8,128)(2,1)S(1)} %gate.1.both_ref), custom_call_target="tpu_custom_call" | custom-call | flops 1 | bytes 1 | tf_op jit(solution)/shard_map/weight_grad/pallas_call | solution.py:344
  31.5 2.1 %collective-permute-start.6 = (f32[640,1280]{1,0:T(8,128)S(1)}, f32[640,1280]{1,0:T(8,128)S(1)}, u32[]{:S(2)}, u32[]{:S(2)}) collective-permute-start(f32[640,1280]{1,0:T(8,128)S(1)} %get-tuple-element.53), channel_id=1, source_target_pairs={{0,4},{1,5},{2,6},{3,7},{4,0},{5,1},{6,2},{7,3},{8,12},{9,13},{10,... | collective-permute-start | bytes 9830408 | tf_op jit(solution)/shard_map/ppermute | solution.py:294
  33.7 6.2 %rest.1 = (f32[3,144,1280]{2,1,0:T(8,128)S(1)}, f32[3,112,1280]{2,1,0:T(8,128)S(1)}) custom-call(s32[2]{0:T(128)S(1)} %pad_add_fusion.at_ref, bf16[1024,1280]{1,0:T(8,128)(2,1)S(1)} %gate.1.both_ref, bf16[1280,640]{1,0:T(8,128)(2,1)S(1)} %copy-done.1, bf16[1280,640]{1,0:T(8,128)(2,1)S(1)} %copy-done), custom_call_target="tpu_custom_call" | custom-call | flops 1 | bytes 1 | tf_op jit(solution)/shard_map/rest/pallas_call | solution.py:361
  39.8 0.0 collective-permute-done.4
  39.9 0.0 copy-start.12
  39.9 0.0 copy-start.13
  39.9 1.1 bitcast_add_fusion.5
  41.0 0.0 collective-permute-done.3
  41.0 0.1 bitcast_add_fusion.2
  41.1 1.4 %collective-permute-start.5 = (f32[144,1280]{1,0:T(8,128)S(1)}, f32[144,1280]{1,0:T(8,128)S(1)}, u32[]{:S(2)}, u32[]{:S(2)}) collective-permute-start(f32[144,1280]{1,0:T(8,128)S(1)} %bitcast_add_fusion.2), channel_id=1, source_target_pairs={{0,1},{1,2},{2,3},{3,0},{4,7},{5,4},{6,5},{7,6},{8,9},{9,10},{10,1... | collective-permute-start | bytes 2211848 | tf_op jit(solution)/shard_map/ppermute | solution.py:300
  42.5 2.4 %ranks.1 = (bf16[1024,2048]{1,0:T(8,128)(2,1)S(1)}, f32[2048,128]{1,0:T(8,128)S(1)}, f32[128,128]{1,0:T(8,128)S(1)}) custom-call(s32[2]{0:T(128)S(1)} %pad_add_fusion.at_ref, s32[8,1024]{1,0:T(8,128)S(1)} %bitcast.28, s32[8,1024]{1,0:T(8,128)S(1)} %bitcast.29), custom_call_target="tpu_custom_call" | custom-call | flops 68719476736 | bytes 134217728 | tf_op jit(solution)/shard_map/ranks/pallas_call | solution.py:395
  44.9 0.0 collective-permute-done.6
  44.9 0.4 add.47
  45.4 0.1 slice.56
  45.5 1.7 %collective-permute-start.8 = (f32[320,1280]{1,0:T(8,128)S(1)}, f32[320,1280]{1,0:T(8,128)S(1)}, u32[]{:S(2)}, u32[]{:S(2)}) collective-permute-start(f32[320,1280]{1,0:T(8,128)S(1)} %slice.56), channel_id=1, source_target_pairs={{0,32},{1,33},{2,34},{3,35},{4,12},{5,13},{6,14},{7,15},{8,40},{9,... | collective-permute-start | bytes 4915208 | tf_op jit(solution)/shard_map/ppermute | solution.py:294
  47.2 1.7 %collective-permute-start.9 = (f32[112,1280]{1,0:T(8,128)S(1)}, f32[112,1280]{1,0:T(8,128)S(1)}, u32[]{:S(2)}, u32[]{:S(2)}) collective-permute-start(f32[112,1280]{1,0:T(8,128)S(1)} %bitcast_add_fusion.5), channel_id=1, source_target_pairs={{0,1},{1,2},{2,3},{3,0},{4,7},{5,4},{6,5},{7,6},{8,9},{9,10},{10,1... | collective-permute-start | bytes 1720328 | tf_op jit(solution)/shard_map/ppermute | solution.py:300
  48.9 2.9 %collective-permute-done.5 = f32[144,1280]{1,0:T(8,128)S(1)} collective-permute-done((f32[144,1280]{1,0:T(8,128)S(1)}, f32[144,1280]{1,0:T(8,128)S(1)}, u32[]{:S(2)}, u32[]{:S(2)}) %collective-permute-start.5) | collective-permute-done | bytes 737312 | tf_op jit(solution)/shard_map/ppermute | solution.py:300
  51.8 0.1 bitcast_add_fusion.1
  51.9 2.3 %collective-permute-start.7 = (f32[144,1280]{1,0:T(8,128)S(1)}, f32[144,1280]{1,0:T(8,128)S(1)}, u32[]{:S(2)}, u32[]{:S(2)}) collective-permute-start(f32[144,1280]{1,0:T(8,128)S(1)} %bitcast_add_fusion.1), channel_id=1, source_target_pairs={{0,1},{1,2},{2,3},{3,0},{4,7},{5,4},{6,5},{7,6},{8,9},{9,10},{10,1... | collective-permute-start | bytes 2211848 | tf_op jit(solution)/shard_map/ppermute | solution.py:300
  54.2 3.7 %collective-permute-done.9 = f32[112,1280]{1,0:T(8,128)S(1)} collective-permute-done((f32[112,1280]{1,0:T(8,128)S(1)}, f32[112,1280]{1,0:T(8,128)S(1)}, u32[]{:S(2)}, u32[]{:S(2)}) %collective-permute-start.9) | collective-permute-done | bytes 573472 | tf_op jit(solution)/shard_map/ppermute | solution.py:300
  57.9 0.1 bitcast_add_fusion.4
  58.0 2.5 %collective-permute-start.10 = (f32[112,1280]{1,0:T(8,128)S(1)}, f32[112,1280]{1,0:T(8,128)S(1)}, u32[]{:S(2)}, u32[]{:S(2)}) collective-permute-start(f32[112,1280]{1,0:T(8,128)S(1)} %bitcast_add_fusion.4), channel_id=1, source_target_pairs={{0,1},{1,2},{2,3},{3,0},{4,7},{5,4},{6,5},{7,6},{8,9},{9,10},{10,1... | collective-permute-start | bytes 1720328 | tf_op jit(solution)/shard_map/ppermute | solution.py:300
  60.5 5.5 %collective-permute-done.8 = f32[320,1280]{1,0:T(8,128)S(1)} collective-permute-done((f32[320,1280]{1,0:T(8,128)S(1)}, f32[320,1280]{1,0:T(8,128)S(1)}, u32[]{:S(2)}, u32[]{:S(2)}) %collective-permute-start.8) | collective-permute-done | bytes 1638432 | tf_op jit(solution)/shard_map/ppermute | solution.py:294
  66.0 0.2 slice_add_fusion
  66.2 0.1 slice.61
  66.2 3.7 %collective-permute-start.11 = (f32[160,1280]{1,0:T(8,128)S(1)}, f32[160,1280]{1,0:T(8,128)S(1)}, u32[]{:S(2)}, u32[]{:S(2)}) collective-permute-start(f32[160,1280]{1,0:T(8,128)S(1)} %slice.61), channel_id=1, source_target_pairs={{0,96},{1,97},{2,98},{3,99},{4,28},{5,29},{6,30},{7,31},{8,104},{9... | collective-permute-start | bytes 2457608 | tf_op jit(solution)/shard_map/ppermute | solution.py:294
  69.9 0.0 collective-permute-done.7
  69.9 0.1 bitcast_add_fusion.top_ref
  70.0 2.0 %collective-permute-done.10 = f32[112,1280]{1,0:T(8,128)S(1)} collective-permute-done((f32[112,1280]{1,0:T(8,128)S(1)}, f32[112,1280]{1,0:T(8,128)S(1)}, u32[]{:S(2)}, u32[]{:S(2)}) %collective-permute-start.10) | collective-permute-done | bytes 573472 | tf_op jit(solution)/shard_map/ppermute | solution.py:300
  72.0 0.1 bitcast_add_fusion.3.low_ref
  72.1 8.0 %pack.1 = f32[5248,128]{1,0:T(8,128)} custom-call(f32[144,1280]{1,0:T(8,128)S(1)} %bitcast_add_fusion.top_ref, f32[112,1280]{1,0:T(8,128)S(1)} %bitcast_add_fusion.3.low_ref, bf16[1024,2048]{1,0:T(8,128)(2,1)S(1)} %get-tuple-element.69.select_ref, f32[2048,128]{1,0:T(8,128)S(1)} %get-tuple-element.70.group_ref, f32[128,128]{1,0:T(8,128)S(1)} %get-tuple-element.71.sent_ref), custom_call_target="tpu_custom_call" | custom-call | flops 5368709120 | bytes 12582912 | tf_op jit(solution)/shard_map/pack/pallas_call | solution.py:427
  80.1 0.0 collective-permute-done.11
  80.1 0.1 slice_add_fusion.1
  80.2 10.7 %all-to-all-start = ((f32[128,1,5248]{2,1,0:T(1,128)}), f32[128,1,5248]{2,1,0:T(1,128)S(1)}, u32[]{:S(2)}, u32[]{:S(2)}) async-start(f32[128,1,5248]{2,1,0:T(1,128)} %bitcast.13), calls=%async_computation | async-start | bytes 5373952 | tf_op jit(solution)/shard_map/all_to_all | solution.py:455
  90.9 0.9 fusion
  91.9 2.6 %collective-permute-start.12 = (f32[40,1280]{1,0:T(8,128)}, f32[40,1280]{1,0:T(8,128)S(1)}, u32[]{:S(2)}, u32[]{:S(2)}) collective-permute-start(f32[40,1280]{1,0:T(8,128)} %get-tuple-element.85), channel_id=1, source_target_pairs={{0,24},{1,25},{2,26},{3,27},{4,100},{5,101},{6,102},{7,103},{8,16}... | collective-permute-start | bytes 614408 | tf_op jit(solution)/shard_map/ppermute | solution.py:294
  94.5 0.6 collective-permute-start.14
  95.0 0.1 collective-permute-start.13
  95.1 5.9 %hidden_grad.1 = bf16[1024,640]{1,0:T(8,128)(2,1)} custom-call(f32[2,1024]{1,0:T(2,128)} %copy-done.5, f32[2,1024]{1,0:T(2,128)} %copy-done.8, f32[2,1024]{1,0:T(2,128)} %copy-done.7, f32[2,1024]{1,0:T(2,128)} %copy-done.6, bf16[1024,1280]{1,0:T(8,128)(2,1)} %memory_ref.5, bf16[1280,640]{1,0:T(8,128)(2,1)} %wk_ref.7), custom_call_target="tpu_custom_call" | custom-call | flops 1677721600 | bytes 6291456 | tf_op jit(solution)/shard_map/hidden_grad/pallas_call | solution.py:445
  101.0 27.7 %all-to-all-done = f32[128,1,5248]{2,1,0:T(1,128)S(1)} async-done(((f32[128,1,5248]{2,1,0:T(1,128)}), f32[128,1,5248]{2,1,0:T(1,128)S(1)}, u32[]{:S(2)}, u32[]{:S(2)}) %all-to-all-start) | async-done | bytes 2687008 | tf_op jit(solution)/shard_map/all_to_all | solution.py:455
  128.7 3.0 %update.1 = (f32[160,512]{1,0:T(8,128)}, f32[160,512]{1,0:T(8,128)}) custom-call(f32[5248,128]{1,0:T(8,128)S(1)} %bitcast.25, f32[160,512]{1,0:T(8,128)S(1)} %bitcast.26, f32[160,512]{1,0:T(8,128)S(1)} %bitcast.27), custom_call_target="tpu_custom_call" | custom-call | flops 1342177280 | bytes 5242880 | tf_op jit(solution)/shard_map/update/pallas_call | solution.py:469
  131.7 0.0 collective-permute-done.12
  131.7 1.1 add_add_fusion
  132.8 0.7 fusion.1
  (23 shorter events, 0.0 us)
Async XLA Ops:
  0.6 15.6 %copy-start = (bf16[1280,640]{1,0:T(8,128)(2,1)S(1)}, bf16[1280,640]{1,0:T(8,128)(2,1)}, u32[]{:S(2)}) copy-start(bf16[1280,640]{1,0:T(8,128)(2,1)} %wv_ref.5) | copy-start | bytes 4915204
  0.7 15.6 %copy-start.1 = (bf16[1280,640]{1,0:T(8,128)(2,1)S(1)}, bf16[1280,640]{1,0:T(8,128)(2,1)}, u32[]{:S(2)}) copy-start(bf16[1280,640]{1,0:T(8,128)(2,1)} %wk_ref.7) | copy-start | bytes 4915204
  8.5 13.4 %copy-start.5 = (f32[2,1024]{1,0:T(2,128)}, f32[2,1024]{1,0:T(2,128)S(1)}, u32[]{:S(2)}) copy-start(f32[2,1024]{1,0:T(2,128)S(1)} %get-tuple-element.74.p0) | copy-start | bytes 24580
  8.5 4.7 %collective-permute-start.2 = (f32[2,1024]{1,0:T(2,128)S(1)}, f32[2,1024]{1,0:T(2,128)S(1)}, u32[]{:S(2)}, u32[]{:S(2)}) collective-permute-start(f32[2,1024]{1,0:T(2,128)S(1)} %get-tuple-element.74.p0), channel_id=1, source_target_pairs={{0,3},{1,0},{2,1},{3,2},{4,7},{5,4},{6,5},{7,6},{8,11},{9,8},{10,9... | collective-permute-start | bytes 24584 | tf_op jit(solution)/shard_map/ppermute | solution.py:285
  12.1 4.0 %collective-permute-start.1 = (f32[2,1024]{1,0:T(2,128)S(1)}, f32[2,1024]{1,0:T(2,128)S(1)}, u32[]{:S(2)}, u32[]{:S(2)}) collective-permute-start(f32[2,1024]{1,0:T(2,128)S(1)} %get-tuple-element.74.p0), channel_id=1, source_target_pairs={{0,2},{1,3},{2,0},{3,1},{4,6},{5,7},{6,4},{7,5},{8,10},{9,11},{10,... | collective-permute-start | bytes 24584 | tf_op jit(solution)/shard_map/ppermute | solution.py:285
  12.5 3.7 %collective-permute-start = (f32[2,1024]{1,0:T(2,128)S(1)}, f32[2,1024]{1,0:T(2,128)S(1)}, u32[]{:S(2)}, u32[]{:S(2)}) collective-permute-start(f32[2,1024]{1,0:T(2,128)S(1)} %get-tuple-element.74.p0), channel_id=1, source_target_pairs={{0,1},{1,2},{2,3},{3,0},{4,5},{5,6},{6,7},{7,4},{8,9},{9,10},{10,1... | collective-permute-start | bytes 24584 | tf_op jit(solution)/shard_map/ppermute | solution.py:285
  13.2 8.7 %copy-start.6 = (f32[2,1024]{1,0:T(2,128)}, f32[2,1024]{1,0:T(2,128)S(1)}, u32[]{:S(2)}) copy-start(f32[2,1024]{1,0:T(2,128)S(1)} %collective-permute-done.2.p3) | copy-start | bytes 24580
  16.1 5.7 %copy-start.7 = (f32[2,1024]{1,0:T(2,128)}, f32[2,1024]{1,0:T(2,128)S(1)}, u32[]{:S(2)}) copy-start(f32[2,1024]{1,0:T(2,128)S(1)} %collective-permute-done.1.p2) | copy-start | bytes 24580
  16.2 5.7 %copy-start.8 = (f32[2,1024]{1,0:T(2,128)}, f32[2,1024]{1,0:T(2,128)S(1)}, u32[]{:S(2)}) copy-start(f32[2,1024]{1,0:T(2,128)S(1)} %collective-permute-done.p1) | copy-start | bytes 24580
  19.0 0.9 copy-start.9
  19.8 20.0 %collective-permute-start.4 = (f32[112,1280]{1,0:T(8,128)}, f32[112,1280]{1,0:T(8,128)}, u32[]{:S(2)}, u32[]{:S(2)}) collective-permute-start(f32[112,1280]{1,0:T(8,128)} %get-tuple-element.48), channel_id=1, source_target_pairs={{0,1},{1,2},{2,3},{3,0},{4,7},{5,4},{6,5},{7,6},{8,9},{9,10},{10,1... | collective-permute-start | bytes 1720328 | tf_op jit(solution)/shard_map/ppermute | solution.py:300
  20.4 20.6 %collective-permute-start.3 = (f32[144,1280]{1,0:T(8,128)}, f32[144,1280]{1,0:T(8,128)S(1)}, u32[]{:S(2)}, u32[]{:S(2)}) collective-permute-start(f32[144,1280]{1,0:T(8,128)} %copy-done.9), channel_id=1, source_target_pairs={{0,1},{1,2},{2,3},{3,0},{4,7},{5,4},{6,5},{7,6},{8,9},{9,10},{10,1... | collective-permute-start | bytes 2211848 | tf_op jit(solution)/shard_map/ppermute | solution.py:300
  21.9 1.3 copy-start.3
  23.2 1.3 copy-start.4
  24.5 1.7 %copy-start.2 = (bf16[1024,1280]{1,0:T(8,128)(2,1)S(1)}, bf16[1024,1280]{1,0:T(8,128)(2,1)}, u32[]{:S(2)}) copy-start(bf16[1024,1280]{1,0:T(8,128)(2,1)} %memory_ref.5) | copy-start | bytes 7864324
  31.5 13.4 %collective-permute-start.6 = (f32[640,1280]{1,0:T(8,128)S(1)}, f32[640,1280]{1,0:T(8,128)S(1)}, u32[]{:S(2)}, u32[]{:S(2)}) collective-permute-start(f32[640,1280]{1,0:T(8,128)S(1)} %get-tuple-element.53), channel_id=1, source_target_pairs={{0,4},{1,5},{2,6},{3,7},{4,0},{5,1},{6,2},{7,3},{8,12},{9,13},{10,... | collective-permute-start | bytes 9830408 | tf_op jit(solution)/shard_map/ppermute | solution.py:294
  39.9 2.7 %copy-start.12 = (s32[1024,8]{0,1:T(8,128)S(1)}, s32[1024,8]{0,1:T(8,128)}, u32[]{:S(2)}) copy-start(s32[1024,8]{0,1:T(8,128)} %param.14) | copy-start | bytes 98308
  39.9 2.7 %copy-start.13 = (s32[1024,8]{0,1:T(8,128)S(1)}, s32[1024,8]{0,1:T(8,128)}, u32[]{:S(2)}) copy-start(s32[1024,8]{0,1:T(8,128)} %param.15) | copy-start | bytes 98308
  41.1 10.7 %collective-permute-start.5 = (f32[144,1280]{1,0:T(8,128)S(1)}, f32[144,1280]{1,0:T(8,128)S(1)}, u32[]{:S(2)}, u32[]{:S(2)}) collective-permute-start(f32[144,1280]{1,0:T(8,128)S(1)} %bitcast_add_fusion.2), channel_id=1, source_target_pairs={{0,1},{1,2},{2,3},{3,0},{4,7},{5,4},{6,5},{7,6},{8,9},{9,10},{10,1... | collective-permute-start | bytes 2211848 | tf_op jit(solution)/shard_map/ppermute | solution.py:300
  45.5 20.5 %collective-permute-start.8 = (f32[320,1280]{1,0:T(8,128)S(1)}, f32[320,1280]{1,0:T(8,128)S(1)}, u32[]{:S(2)}, u32[]{:S(2)}) collective-permute-start(f32[320,1280]{1,0:T(8,128)S(1)} %slice.56), channel_id=1, source_target_pairs={{0,32},{1,33},{2,34},{3,35},{4,12},{5,13},{6,14},{7,15},{8,40},{9,... | collective-permute-start | bytes 4915208 | tf_op jit(solution)/shard_map/ppermute | solution.py:294
  47.2 10.7 %collective-permute-start.9 = (f32[112,1280]{1,0:T(8,128)S(1)}, f32[112,1280]{1,0:T(8,128)S(1)}, u32[]{:S(2)}, u32[]{:S(2)}) collective-permute-start(f32[112,1280]{1,0:T(8,128)S(1)} %bitcast_add_fusion.5), channel_id=1, source_target_pairs={{0,1},{1,2},{2,3},{3,0},{4,7},{5,4},{6,5},{7,6},{8,9},{9,10},{10,1... | collective-permute-start | bytes 1720328 | tf_op jit(solution)/shard_map/ppermute | solution.py:300
  51.9 18.0 %collective-permute-start.7 = (f32[144,1280]{1,0:T(8,128)S(1)}, f32[144,1280]{1,0:T(8,128)S(1)}, u32[]{:S(2)}, u32[]{:S(2)}) collective-permute-start(f32[144,1280]{1,0:T(8,128)S(1)} %bitcast_add_fusion.1), channel_id=1, source_target_pairs={{0,1},{1,2},{2,3},{3,0},{4,7},{5,4},{6,5},{7,6},{8,9},{9,10},{10,1... | collective-permute-start | bytes 2211848 | tf_op jit(solution)/shard_map/ppermute | solution.py:300
  58.0 14.0 %collective-permute-start.10 = (f32[112,1280]{1,0:T(8,128)S(1)}, f32[112,1280]{1,0:T(8,128)S(1)}, u32[]{:S(2)}, u32[]{:S(2)}) collective-permute-start(f32[112,1280]{1,0:T(8,128)S(1)} %bitcast_add_fusion.4), channel_id=1, source_target_pairs={{0,1},{1,2},{2,3},{3,0},{4,7},{5,4},{6,5},{7,6},{8,9},{9,10},{10,1... | collective-permute-start | bytes 1720328 | tf_op jit(solution)/shard_map/ppermute | solution.py:300
  66.2 13.8 %collective-permute-start.11 = (f32[160,1280]{1,0:T(8,128)S(1)}, f32[160,1280]{1,0:T(8,128)S(1)}, u32[]{:S(2)}, u32[]{:S(2)}) collective-permute-start(f32[160,1280]{1,0:T(8,128)S(1)} %slice.61), channel_id=1, source_target_pairs={{0,96},{1,97},{2,98},{3,99},{4,28},{5,29},{6,30},{7,31},{8,104},{9... | collective-permute-start | bytes 2457608 | tf_op jit(solution)/shard_map/ppermute | solution.py:294
  80.2 48.5 %all-to-all-start = ((f32[128,1,5248]{2,1,0:T(1,128)}), f32[128,1,5248]{2,1,0:T(1,128)S(1)}, u32[]{:S(2)}, u32[]{:S(2)}) async-start(f32[128,1,5248]{2,1,0:T(1,128)} %bitcast.13), calls=%async_computation | async-start | bytes 5373952 | tf_op jit(solution)/shard_map/all_to_all | solution.py:455
  91.9 39.9 %collective-permute-start.12 = (f32[40,1280]{1,0:T(8,128)}, f32[40,1280]{1,0:T(8,128)S(1)}, u32[]{:S(2)}, u32[]{:S(2)}) collective-permute-start(f32[40,1280]{1,0:T(8,128)} %get-tuple-element.85), channel_id=1, source_target_pairs={{0,24},{1,25},{2,26},{3,27},{4,100},{5,101},{6,102},{7,103},{8,16}... | collective-permute-start | bytes 614408 | tf_op jit(solution)/shard_map/ppermute | solution.py:294
  94.5 37.3 %collective-permute-start.14 = (f32[40,1280]{1,0:T(8,128)}, f32[40,1280]{1,0:T(8,128)}, u32[]{:S(2)}, u32[]{:S(2)}) collective-permute-start(f32[40,1280]{1,0:T(8,128)} %get-tuple-element.86), channel_id=1, source_target_pairs={{0,16},{1,17},{2,18},{3,19},{4,68},{5,69},{6,70},{7,71},{8,24},{9,... | collective-permute-start | bytes 614408 | tf_op jit(solution)/shard_map/ppermute | solution.py:294
  95.0 33.7 %copy-start.10 = (f32[512,160]{0,1:T(8,128)S(1)}, f32[512,160]{0,1:T(8,128)}, u32[]{:S(2)}) copy-start(f32[512,160]{0,1:T(8,128)} %param.16) | copy-start | bytes 983044
  95.0 33.7 %copy-start.11 = (f32[512,160]{0,1:T(8,128)S(1)}, f32[512,160]{0,1:T(8,128)}, u32[]{:S(2)}) copy-start(f32[512,160]{0,1:T(8,128)} %param.17) | copy-start | bytes 983044
  95.0 36.7 %collective-permute-start.13 = (f32[40,1280]{1,0:T(8,128)}, f32[40,1280]{1,0:T(8,128)}, u32[]{:S(2)}, u32[]{:S(2)}) collective-permute-start(f32[40,1280]{1,0:T(8,128)} %get-tuple-element.87), channel_id=1, source_target_pairs={{0,8},{1,9},{2,10},{3,11},{4,36},{5,37},{6,38},{7,39},{8,0},{9,1},... | collective-permute-start | bytes 614408 | tf_op jit(solution)/shard_map/ppermute | solution.py:294
  128.7 3.0 %copy-start.14 = (f32[40,1280]{1,0:T(8,128)S(1)}, f32[40,1280]{1,0:T(8,128)}, u32[]{:S(2)}) copy-start(f32[40,1280]{1,0:T(8,128)} %get-tuple-element.82) | copy-start | bytes 614404

commit v5 on v4

--- a/solution.py
+++ b/solution.py
@@ -68,13 +68,16 @@
         lower = jnp.where(match, (slot % 16).astype(F32), 0.0).astype(BF16)
         high = high + lax.dot_general(upper, place, OVER_LANES, preferred_element_type=F32)
         low = low + lax.dot_general(lower, place, OVER_LANES, preferred_element_type=F32)
-        columns = slice(h * count, (h + 1) * count)
-        group_ref[columns, :] = jnp.broadcast_to((rank // GROUP).astype(F32), (128, count)).T
+        groups = jnp.broadcast_to((rank // GROUP).astype(F32), (128, count)).T
         within = jnp.where(match, rank % GROUP, -1)
-        for k in range(GROUP):
-            select_ref[k * 128 : (k + 1) * 128, columns] = jnp.where(within == k, 1.0, 0.0).astype(
-                BF16
-            )
+        for piece in range(2):
+            tokens = slice(piece * 128, (piece + 1) * 128)
+            columns = slice((piece * HEADS + h) * 128, (piece * HEADS + h + 1) * 128)
+            group_ref[columns, :] = groups[tokens]
+            for k in range(GROUP):
+                select_ref[k * 128 : (k + 1) * 128, columns] = jnp.where(
+                    within[:, tokens] == k, 1.0, 0.0
+                ).astype(BF16)
     sent_ref[...] = 16.0 * high + low
 
 
@@ -107,18 +110,18 @@
 
 
 def memory_grad_tile(key_grad, value_grad, wk_ref, wv_ref, *out_refs):
-    for h in range(HEADS):
-        rows = slice(h * EH, (h + 1) * EH)
-        head = lax.dot_general(
-            key_grad, wk_ref[rows, :], OVER_LANES, preferred_element_type=F32
-        ) + lax.dot_general(value_grad, wv_ref[rows, :], OVER_LANES, preferred_element_type=F32)
-        tail = slice(HEADS * MAIN + h * TAIL, HEADS * MAIN + (h + 1) * TAIL)
-        at = 0
-        for out_ref in out_refs:
-            here = slice(at, at + out_ref.shape[0])
-            out_ref[:, h * MAIN : (h + 1) * MAIN] = head[here, :MAIN]
-            out_ref[:, tail] = head[here, MAIN:]
-            at += out_ref.shape[0]
+    grads = lax.dot_general(
+        key_grad, wk_ref[...], OVER_LANES, preferred_element_type=F32
+    ) + lax.dot_general(value_grad, wv_ref[...], OVER_LANES, preferred_element_type=F32)
+    at = 0
+    for out_ref in out_refs:
+        here = grads[at : at + out_ref.shape[0]]
+        for h in range(HEADS):
+            first = h * EH
+            out_ref[:, h * MAIN : (h + 1) * MAIN] = here[:, first : first + MAIN]
+            tail = slice(HEADS * MAIN + h * TAIL, HEADS * MAIN + (h + 1) * TAIL)
+            out_ref[:, tail] = here[:, first + MAIN : first + EH]
+        at += out_ref.shape[0]
 
 
 def first_kernel(at_ref, p0, p1, p2, p3, first_ref, wk_ref, wv_ref, top_ref, low_ref):
@@ -178,28 +181,32 @@
             other_ref[to, :] = value
 
 
-def pack_kernel(top_ref, low_ref, select_ref, group_ref, sent_ref, out_ref, rows):
-    count = top_ref.shape[0] + low_ref.shape[0]
-
-    def summed(cols):
-        return jnp.concatenate([top_ref[:, cols], low_ref[:, cols]], axis=0)
-
+def packed_group(j, sum_ref, select_ref, group_ref, rows):
+    count = sum_ref.shape[0]
     lane_group = lax.broadcasted_iota(jnp.int32, (count, 128), 1) // TAIL
+    for h in range(HEADS):
+        group = group_ref[h * count : (h + 1) * count, :]
+        if j < 4:
+            value = jnp.where(group == j, sum_ref[:, h * MAIN : (h + 1) * MAIN], 0.0)
+        else:
+            at = HEADS * MAIN + h * TAIL
+            tail = jnp.concatenate([sum_ref[:, at : at + TAIL]] * 4, axis=1)
+            value = jnp.where(group == lane_group.astype(F32), tail, 0.0)
+        top = value.astype(BF16)
+        rows[j, h * count : (h + 1) * count, :MAIN] = top
+        rows[j, h * count : (h + 1) * count, MAIN:] = (value - top.astype(F32)).astype(BF16)
+    found = jnp.dot(select_ref[...], rows[j], preferred_element_type=F32)
+    return found[:, :MAIN] + found[:, MAIN:]
+
+
+def pack_top_kernel(sum_ref, select_ref, group_ref, out_ref, rows):
     for j in range(5):
-        for h in range(HEADS):
-            group = group_ref[h * count : (h + 1) * count, :]
-            if j < 4:
-                value = jnp.where(group == j, summed(slice(h * MAIN, (h + 1) * MAIN)), 0.0)
-            else:
-                at = HEADS * MAIN + h * TAIL
-                tail = summed(slice(at, at + TAIL))
-                tail = jnp.concatenate([tail] * 4, axis=1)
-                value = jnp.where(group == lane_group.astype(F32), tail, 0.0)
-            top = value.astype(BF16)
-            rows[j, h * count : (h + 1) * count, :MAIN] = top
-            rows[j, h * count : (h + 1) * count, MAIN:] = (value - top.astype(F32)).astype(BF16)
-        found = jnp.dot(select_ref[...], rows[j], preferred_element_type=F32)
-        found = found[:, :MAIN] + found[:, MAIN:]
+        out_ref[j] = packed_group(j, sum_ref, select_ref, group_ref, rows)
+
+
+def pack_low_kernel(sum_ref, select_ref, group_ref, part_ref, sent_ref, out_ref, rows):
+    for j in range(5):
+        found = part_ref[j] + packed_group(j, sum_ref, select_ref, group_ref, rows)
         for k in range(GROUP):
             out_ref[pl.ds(j * GROUP + k, 128, stride=CHUNK), :] = found[k * 128 : (k + 1) * 128]
     out_ref[pl.ds(CAP + GROUP, 128, stride=CHUNK), :] = sent_ref[...]
@@ -304,7 +311,7 @@
 
     weights = [whole((depth, width))] * 2
     part_whole = whole((2, tokens))
-    top = 144
+    top = 128
     low = quarter - top
 
     first_top, first_low = pl.pallas_call(
@@ -424,23 +431,41 @@
     sum_low = moved_low + rest_low[2]
     grads = folded(grads, ((24, 0), (6, 0)))
 
+    half_rows = HEADS * quarter // 2
+
+    def piece_specs(piece):
+        return [
+            whole((quarter // 2, depth)),
+            pl.BlockSpec((GROUP * 128, half_rows), lambda i: (0, piece)),
+            pl.BlockSpec((half_rows, 128), lambda i: (piece, 0)),
+        ]
+
+    pack_part = pl.pallas_call(
+        pack_top_kernel,
+        grid=(1,),
+        in_specs=piece_specs(0),
+        out_specs=whole((5, GROUP * 128, 128)),
+        out_shape=jax.ShapeDtypeStruct((5, GROUP * 128, 128), F32),
+        scratch_shapes=[pltpu.VMEM((5, half_rows, 256), BF16)],
+        compiler_params=params(24),
+        cost_estimate=cost(1024 * 2048 * 1280, 8 << 20),
+        name="pack_top",
+    )(sum_top, select, group)
     packed = pl.pallas_call(
-        pack_kernel,
+        pack_low_kernel,
         grid=(1,),
         in_specs=[
-            whole((top, depth)),
-            whole((low, depth)),
-            whole((GROUP * 128, HEADS * quarter)),
-            whole((HEADS * quarter, 128)),
+            *piece_specs(1),
+            whole((5, GROUP * 128, 128)),
             whole((128, 128)),
         ],
         out_specs=whole((128 * CHUNK, 128)),
         out_shape=jax.ShapeDtypeStruct((128 * CHUNK, 128), F32),
-        scratch_shapes=[pltpu.VMEM((5, HEADS * quarter, 256), BF16)],
+        scratch_shapes=[pltpu.VMEM((5, half_rows, 256), BF16)],
         compiler_params=params(32),
-        cost_estimate=cost(2 * 1024 * 2048 * 1280, 12 << 20),
-        name="pack",
-    )(sum_top, sum_low, select, group, sent)
+        cost_estimate=cost(1024 * 2048 * 1280, 12 << 20),
+        name="pack_low",
+    )(sum_low, select, group, pack_part, sent)
     packed, grads, parts = lax.optimization_barrier((packed, grads, parts))
     hidden_grad = pl.pallas_call(
         hidden_grad_kernel,
@@ -481,9 +506,10 @@
         name="update",
     )(received, mem_table.T, adagrad_sum.T)
     kept, new_table = lax.optimization_barrier((blocks[0], new_table))
-    total = (kept + got[0]) + (got[1] + got[2])
-    key_weight_grad = total[:, :width]
-    value_weight_grad = total[:, width:]
+    sides = [slice(0, width), slice(width, 2 * width)]
+    key_weight_grad, value_weight_grad = (
+        (kept[:, at] + got[0][:, at]) + (got[1][:, at] + got[2][:, at]) for at in sides
+    )
     return (hidden_grad, key_weight_grad, value_weight_grad, new_table.T, new_sum.T)
 
 

time: 134 us -> 132 us (0.985)
  Pallas kernels: 42.1 us -> 40.4 us
    ppermute x6, waiting for transfers between devices: 8.63 us -> 6.3 us  [turned(): lax.ppermute(value, ('dp', 'tensor'), [(i, goal(i)) for i in range(128)])]
    ppermute x6, waiting for transfers between devices: 5.51 us -> 7.56 us  [swapped(): lax.ppermute(value, ('dp', 'tensor'), [(i, goal(i)) for i in range(128)])]
    pallas_call x1, Pallas kernels: 6.17 us -> 4.58 us  [body(): pl.pallas_call(rest_kernel, grid_spec=pltpu.PrefetchScalarGridSpec(num_sc...]
    pallas_call x1 -> x2, Pallas kernels: 8.02 us -> 8.06 us  [the longest x1 4.76 us: body(): pl.pallas_call(pack_low_kernel, grid=(1,), in_specs=[*piece_specs(1), who...]
  transfers between devices with their start and end apart: 16 -> 16, of which waited for: 7 -> 7; matrix products, arithmetic and copies ran while one was open for 3% -> 3% of each run, Pallas kernels for 24% -> 23%
where the time goes in v5:
time: 132 us
  waiting for transfers between devices  44.1 us (33%)
  Pallas kernels  40.4 us (31%)
  starting transfers between devices  36.7 us (28%)
  local copies, waits for them, and re-layouts  5.48 us (4%)
  other arithmetic  4.29 us (3%)
    all_to_all x1, waiting for transfers between devices, body(): lax.all_to_all(packed.reshape(128, 1, CHUNK * 128), ('dp', 'tensor'), spl...  27.2 us
    ppermute x6, starting transfers between devices, swapped(): lax.ppermute(value, ('dp', 'tensor'), [(i, goal(i)) for i in range(128)])  11.3 us
    all_to_all x1, starting transfers between devices, body(): lax.all_to_all(packed.reshape(128, 1, CHUNK * 128), ('dp', 'tensor'), spl...  10.8 us
    ppermute x6, starting transfers between devices, turned(): lax.ppermute(value, ('dp', 'tensor'), [(i, goal(i)) for i in range(128)])  9.97 us
    pallas_call x1, Pallas kernels, body(): pl.pallas_call(forward_kernel, grid_spec=pltpu.PrefetchScalarGridSpec(num...  7.81 us
    ppermute x6, waiting for transfers between devices, swapped(): lax.ppermute(value, ('dp', 'tensor'), [(i, goal(i)) for i in range(128)])  7.56 us
    ppermute x6, waiting for transfers between devices, turned(): lax.ppermute(value, ('dp', 'tensor'), [(i, goal(i)) for i in range(128)])  6.3 us
    pallas_call x1, Pallas kernels, body(): pl.pallas_call(hidden_grad_kernel, grid=(4,), in_specs=[total_spec] * 4 +...  5.89 us
  transfers between devices with their start and end apart: 16, of which 7 were waited for; matrix products, arithmetic and copies ran while one was open for 3% of the time, Pallas kernels for 23%

profile of v5, /device:TPU:1, one launch (start us, length us, event | category | flops | bytes accessed | tf_op | source)
XLA Modules:
  0.0 131.8 jit_solution(2275174125629061087)
XLA Ops:
  0.7 0.0 copy-start.1
  0.7 7.8 %forward.1 = (f32[2,1024]{1,0:T(2,128)S(1)}, bf16[256,1280]{1,0:T(8,128)(2,1)S(1)}) custom-call(s32[1]{0:T(128)} %bitcast.at_ref, bf16[1024,1280]{1,0:T(8,128)(2,1)} %memory_ref.5, bf16[1024,640]{1,0:T(8,128)(2,1)} %hidden_ref.3, bf16[1024,640]{1,0:T(8,128)(2,1)} %grad_ref.3, bf16[1280,640]{1,0:T(8,128)(2,1)} %wk_ref.7, bf16[1280,640]{1,0:T(8,128)(2,1)} %wv_ref.5), custom_call_target="tpu_custom_call" | custom-call | flops 3355443200 | bytes 12582912 | tf_op jit(solution)/shard_map/forward/pallas_call | solution.py:266
  8.5 0.0 copy-start.5
  8.5 3.6 %collective-permute-start.2 = (f32[2,1024]{1,0:T(2,128)S(1)}, f32[2,1024]{1,0:T(2,128)S(1)}, u32[]{:S(2)}, u32[]{:S(2)}) collective-permute-start(f32[2,1024]{1,0:T(2,128)S(1)} %get-tuple-element.74.p0), channel_id=1, source_target_pairs={{0,3},{1,0},{2,1},{3,2},{4,7},{5,4},{6,5},{7,6},{8,11},{9,8},{10,9... | collective-permute-start | bytes 24584 | tf_op jit(solution)/shard_map/ppermute | solution.py:292
  12.1 0.3 collective-permute-start.1
  12.5 0.7 collective-permute-start
  13.2 0.0 collective-permute-done.2.p3
  13.2 3.0 %collective-permute-done.1.p2 = f32[2,1024]{1,0:T(2,128)S(1)} collective-permute-done((f32[2,1024]{1,0:T(2,128)S(1)}, f32[2,1024]{1,0:T(2,128)S(1)}, u32[]{:S(2)}, u32[]{:S(2)}) %collective-permute-start.1) | collective-permute-done | bytes 8224 | tf_op jit(solution)/shard_map/ppermute | solution.py:292
  16.1 0.1 collective-permute-done.p1
  16.2 2.2 %first.1 = (f32[128,1280]{1,0:T(8,128)}, f32[128,1280]{1,0:T(8,128)S(1)}) custom-call(s32[1]{0:T(128)} %bitcast.at_ref, f32[2,1024]{1,0:T(2,128)S(1)} %get-tuple-element.74.p0, f32[2,1024]{1,0:T(2,128)S(1)} %collective-permute-done.p1, f32[2,1024]{1,0:T(2,128)S(1)} %collective-permute-done.1.p2, f32[2,1024]{1,0:T(2,128)S(1)} %collective-permute-done.2.p3, ...), custom_call_target="tpu_custom_call" | custom-call | flops 838860800 | bytes 6291456 | tf_op jit(solution)/shard_map/first/pallas_call | solution.py:317
  18.5 0.9 copy-done.9
  19.3 0.6 collective-permute-start.3
  19.9 1.4 %collective-permute-start.4 = (f32[128,1280]{1,0:T(8,128)}, f32[128,1280]{1,0:T(8,128)S(1)}, u32[]{:S(2)}, u32[]{:S(2)}) collective-permute-start(f32[128,1280]{1,0:T(8,128)} %copy-done.9), channel_id=1, source_target_pairs={{0,1},{1,2},{2,3},{3,0},{4,7},{5,4},{6,5},{7,6},{8,9},{9,10},{10,1... | collective-permute-start | bytes 1966088 | tf_op jit(solution)/shard_map/ppermute | solution.py:307
  21.3 0.1 pad_add_fusion.1.at_ref
  21.4 0.0 copy-start.3
  21.4 1.3 copy-done.3
  22.7 1.3 copy-done.4
  24.0 0.8 gate.1.both_ref
  24.8 0.1 pad_add_fusion.at_ref
  24.9 0.8 copy-done.2
  25.8 5.3 %weight_grad.1 = (f32[640,1280]{1,0:T(8,128)S(1)}, f32[640,1280]{1,0:T(8,128)S(1)}) custom-call(s32[3]{0:T(128)S(1)} %pad_add_fusion.1.at_ref, bf16[1024,1280]{1,0:T(8,128)(2,1)S(1)} %copy-done.2, bf16[1024,1280]{1,0:T(8,128)(2,1)S(1)} %gate.1.both_ref), custom_call_target="tpu_custom_call" | custom-call | flops 1 | bytes 1 | tf_op jit(solution)/shard_map/weight_grad/pallas_call | solution.py:351
  31.0 2.1 %collective-permute-start.6 = (f32[640,1280]{1,0:T(8,128)S(1)}, f32[640,1280]{1,0:T(8,128)S(1)}, u32[]{:S(2)}, u32[]{:S(2)}) collective-permute-start(f32[640,1280]{1,0:T(8,128)S(1)} %get-tuple-element.53), channel_id=1, source_target_pairs={{0,4},{1,5},{2,6},{3,7},{4,0},{5,1},{6,2},{7,3},{8,12},{9,13},{10,... | collective-permute-start | bytes 9830408 | tf_op jit(solution)/shard_map/ppermute | solution.py:301
  33.2 4.6 %rest.1 = (f32[3,128,1280]{2,1,0:T(8,128)S(1)}, f32[3,128,1280]{2,1,0:T(8,128)S(1)}) custom-call(s32[2]{0:T(128)S(1)} %pad_add_fusion.at_ref, bf16[1024,1280]{1,0:T(8,128)(2,1)S(1)} %gate.1.both_ref, bf16[1280,640]{1,0:T(8,128)(2,1)S(1)} %copy-done.1, bf16[1280,640]{1,0:T(8,128)(2,1)S(1)} %copy-done), custom_call_target="tpu_custom_call" | custom-call | flops 1 | bytes 1 | tf_op jit(solution)/shard_map/rest/pallas_call | solution.py:368
  37.7 0.0 collective-permute-done.3
  37.8 0.0 copy-start.12
  37.8 0.0 copy-start.13
  37.8 1.2 bitcast_add_fusion.5
  39.0 0.0 collective-permute-done.4
  39.0 0.1 bitcast_add_fusion.4
  39.1 1.4 %collective-permute-start.9 = (f32[128,1280]{1,0:T(8,128)S(1)}, f32[128,1280]{1,0:T(8,128)S(1)}, u32[]{:S(2)}, u32[]{:S(2)}) collective-permute-start(f32[128,1280]{1,0:T(8,128)S(1)} %bitcast_add_fusion.5), channel_id=1, source_target_pairs={{0,1},{1,2},{2,3},{3,0},{4,7},{5,4},{6,5},{7,6},{8,9},{9,10},{10,1... | collective-permute-start | bytes 1966088 | tf_op jit(solution)/shard_map/ppermute | solution.py:307
  40.5 2.7 %ranks.1 = (bf16[1024,2048]{1,0:T(8,128)(2,1)S(1)}, f32[2048,128]{1,0:T(8,128)S(1)}, f32[128,128]{1,0:T(8,128)S(1)}) custom-call(s32[2]{0:T(128)S(1)} %pad_add_fusion.at_ref, s32[8,1024]{1,0:T(8,128)S(1)} %bitcast.28, s32[8,1024]{1,0:T(8,128)S(1)} %bitcast.29), custom_call_target="tpu_custom_call" | custom-call | flops 68719476736 | bytes 134217728 | tf_op jit(solution)/shard_map/ranks/pallas_call | solution.py:402
  43.2 0.4 add.56
  43.6 0.1 slice.74
  43.8 1.7 %collective-permute-start.8 = (f32[320,1280]{1,0:T(8,128)S(1)}, f32[320,1280]{1,0:T(8,128)S(1)}, u32[]{:S(2)}, u32[]{:S(2)}) collective-permute-start(f32[320,1280]{1,0:T(8,128)S(1)} %slice.74), channel_id=1, source_target_pairs={{0,32},{1,33},{2,34},{3,35},{4,12},{5,13},{6,14},{7,15},{8,40},{9,... | collective-permute-start | bytes 4915208 | tf_op jit(solution)/shard_map/ppermute | solution.py:301
  45.5 1.7 %collective-permute-start.5 = (f32[128,1280]{1,0:T(8,128)S(1)}, f32[128,1280]{1,0:T(8,128)S(1)}, u32[]{:S(2)}, u32[]{:S(2)}) collective-permute-start(f32[128,1280]{1,0:T(8,128)S(1)} %bitcast_add_fusion.4), channel_id=1, source_target_pairs={{0,1},{1,2},{2,3},{3,0},{4,7},{5,4},{6,5},{7,6},{8,9},{9,10},{10,1... | collective-permute-start | bytes 1966088 | tf_op jit(solution)/shard_map/ppermute | solution.py:307
  47.2 1.7 %collective-permute-done.9 = f32[128,1280]{1,0:T(8,128)S(1)} collective-permute-done((f32[128,1280]{1,0:T(8,128)S(1)}, f32[128,1280]{1,0:T(8,128)S(1)}, u32[]{:S(2)}, u32[]{:S(2)}) %collective-permute-start.9) | collective-permute-done | bytes 655392 | tf_op jit(solution)/shard_map/ppermute | solution.py:307
  48.9 0.1 bitcast_add_fusion.1
  48.9 2.3 %collective-permute-start.10 = (f32[128,1280]{1,0:T(8,128)S(1)}, f32[128,1280]{1,0:T(8,128)S(1)}, u32[]{:S(2)}, u32[]{:S(2)}) collective-permute-start(f32[128,1280]{1,0:T(8,128)S(1)} %bitcast_add_fusion.1), channel_id=1, source_target_pairs={{0,1},{1,2},{2,3},{3,0},{4,7},{5,4},{6,5},{7,6},{8,9},{9,10},{10,1... | collective-permute-start | bytes 1966088 | tf_op jit(solution)/shard_map/ppermute | solution.py:307
  51.3 4.6 %collective-permute-done.5 = f32[128,1280]{1,0:T(8,128)S(1)} collective-permute-done((f32[128,1280]{1,0:T(8,128)S(1)}, f32[128,1280]{1,0:T(8,128)S(1)}, u32[]{:S(2)}, u32[]{:S(2)}) %collective-permute-start.5) | collective-permute-done | bytes 655392 | tf_op jit(solution)/shard_map/ppermute | solution.py:307
  55.9 0.1 bitcast_add_fusion.3
  56.0 2.5 %collective-permute-start.7 = (f32[128,1280]{1,0:T(8,128)S(1)}, f32[128,1280]{1,0:T(8,128)S(1)}, u32[]{:S(2)}, u32[]{:S(2)}) collective-permute-start(f32[128,1280]{1,0:T(8,128)S(1)} %bitcast_add_fusion.3), channel_id=1, source_target_pairs={{0,1},{1,2},{2,3},{3,0},{4,7},{5,4},{6,5},{7,6},{8,9},{9,10},{10,1... | collective-permute-start | bytes 1966088 | tf_op jit(solution)/shard_map/ppermute | solution.py:307
  58.5 5.8 %collective-permute-done.8 = f32[320,1280]{1,0:T(8,128)S(1)} collective-permute-done((f32[320,1280]{1,0:T(8,128)S(1)}, f32[320,1280]{1,0:T(8,128)S(1)}, u32[]{:S(2)}, u32[]{:S(2)}) %collective-permute-start.8) | collective-permute-done | bytes 1638432 | tf_op jit(solution)/shard_map/ppermute | solution.py:301
  64.3 0.3 slice_add_fusion
  64.6 0.1 slice.79
  64.6 3.7 %collective-permute-start.11 = (f32[160,1280]{1,0:T(8,128)S(1)}, f32[160,1280]{1,0:T(8,128)S(1)}, u32[]{:S(2)}, u32[]{:S(2)}) collective-permute-start(f32[160,1280]{1,0:T(8,128)S(1)} %slice.79), channel_id=1, source_target_pairs={{0,96},{1,97},{2,98},{3,99},{4,28},{5,29},{6,30},{7,31},{8,104},{9... | collective-permute-start | bytes 2457608 | tf_op jit(solution)/shard_map/ppermute | solution.py:301
  68.3 0.0 collective-permute-done.10
  68.3 0.1 bitcast_add_fusion.sum_ref
  68.4 3.3 %pack_top.1.part_ref = f32[5,1024,128]{2,1,0:T(8,128)S(1)} custom-call(f32[128,1280]{1,0:T(8,128)S(1)} %bitcast_add_fusion.sum_ref, bf16[1024,2048]{1,0:T(8,128)(2,1)S(1)} %get-tuple-element.67.select_ref, f32[2048,128]{1,0:T(8,128)S(1)} %get-tuple-element.68.group_ref), custom_call_target="tpu_custom_call" | custom-call | flops 2684354560 | bytes 8388608 | tf_op jit(solution)/shard_map/pack_top/pallas_call | solution.py:443
  71.7 0.0 collective-permute-done.7
  71.7 0.1 bitcast_add_fusion.2.sum_ref
  71.8 4.8 %pack_low.1 = f32[5248,128]{1,0:T(8,128)} custom-call(f32[128,1280]{1,0:T(8,128)S(1)} %bitcast_add_fusion.2.sum_ref, bf16[1024,2048]{1,0:T(8,128)(2,1)S(1)} %get-tuple-element.67.select_ref, f32[2048,128]{1,0:T(8,128)S(1)} %get-tuple-element.68.group_ref, f32[5,1024,128]{2,1,0:T(8,128)S(1)} %pack_top.1.part_ref, f32[128,128]{1,0:T(8,128)S(1)} %get-tuple-element.71.sent_ref), custom_call_target="tpu_custom_call" | custom-call | flops 2684354560 | bytes 12582912 | tf_op jit(solution)/shard_map/pack_low/pallas_call | solution.py:454
  76.5 1.8 %collective-permute-done.11 = f32[160,1280]{1,0:T(8,128)S(1)} collective-permute-done((f32[160,1280]{1,0:T(8,128)S(1)}, f32[160,1280]{1,0:T(8,128)S(1)}, u32[]{:S(2)}, u32[]{:S(2)}) %collective-permute-start.11) | collective-permute-done | bytes 819232 | tf_op jit(solution)/shard_map/ppermute | solution.py:301
  78.3 0.1 slice_add_fusion.1
  78.4 10.8 %all-to-all-start = ((f32[128,1,5248]{2,1,0:T(1,128)}), f32[128,1,5248]{2,1,0:T(1,128)S(1)}, u32[]{:S(2)}, u32[]{:S(2)}) async-start(f32[128,1,5248]{2,1,0:T(1,128)} %bitcast.13), calls=%async_computation | async-start | bytes 5373952 | tf_op jit(solution)/shard_map/all_to_all | solution.py:480
  89.2 0.9 fusion.2
  90.1 2.9 %collective-permute-start.14 = (f32[40,1280]{1,0:T(8,128)}, f32[40,1280]{1,0:T(8,128)S(1)}, u32[]{:S(2)}, u32[]{:S(2)}) collective-permute-start(f32[40,1280]{1,0:T(8,128)} %get-tuple-element.88), channel_id=1, source_target_pairs={{0,16},{1,17},{2,18},{3,19},{4,68},{5,69},{6,70},{7,71},{8,24},{9,... | collective-permute-start | bytes 614408 | tf_op jit(solution)/shard_map/ppermute | solution.py:301
  93.0 0.3 collective-permute-start.13
  93.3 0.6 collective-permute-start.12
  93.9 5.9 %hidden_grad.1 = bf16[1024,640]{1,0:T(8,128)(2,1)} custom-call(f32[2,1024]{1,0:T(2,128)} %copy-done.5, f32[2,1024]{1,0:T(2,128)} %copy-done.8, f32[2,1024]{1,0:T(2,128)} %copy-done.7, f32[2,1024]{1,0:T(2,128)} %copy-done.6, bf16[1024,1280]{1,0:T(8,128)(2,1)} %memory_ref.5, bf16[1280,640]{1,0:T(8,128)(2,1)} %wk_ref.7), custom_call_target="tpu_custom_call" | custom-call | flops 1677721600 | bytes 6291456 | tf_op jit(solution)/shard_map/hidden_grad/pallas_call | solution.py:470
  99.8 27.2 %all-to-all-done = f32[128,1,5248]{2,1,0:T(1,128)S(1)} async-done(((f32[128,1,5248]{2,1,0:T(1,128)}), f32[128,1,5248]{2,1,0:T(1,128)S(1)}, u32[]{:S(2)}, u32[]{:S(2)}) %all-to-all-start) | async-done | bytes 2687008 | tf_op jit(solution)/shard_map/all_to_all | solution.py:480
  127.0 3.0 %update.1 = (f32[160,512]{1,0:T(8,128)}, f32[160,512]{1,0:T(8,128)}) custom-call(f32[5248,128]{1,0:T(8,128)S(1)} %bitcast.25, f32[160,512]{1,0:T(8,128)S(1)} %bitcast.26, f32[160,512]{1,0:T(8,128)S(1)} %bitcast.27), custom_call_target="tpu_custom_call" | custom-call | flops 1342177280 | bytes 5242880 | tf_op jit(solution)/shard_map/update/pallas_call | solution.py:494
  130.0 0.0 collective-permute-done.13
  130.0 0.0 collective-permute-done.12
  130.0 1.8 %fusion = (f32[40,640]{1,0:T(8,128)}, f32[40,640]{1,0:T(8,128)}) fusion(f32[40,1280]{1,0:T(8,128)S(1)} %collective-permute-done.14, f32[40,1280]{1,0:T(8,128)} %collective-permute-done.13, f32[40,1280]{1,0:T(8,128)} %collective-permute-done.12, f32[40,1280]{1,0:T(8,128)S(1)} %copy-done.14), kind=kLoop, calls=%fused_computation.9 | loop fusion | flops 153600 | bytes 1024000 | tf_op jit(solution)/shard_map/add | solution.py:511
  (23 shorter events, 0.0 us)
Async XLA Ops:
  0.6 15.6 %copy-start = (bf16[1280,640]{1,0:T(8,128)(2,1)S(1)}, bf16[1280,640]{1,0:T(8,128)(2,1)}, u32[]{:S(2)}) copy-start(bf16[1280,640]{1,0:T(8,128)(2,1)} %wv_ref.5) | copy-start | bytes 4915204
  0.7 15.6 %copy-start.1 = (bf16[1280,640]{1,0:T(8,128)(2,1)S(1)}, bf16[1280,640]{1,0:T(8,128)(2,1)}, u32[]{:S(2)}) copy-start(bf16[1280,640]{1,0:T(8,128)(2,1)} %wk_ref.7) | copy-start | bytes 4915204
  8.5 12.9 %copy-start.5 = (f32[2,1024]{1,0:T(2,128)}, f32[2,1024]{1,0:T(2,128)S(1)}, u32[]{:S(2)}) copy-start(f32[2,1024]{1,0:T(2,128)S(1)} %get-tuple-element.74.p0) | copy-start | bytes 24580
  8.5 4.7 %collective-permute-start.2 = (f32[2,1024]{1,0:T(2,128)S(1)}, f32[2,1024]{1,0:T(2,128)S(1)}, u32[]{:S(2)}, u32[]{:S(2)}) collective-permute-start(f32[2,1024]{1,0:T(2,128)S(1)} %get-tuple-element.74.p0), channel_id=1, source_target_pairs={{0,3},{1,0},{2,1},{3,2},{4,7},{5,4},{6,5},{7,6},{8,11},{9,8},{10,9... | collective-permute-start | bytes 24584 | tf_op jit(solution)/shard_map/ppermute | solution.py:292
  12.1 4.0 %collective-permute-start.1 = (f32[2,1024]{1,0:T(2,128)S(1)}, f32[2,1024]{1,0:T(2,128)S(1)}, u32[]{:S(2)}, u32[]{:S(2)}) collective-permute-start(f32[2,1024]{1,0:T(2,128)S(1)} %get-tuple-element.74.p0), channel_id=1, source_target_pairs={{0,2},{1,3},{2,0},{3,1},{4,6},{5,7},{6,4},{7,5},{8,10},{9,11},{10,... | collective-permute-start | bytes 24584 | tf_op jit(solution)/shard_map/ppermute | solution.py:292
  12.5 3.7 %collective-permute-start = (f32[2,1024]{1,0:T(2,128)S(1)}, f32[2,1024]{1,0:T(2,128)S(1)}, u32[]{:S(2)}, u32[]{:S(2)}) collective-permute-start(f32[2,1024]{1,0:T(2,128)S(1)} %get-tuple-element.74.p0), channel_id=1, source_target_pairs={{0,1},{1,2},{2,3},{3,0},{4,5},{5,6},{6,7},{7,4},{8,9},{9,10},{10,1... | collective-permute-start | bytes 24584 | tf_op jit(solution)/shard_map/ppermute | solution.py:292
  13.2 8.2 %copy-start.6 = (f32[2,1024]{1,0:T(2,128)}, f32[2,1024]{1,0:T(2,128)S(1)}, u32[]{:S(2)}) copy-start(f32[2,1024]{1,0:T(2,128)S(1)} %collective-permute-done.2.p3) | copy-start | bytes 24580
  16.1 5.2 %copy-start.7 = (f32[2,1024]{1,0:T(2,128)}, f32[2,1024]{1,0:T(2,128)S(1)}, u32[]{:S(2)}) copy-start(f32[2,1024]{1,0:T(2,128)S(1)} %collective-permute-done.1.p2) | copy-start | bytes 24580
  16.2 5.1 %copy-start.8 = (f32[2,1024]{1,0:T(2,128)}, f32[2,1024]{1,0:T(2,128)S(1)}, u32[]{:S(2)}) copy-start(f32[2,1024]{1,0:T(2,128)S(1)} %collective-permute-done.p1) | copy-start | bytes 24580
  18.5 0.9 copy-start.9
  19.3 18.4 %collective-permute-start.3 = (f32[128,1280]{1,0:T(8,128)}, f32[128,1280]{1,0:T(8,128)}, u32[]{:S(2)}, u32[]{:S(2)}) collective-permute-start(f32[128,1280]{1,0:T(8,128)} %get-tuple-element.47), channel_id=1, source_target_pairs={{0,1},{1,2},{2,3},{3,0},{4,7},{5,4},{6,5},{7,6},{8,9},{9,10},{10,1... | collective-permute-start | bytes 1966088 | tf_op jit(solution)/shard_map/ppermute | solution.py:307
  19.9 19.1 %collective-permute-start.4 = (f32[128,1280]{1,0:T(8,128)}, f32[128,1280]{1,0:T(8,128)S(1)}, u32[]{:S(2)}, u32[]{:S(2)}) collective-permute-start(f32[128,1280]{1,0:T(8,128)} %copy-done.9), channel_id=1, source_target_pairs={{0,1},{1,2},{2,3},{3,0},{4,7},{5,4},{6,5},{7,6},{8,9},{9,10},{10,1... | collective-permute-start | bytes 1966088 | tf_op jit(solution)/shard_map/ppermute | solution.py:307
  21.4 1.3 %copy-start.3 = (bf16[1024,640]{1,0:T(8,128)(2,1)S(1)}, bf16[1024,640]{1,0:T(8,128)(2,1)}, u32[]{:S(2)}) copy-start(bf16[1024,640]{1,0:T(8,128)(2,1)} %hidden_ref.3) | copy-start | bytes 3932164
  22.7 1.3 copy-start.4
  24.0 1.7 %copy-start.2 = (bf16[1024,1280]{1,0:T(8,128)(2,1)S(1)}, bf16[1024,1280]{1,0:T(8,128)(2,1)}, u32[]{:S(2)}) copy-start(bf16[1024,1280]{1,0:T(8,128)(2,1)} %memory_ref.5) | copy-start | bytes 7864324
  31.0 12.2 %collective-permute-start.6 = (f32[640,1280]{1,0:T(8,128)S(1)}, f32[640,1280]{1,0:T(8,128)S(1)}, u32[]{:S(2)}, u32[]{:S(2)}) collective-permute-start(f32[640,1280]{1,0:T(8,128)S(1)} %get-tuple-element.53), channel_id=1, source_target_pairs={{0,4},{1,5},{2,6},{3,7},{4,0},{5,1},{6,2},{7,3},{8,12},{9,13},{10,... | collective-permute-start | bytes 9830408 | tf_op jit(solution)/shard_map/ppermute | solution.py:301
  37.8 2.7 %copy-start.12 = (s32[1024,8]{0,1:T(8,128)S(1)}, s32[1024,8]{0,1:T(8,128)}, u32[]{:S(2)}) copy-start(s32[1024,8]{0,1:T(8,128)} %param.14) | copy-start | bytes 98308
  37.8 2.7 %copy-start.13 = (s32[1024,8]{0,1:T(8,128)S(1)}, s32[1024,8]{0,1:T(8,128)}, u32[]{:S(2)}) copy-start(s32[1024,8]{0,1:T(8,128)} %param.15) | copy-start | bytes 98308
  39.1 9.8 %collective-permute-start.9 = (f32[128,1280]{1,0:T(8,128)S(1)}, f32[128,1280]{1,0:T(8,128)S(1)}, u32[]{:S(2)}, u32[]{:S(2)}) collective-permute-start(f32[128,1280]{1,0:T(8,128)S(1)} %bitcast_add_fusion.5), channel_id=1, source_target_pairs={{0,1},{1,2},{2,3},{3,0},{4,7},{5,4},{6,5},{7,6},{8,9},{9,10},{10,1... | collective-permute-start | bytes 1966088 | tf_op jit(solution)/shard_map/ppermute | solution.py:307
  43.8 20.5 %collective-permute-start.8 = (f32[320,1280]{1,0:T(8,128)S(1)}, f32[320,1280]{1,0:T(8,128)S(1)}, u32[]{:S(2)}, u32[]{:S(2)}) collective-permute-start(f32[320,1280]{1,0:T(8,128)S(1)} %slice.74), channel_id=1, source_target_pairs={{0,32},{1,33},{2,34},{3,35},{4,12},{5,13},{6,14},{7,15},{8,40},{9,... | collective-permute-start | bytes 4915208 | tf_op jit(solution)/shard_map/ppermute | solution.py:301
  45.5 10.4 %collective-permute-start.5 = (f32[128,1280]{1,0:T(8,128)S(1)}, f32[128,1280]{1,0:T(8,128)S(1)}, u32[]{:S(2)}, u32[]{:S(2)}) collective-permute-start(f32[128,1280]{1,0:T(8,128)S(1)} %bitcast_add_fusion.4), channel_id=1, source_target_pairs={{0,1},{1,2},{2,3},{3,0},{4,7},{5,4},{6,5},{7,6},{8,9},{9,10},{10,1... | collective-permute-start | bytes 1966088 | tf_op jit(solution)/shard_map/ppermute | solution.py:307
  48.9 19.4 %collective-permute-start.10 = (f32[128,1280]{1,0:T(8,128)S(1)}, f32[128,1280]{1,0:T(8,128)S(1)}, u32[]{:S(2)}, u32[]{:S(2)}) collective-permute-start(f32[128,1280]{1,0:T(8,128)S(1)} %bitcast_add_fusion.1), channel_id=1, source_target_pairs={{0,1},{1,2},{2,3},{3,0},{4,7},{5,4},{6,5},{7,6},{8,9},{9,10},{10,1... | collective-permute-start | bytes 1966088 | tf_op jit(solution)/shard_map/ppermute | solution.py:307
  56.0 15.7 %collective-permute-start.7 = (f32[128,1280]{1,0:T(8,128)S(1)}, f32[128,1280]{1,0:T(8,128)S(1)}, u32[]{:S(2)}, u32[]{:S(2)}) collective-permute-start(f32[128,1280]{1,0:T(8,128)S(1)} %bitcast_add_fusion.3), channel_id=1, source_target_pairs={{0,1},{1,2},{2,3},{3,0},{4,7},{5,4},{6,5},{7,6},{8,9},{9,10},{10,1... | collective-permute-start | bytes 1966088 | tf_op jit(solution)/shard_map/ppermute | solution.py:307
  64.6 13.7 %collective-permute-start.11 = (f32[160,1280]{1,0:T(8,128)S(1)}, f32[160,1280]{1,0:T(8,128)S(1)}, u32[]{:S(2)}, u32[]{:S(2)}) collective-permute-start(f32[160,1280]{1,0:T(8,128)S(1)} %slice.79), channel_id=1, source_target_pairs={{0,96},{1,97},{2,98},{3,99},{4,28},{5,29},{6,30},{7,31},{8,104},{9... | collective-permute-start | bytes 2457608 | tf_op jit(solution)/shard_map/ppermute | solution.py:301
  78.4 48.6 %all-to-all-start = ((f32[128,1,5248]{2,1,0:T(1,128)}), f32[128,1,5248]{2,1,0:T(1,128)S(1)}, u32[]{:S(2)}, u32[]{:S(2)}) async-start(f32[128,1,5248]{2,1,0:T(1,128)} %bitcast.13), calls=%async_computation | async-start | bytes 5373952 | tf_op jit(solution)/shard_map/all_to_all | solution.py:480
  90.1 39.9 %collective-permute-start.14 = (f32[40,1280]{1,0:T(8,128)}, f32[40,1280]{1,0:T(8,128)S(1)}, u32[]{:S(2)}, u32[]{:S(2)}) collective-permute-start(f32[40,1280]{1,0:T(8,128)} %get-tuple-element.88), channel_id=1, source_target_pairs={{0,16},{1,17},{2,18},{3,19},{4,68},{5,69},{6,70},{7,71},{8,24},{9,... | collective-permute-start | bytes 614408 | tf_op jit(solution)/shard_map/ppermute | solution.py:301
  93.0 37.0 %collective-permute-start.13 = (f32[40,1280]{1,0:T(8,128)}, f32[40,1280]{1,0:T(8,128)}, u32[]{:S(2)}, u32[]{:S(2)}) collective-permute-start(f32[40,1280]{1,0:T(8,128)} %get-tuple-element.89), channel_id=1, source_target_pairs={{0,8},{1,9},{2,10},{3,11},{4,36},{5,37},{6,38},{7,39},{8,0},{9,1},... | collective-permute-start | bytes 614408 | tf_op jit(solution)/shard_map/ppermute | solution.py:301
  93.3 33.7 %copy-start.10 = (f32[512,160]{0,1:T(8,128)S(1)}, f32[512,160]{0,1:T(8,128)}, u32[]{:S(2)}) copy-start(f32[512,160]{0,1:T(8,128)} %param.16) | copy-start | bytes 983044
  93.3 33.7 %copy-start.11 = (f32[512,160]{0,1:T(8,128)S(1)}, f32[512,160]{0,1:T(8,128)}, u32[]{:S(2)}) copy-start(f32[512,160]{0,1:T(8,128)} %param.17) | copy-start | bytes 983044
  93.3 36.7 %collective-permute-start.12 = (f32[40,1280]{1,0:T(8,128)}, f32[40,1280]{1,0:T(8,128)}, u32[]{:S(2)}, u32[]{:S(2)}) collective-permute-start(f32[40,1280]{1,0:T(8,128)} %get-tuple-element.90), channel_id=1, source_target_pairs={{0,24},{1,25},{2,26},{3,27},{4,100},{5,101},{6,102},{7,103},{8,16}... | collective-permute-start | bytes 614408 | tf_op jit(solution)/shard_map/ppermute | solution.py:301
  127.0 3.0 %copy-start.14 = (f32[40,1280]{1,0:T(8,128)S(1)}, f32[40,1280]{1,0:T(8,128)}, u32[]{:S(2)}) copy-start(f32[40,1280]{1,0:T(8,128)} %get-tuple-element.82) | copy-start | bytes 614404

commit v6 on v5

--- a/solution.py
+++ b/solution.py
@@ -212,7 +212,13 @@
     out_ref[pl.ds(CAP + GROUP, 128, stride=CHUNK), :] = sent_ref[...]
 
 
-def update_kernel(got_ref, table_ref, sums_ref, new_table_ref, new_sum_ref, values, select):
+def update_kernel(
+    got_ref, table_ref, sums_ref, b0, b1, b2, b3, new_table_ref, new_sum_ref, wk_grad, wv_grad, values, select
+):
+    width = wk_grad.shape[1]
+    total = (b0[...] + b1[...]) + (b2[...] + b3[...])
+    wk_grad[...] = total[:, :width]
+    wv_grad[...] = total[:, width:]
     owned = table_ref.shape[1]
     slots = got_ref[pl.ds(CAP + GROUP, 128, stride=CHUNK), :]
     ids = (lax.broadcasted_iota(jnp.int32, (128, owned), 1) + 1).astype(F32)
@@ -490,13 +496,16 @@
     ]
     received, hidden_grad = lax.optimization_barrier((received, hidden_grad))
     owned = mem_table.shape[0]
+    share = blocks.shape[1]
     table_spec = whole((EH, owned))
-    new_table, new_sum = pl.pallas_call(
+    new_table, new_sum, key_weight_grad, value_weight_grad = pl.pallas_call(
         update_kernel,
         grid=(1,),
-        in_specs=[whole((128 * CHUNK, 128)), table_spec, table_spec],
-        out_specs=[table_spec, table_spec],
-        out_shape=[jax.ShapeDtypeStruct((EH, owned), F32)] * 2,
+        in_specs=[whole((128 * CHUNK, 128)), table_spec, table_spec]
+        + [whole((share, 2 * width))] * 4,
+        out_specs=[table_spec, table_spec] + [whole((share, width))] * 2,
+        out_shape=[jax.ShapeDtypeStruct((EH, owned), F32)] * 2
+        + [jax.ShapeDtypeStruct((share, width), F32)] * 2,
         scratch_shapes=[
             pltpu.VMEM((2 * EH, CAP * 128), BF16),
             pltpu.VMEM((CAP * 128, owned), BF16),
@@ -504,12 +513,7 @@
         compiler_params=params(48),
         cost_estimate=cost(4 * EH * 4096 * 512, 5 << 20),
         name="update",
-    )(received, mem_table.T, adagrad_sum.T)
-    kept, new_table = lax.optimization_barrier((blocks[0], new_table))
-    sides = [slice(0, width), slice(width, 2 * width)]
-    key_weight_grad, value_weight_grad = (
-        (kept[:, at] + got[0][:, at]) + (got[1][:, at] + got[2][:, at]) for at in sides
-    )
+    )(received, mem_table.T, adagrad_sum.T, blocks[0], *got)
     return (hidden_grad, key_weight_grad, value_weight_grad, new_table.T, new_sum.T)
 
 

time: 132 us -> 132 us (level)
    add x1 -> x0, other arithmetic: 1.76 us -> none  [body(): kept[:, at] + got[0][:, at] + (got[1][:, at] + got[2][:, at])]
    unnamed x30 -> x28, local copies, waits for them, and re-layouts: 4.38 us -> 4.37 us
  transfers between devices with their start and end apart: 16 -> 16, of which waited for: 7 -> 7; matrix products, arithmetic and copies ran while one was open for 3% -> 3% of each run, Pallas kernels for 23% -> 21%
where the time goes in v6:
time: 132 us
  waiting for transfers between devices  43.1 us (33%)
  Pallas kernels  41.4 us (31%)
  starting transfers between devices  36.7 us (28%)
  local copies, waits for them, and re-layouts  6.6 us (5%)
  other arithmetic  3.24 us (2%)
    all_to_all x1, waiting for transfers between devices, body(): lax.all_to_all(packed.reshape(128, 1, CHUNK * 128), ('dp', 'tensor'), spl...  26.1 us
    ppermute x6, starting transfers between devices, swapped(): lax.ppermute(value, ('dp', 'tensor'), [(i, goal(i)) for i in range(128)])  11.3 us
    all_to_all x1, starting transfers between devices, body(): lax.all_to_all(packed.reshape(128, 1, CHUNK * 128), ('dp', 'tensor'), spl...  10.8 us
    ppermute x6, starting transfers between devices, turned(): lax.ppermute(value, ('dp', 'tensor'), [(i, goal(i)) for i in range(128)])  9.95 us
    pallas_call x1, Pallas kernels, body(): pl.pallas_call(forward_kernel, grid_spec=pltpu.PrefetchScalarGridSpec(num...  7.81 us
    ppermute x6, waiting for transfers between devices, swapped(): lax.ppermute(value, ('dp', 'tensor'), [(i, goal(i)) for i in range(128)])  7.67 us
    ppermute x6, waiting for transfers between devices, turned(): lax.ppermute(value, ('dp', 'tensor'), [(i, goal(i)) for i in range(128)])  6.28 us
    pallas_call x1, Pallas kernels, body(): pl.pallas_call(hidden_grad_kernel, grid=(4,), in_specs=[total_spec] * 4 +...  5.84 us
  transfers between devices with their start and end apart: 16, of which 7 were waited for; matrix products, arithmetic and copies ran while one was open for 3% of the time, Pallas kernels for 21%

profile of v6, /device:TPU:1, one launch (start us, length us, event | category | flops | bytes accessed | tf_op | source)
XLA Modules:
  0.0 131.9 jit_solution(2994277795534718741)
XLA Ops:
  0.7 0.0 copy-start.1
  0.7 7.8 %forward.1 = (f32[2,1024]{1,0:T(2,128)S(1)}, bf16[256,1280]{1,0:T(8,128)(2,1)S(1)}) custom-call(s32[1]{0:T(128)} %bitcast.at_ref, bf16[1024,1280]{1,0:T(8,128)(2,1)} %memory_ref.5, bf16[1024,640]{1,0:T(8,128)(2,1)} %hidden_ref.3, bf16[1024,640]{1,0:T(8,128)(2,1)} %grad_ref.3, bf16[1280,640]{1,0:T(8,128)(2,1)} %wk_ref.7, bf16[1280,640]{1,0:T(8,128)(2,1)} %wv_ref.5), custom_call_target="tpu_custom_call" | custom-call | flops 3355443200 | bytes 12582912 | tf_op jit(solution)/shard_map/forward/pallas_call | solution.py:272
  8.5 0.0 copy-start.5
  8.5 3.6 %collective-permute-start.2 = (f32[2,1024]{1,0:T(2,128)S(1)}, f32[2,1024]{1,0:T(2,128)S(1)}, u32[]{:S(2)}, u32[]{:S(2)}) collective-permute-start(f32[2,1024]{1,0:T(2,128)S(1)} %get-tuple-element.74.p0), channel_id=1, source_target_pairs={{0,3},{1,0},{2,1},{3,2},{4,7},{5,4},{6,5},{7,6},{8,11},{9,8},{10,9... | collective-permute-start | bytes 24584 | tf_op jit(solution)/shard_map/ppermute | solution.py:298
  12.1 0.3 collective-permute-start.1
  12.5 0.7 collective-permute-start
  13.2 0.0 collective-permute-done.2.p3
  13.2 3.0 %collective-permute-done.1.p2 = f32[2,1024]{1,0:T(2,128)S(1)} collective-permute-done((f32[2,1024]{1,0:T(2,128)S(1)}, f32[2,1024]{1,0:T(2,128)S(1)}, u32[]{:S(2)}, u32[]{:S(2)}) %collective-permute-start.1) | collective-permute-done | bytes 8224 | tf_op jit(solution)/shard_map/ppermute | solution.py:298
  16.1 0.1 collective-permute-done.p1
  16.2 2.2 %first.1 = (f32[128,1280]{1,0:T(8,128)}, f32[128,1280]{1,0:T(8,128)S(1)}) custom-call(s32[1]{0:T(128)} %bitcast.at_ref, f32[2,1024]{1,0:T(2,128)S(1)} %get-tuple-element.74.p0, f32[2,1024]{1,0:T(2,128)S(1)} %collective-permute-done.p1, f32[2,1024]{1,0:T(2,128)S(1)} %collective-permute-done.1.p2, f32[2,1024]{1,0:T(2,128)S(1)} %collective-permute-done.2.p3, ...), custom_call_target="tpu_custom_call" | custom-call | flops 838860800 | bytes 6291456 | tf_op jit(solution)/shard_map/first/pallas_call | solution.py:323
  18.5 0.8 copy-done.9
  19.3 0.6 collective-permute-start.3
  19.9 1.4 %collective-permute-start.4 = (f32[128,1280]{1,0:T(8,128)}, f32[128,1280]{1,0:T(8,128)S(1)}, u32[]{:S(2)}, u32[]{:S(2)}) collective-permute-start(f32[128,1280]{1,0:T(8,128)} %copy-done.9), channel_id=1, source_target_pairs={{0,1},{1,2},{2,3},{3,0},{4,7},{5,4},{6,5},{7,6},{8,9},{9,10},{10,1... | collective-permute-start | bytes 1966088 | tf_op jit(solution)/shard_map/ppermute | solution.py:313
  21.3 0.1 pad_add_fusion.1.at_ref
  21.4 0.0 copy-start.3
  21.4 1.3 copy-done.3
  22.7 1.3 copy-done.4
  24.0 0.8 gate.1.both_ref
  24.8 0.1 pad_add_fusion.at_ref
  24.9 0.8 copy-done.2
  25.7 5.3 %weight_grad.1 = (f32[640,1280]{1,0:T(8,128)S(1)}, f32[640,1280]{1,0:T(8,128)S(1)}) custom-call(s32[3]{0:T(128)S(1)} %pad_add_fusion.1.at_ref, bf16[1024,1280]{1,0:T(8,128)(2,1)S(1)} %copy-done.2, bf16[1024,1280]{1,0:T(8,128)(2,1)S(1)} %gate.1.both_ref), custom_call_target="tpu_custom_call" | custom-call | flops 1 | bytes 1 | tf_op jit(solution)/shard_map/weight_grad/pallas_call | solution.py:357
  31.0 2.1 %collective-permute-start.6 = (f32[640,1280]{1,0:T(8,128)S(1)}, f32[640,1280]{1,0:T(8,128)S(1)}, u32[]{:S(2)}, u32[]{:S(2)}) collective-permute-start(f32[640,1280]{1,0:T(8,128)S(1)} %get-tuple-element.53), channel_id=1, source_target_pairs={{0,4},{1,5},{2,6},{3,7},{4,0},{5,1},{6,2},{7,3},{8,12},{9,13},{10,... | collective-permute-start | bytes 9830408 | tf_op jit(solution)/shard_map/ppermute | solution.py:307
  33.2 4.6 %rest.1 = (f32[3,128,1280]{2,1,0:T(8,128)S(1)}, f32[3,128,1280]{2,1,0:T(8,128)S(1)}) custom-call(s32[2]{0:T(128)S(1)} %pad_add_fusion.at_ref, bf16[1024,1280]{1,0:T(8,128)(2,1)S(1)} %gate.1.both_ref, bf16[1280,640]{1,0:T(8,128)(2,1)S(1)} %copy-done.1, bf16[1280,640]{1,0:T(8,128)(2,1)S(1)} %copy-done), custom_call_target="tpu_custom_call" | custom-call | flops 1 | bytes 1 | tf_op jit(solution)/shard_map/rest/pallas_call | solution.py:374
  37.7 0.0 collective-permute-done.3
  37.7 0.0 copy-start.12
  37.8 0.0 copy-start.13
  37.8 1.2 bitcast_add_fusion.5
  38.9 0.0 collective-permute-done.4
  39.0 0.1 bitcast_add_fusion.4
  39.0 1.4 %collective-permute-start.9 = (f32[128,1280]{1,0:T(8,128)S(1)}, f32[128,1280]{1,0:T(8,128)S(1)}, u32[]{:S(2)}, u32[]{:S(2)}) collective-permute-start(f32[128,1280]{1,0:T(8,128)S(1)} %bitcast_add_fusion.5), channel_id=1, source_target_pairs={{0,1},{1,2},{2,3},{3,0},{4,7},{5,4},{6,5},{7,6},{8,9},{9,10},{10,1... | collective-permute-start | bytes 1966088 | tf_op jit(solution)/shard_map/ppermute | solution.py:313
  40.5 2.7 %ranks.1 = (bf16[1024,2048]{1,0:T(8,128)(2,1)S(1)}, f32[2048,128]{1,0:T(8,128)S(1)}, f32[128,128]{1,0:T(8,128)S(1)}) custom-call(s32[2]{0:T(128)S(1)} %pad_add_fusion.at_ref, s32[8,1024]{1,0:T(8,128)S(1)} %bitcast.28, s32[8,1024]{1,0:T(8,128)S(1)} %bitcast.29), custom_call_target="tpu_custom_call" | custom-call | flops 68719476736 | bytes 134217728 | tf_op jit(solution)/shard_map/ranks/pallas_call | solution.py:408
  43.2 0.0 collective-permute-done.6
  43.2 0.4 add.38
  43.6 0.1 slice.50
  43.7 1.7 %collective-permute-start.8 = (f32[320,1280]{1,0:T(8,128)S(1)}, f32[320,1280]{1,0:T(8,128)S(1)}, u32[]{:S(2)}, u32[]{:S(2)}) collective-permute-start(f32[320,1280]{1,0:T(8,128)S(1)} %slice.50), channel_id=1, source_target_pairs={{0,32},{1,33},{2,34},{3,35},{4,12},{5,13},{6,14},{7,15},{8,40},{9,... | collective-permute-start | bytes 4915208 | tf_op jit(solution)/shard_map/ppermute | solution.py:307
  45.5 1.7 %collective-permute-start.5 = (f32[128,1280]{1,0:T(8,128)S(1)}, f32[128,1280]{1,0:T(8,128)S(1)}, u32[]{:S(2)}, u32[]{:S(2)}) collective-permute-start(f32[128,1280]{1,0:T(8,128)S(1)} %bitcast_add_fusion.4), channel_id=1, source_target_pairs={{0,1},{1,2},{2,3},{3,0},{4,7},{5,4},{6,5},{7,6},{8,9},{9,10},{10,1... | collective-permute-start | bytes 1966088 | tf_op jit(solution)/shard_map/ppermute | solution.py:313
  47.2 1.7 %collective-permute-done.9 = f32[128,1280]{1,0:T(8,128)S(1)} collective-permute-done((f32[128,1280]{1,0:T(8,128)S(1)}, f32[128,1280]{1,0:T(8,128)S(1)}, u32[]{:S(2)}, u32[]{:S(2)}) %collective-permute-start.9) | collective-permute-done | bytes 655392 | tf_op jit(solution)/shard_map/ppermute | solution.py:313
  48.8 0.1 bitcast_add_fusion.1
  48.9 2.3 %collective-permute-start.10 = (f32[128,1280]{1,0:T(8,128)S(1)}, f32[128,1280]{1,0:T(8,128)S(1)}, u32[]{:S(2)}, u32[]{:S(2)}) collective-permute-start(f32[128,1280]{1,0:T(8,128)S(1)} %bitcast_add_fusion.1), channel_id=1, source_target_pairs={{0,1},{1,2},{2,3},{3,0},{4,7},{5,4},{6,5},{7,6},{8,9},{9,10},{10,1... | collective-permute-start | bytes 1966088 | tf_op jit(solution)/shard_map/ppermute | solution.py:313
  51.3 4.6 %collective-permute-done.5 = f32[128,1280]{1,0:T(8,128)S(1)} collective-permute-done((f32[128,1280]{1,0:T(8,128)S(1)}, f32[128,1280]{1,0:T(8,128)S(1)}, u32[]{:S(2)}, u32[]{:S(2)}) %collective-permute-start.5) | collective-permute-done | bytes 655392 | tf_op jit(solution)/shard_map/ppermute | solution.py:313
  55.9 0.1 bitcast_add_fusion.3
  55.9 2.5 %collective-permute-start.7 = (f32[128,1280]{1,0:T(8,128)S(1)}, f32[128,1280]{1,0:T(8,128)S(1)}, u32[]{:S(2)}, u32[]{:S(2)}) collective-permute-start(f32[128,1280]{1,0:T(8,128)S(1)} %bitcast_add_fusion.3), channel_id=1, source_target_pairs={{0,1},{1,2},{2,3},{3,0},{4,7},{5,4},{6,5},{7,6},{8,9},{9,10},{10,1... | collective-permute-start | bytes 1966088 | tf_op jit(solution)/shard_map/ppermute | solution.py:313
  58.5 5.8 %collective-permute-done.8 = f32[320,1280]{1,0:T(8,128)S(1)} collective-permute-done((f32[320,1280]{1,0:T(8,128)S(1)}, f32[320,1280]{1,0:T(8,128)S(1)}, u32[]{:S(2)}, u32[]{:S(2)}) %collective-permute-start.8) | collective-permute-done | bytes 1638432 | tf_op jit(solution)/shard_map/ppermute | solution.py:307
  64.3 0.2 slice_add_fusion
  64.4 0.1 slice.55
  64.5 3.6 %collective-permute-start.11 = (f32[160,1280]{1,0:T(8,128)S(1)}, f32[160,1280]{1,0:T(8,128)S(1)}, u32[]{:S(2)}, u32[]{:S(2)}) collective-permute-start(f32[160,1280]{1,0:T(8,128)S(1)} %slice.55), channel_id=1, source_target_pairs={{0,96},{1,97},{2,98},{3,99},{4,28},{5,29},{6,30},{7,31},{8,104},{9... | collective-permute-start | bytes 2457608 | tf_op jit(solution)/shard_map/ppermute | solution.py:307
  68.1 0.0 collective-permute-done.10
  68.1 0.1 bitcast_add_fusion.sum_ref
  68.2 3.3 %pack_top.1.part_ref = f32[5,1024,128]{2,1,0:T(8,128)S(1)} custom-call(f32[128,1280]{1,0:T(8,128)S(1)} %bitcast_add_fusion.sum_ref, bf16[1024,2048]{1,0:T(8,128)(2,1)S(1)} %get-tuple-element.67.select_ref, f32[2048,128]{1,0:T(8,128)S(1)} %get-tuple-element.68.group_ref), custom_call_target="tpu_custom_call" | custom-call | flops 2684354560 | bytes 8388608 | tf_op jit(solution)/shard_map/pack_top/pallas_call | solution.py:449
  71.5 0.0 collective-permute-done.7
  71.5 0.1 bitcast_add_fusion.2.sum_ref
  71.6 4.7 %pack_low.1 = f32[5248,128]{1,0:T(8,128)} custom-call(f32[128,1280]{1,0:T(8,128)S(1)} %bitcast_add_fusion.2.sum_ref, bf16[1024,2048]{1,0:T(8,128)(2,1)S(1)} %get-tuple-element.67.select_ref, f32[2048,128]{1,0:T(8,128)S(1)} %get-tuple-element.68.group_ref, f32[5,1024,128]{2,1,0:T(8,128)S(1)} %pack_top.1.part_ref, f32[128,128]{1,0:T(8,128)S(1)} %get-tuple-element.71.sent_ref), custom_call_target="tpu_custom_call" | custom-call | flops 2684354560 | bytes 12582912 | tf_op jit(solution)/shard_map/pack_low/pallas_call | solution.py:460
  76.3 1.9 %collective-permute-done.11 = f32[160,1280]{1,0:T(8,128)S(1)} collective-permute-done((f32[160,1280]{1,0:T(8,128)S(1)}, f32[160,1280]{1,0:T(8,128)S(1)}, u32[]{:S(2)}, u32[]{:S(2)}) %collective-permute-start.11) | collective-permute-done | bytes 819232 | tf_op jit(solution)/shard_map/ppermute | solution.py:307
  78.2 1.0 slice_add_fusion.1
  79.1 10.8 %all-to-all-start = ((f32[128,1,5248]{2,1,0:T(1,128)}), f32[128,1,5248]{2,1,0:T(1,128)S(1)}, u32[]{:S(2)}, u32[]{:S(2)}) async-start(f32[128,1,5248]{2,1,0:T(1,128)} %bitcast.13), calls=%async_computation | async-start | bytes 5373952 | tf_op jit(solution)/shard_map/all_to_all | solution.py:486
  89.9 2.1 %fusion = (f32[40,1280]{1,0:T(8,128)}, f32[40,1280]{1,0:T(8,128)}, f32[40,1280]{1,0:T(8,128)}, f32[40,1280]{1,0:T(8,128)S(1)}) fusion(f32[160,1280]{1,0:T(8,128)} %slice_add_fusion.1), kind=kLoop, calls=%fused_computation.10 | loop fusion | bytes 1638400 | tf_op jit(solution)/shard_map/slice | solution.py:495
  92.0 2.9 %collective-permute-start.14 = (f32[40,1280]{1,0:T(8,128)}, f32[40,1280]{1,0:T(8,128)}, u32[]{:S(2)}, u32[]{:S(2)}) collective-permute-start(f32[40,1280]{1,0:T(8,128)} %get-tuple-element.85), channel_id=1, source_target_pairs={{0,16},{1,17},{2,18},{3,19},{4,68},{5,69},{6,70},{7,71},{8,24},{9,... | collective-permute-start | bytes 614408 | tf_op jit(solution)/shard_map/ppermute | solution.py:307
  94.9 0.3 collective-permute-start.13
  95.2 0.6 collective-permute-start.12
  95.8 5.8 %hidden_grad.1 = bf16[1024,640]{1,0:T(8,128)(2,1)} custom-call(f32[2,1024]{1,0:T(2,128)} %copy-done.5, f32[2,1024]{1,0:T(2,128)} %copy-done.8, f32[2,1024]{1,0:T(2,128)} %copy-done.7, f32[2,1024]{1,0:T(2,128)} %copy-done.6, bf16[1024,1280]{1,0:T(8,128)(2,1)} %memory_ref.5, bf16[1280,640]{1,0:T(8,128)(2,1)} %wk_ref.7), custom_call_target="tpu_custom_call" | custom-call | flops 1677721600 | bytes 6291456 | tf_op jit(solution)/shard_map/hidden_grad/pallas_call | solution.py:476
  101.6 26.1 %all-to-all-done = f32[128,1,5248]{2,1,0:T(1,128)S(1)} async-done(((f32[128,1,5248]{2,1,0:T(1,128)}), f32[128,1,5248]{2,1,0:T(1,128)S(1)}, u32[]{:S(2)}, u32[]{:S(2)}) %all-to-all-start) | async-done | bytes 2687008 | tf_op jit(solution)/shard_map/all_to_all | solution.py:486
  127.7 0.0 collective-permute-done.14.b3
  127.7 0.0 collective-permute-done.13.b2
  127.8 4.2 %update.1 = (f32[160,512]{1,0:T(8,128)}, f32[160,512]{1,0:T(8,128)}, f32[40,640]{1,0:T(8,128)}, f32[40,640]{1,0:T(8,128)}) custom-call(f32[5248,128]{1,0:T(8,128)S(1)} %bitcast.25, f32[160,512]{1,0:T(8,128)S(1)} %bitcast.26, f32[160,512]{1,0:T(8,128)S(1)} %bitcast.27, f32[40,1280]{1,0:T(8,128)S(1)} %get-tuple-element.88.b0, ...), custom_call_target="tpu_custom_call" | custom-call | flops 1342177280 | bytes 5242880 | tf_op jit(solution)/shard_map/update/pallas_call | solution.py:501
  (20 shorter events, 0.0 us)
Async XLA Ops:
  0.6 15.6 %copy-start = (bf16[1280,640]{1,0:T(8,128)(2,1)S(1)}, bf16[1280,640]{1,0:T(8,128)(2,1)}, u32[]{:S(2)}) copy-start(bf16[1280,640]{1,0:T(8,128)(2,1)} %wv_ref.5) | copy-start | bytes 4915204
  0.7 15.6 %copy-start.1 = (bf16[1280,640]{1,0:T(8,128)(2,1)S(1)}, bf16[1280,640]{1,0:T(8,128)(2,1)}, u32[]{:S(2)}) copy-start(bf16[1280,640]{1,0:T(8,128)(2,1)} %wk_ref.7) | copy-start | bytes 4915204
  8.5 12.9 %copy-start.5 = (f32[2,1024]{1,0:T(2,128)}, f32[2,1024]{1,0:T(2,128)S(1)}, u32[]{:S(2)}) copy-start(f32[2,1024]{1,0:T(2,128)S(1)} %get-tuple-element.74.p0) | copy-start | bytes 24580
  8.5 4.7 %collective-permute-start.2 = (f32[2,1024]{1,0:T(2,128)S(1)}, f32[2,1024]{1,0:T(2,128)S(1)}, u32[]{:S(2)}, u32[]{:S(2)}) collective-permute-start(f32[2,1024]{1,0:T(2,128)S(1)} %get-tuple-element.74.p0), channel_id=1, source_target_pairs={{0,3},{1,0},{2,1},{3,2},{4,7},{5,4},{6,5},{7,6},{8,11},{9,8},{10,9... | collective-permute-start | bytes 24584 | tf_op jit(solution)/shard_map/ppermute | solution.py:298
  12.1 4.0 %collective-permute-start.1 = (f32[2,1024]{1,0:T(2,128)S(1)}, f32[2,1024]{1,0:T(2,128)S(1)}, u32[]{:S(2)}, u32[]{:S(2)}) collective-permute-start(f32[2,1024]{1,0:T(2,128)S(1)} %get-tuple-element.74.p0), channel_id=1, source_target_pairs={{0,2},{1,3},{2,0},{3,1},{4,6},{5,7},{6,4},{7,5},{8,10},{9,11},{10,... | collective-permute-start | bytes 24584 | tf_op jit(solution)/shard_map/ppermute | solution.py:298
  12.5 3.7 %collective-permute-start = (f32[2,1024]{1,0:T(2,128)S(1)}, f32[2,1024]{1,0:T(2,128)S(1)}, u32[]{:S(2)}, u32[]{:S(2)}) collective-permute-start(f32[2,1024]{1,0:T(2,128)S(1)} %get-tuple-element.74.p0), channel_id=1, source_target_pairs={{0,1},{1,2},{2,3},{3,0},{4,5},{5,6},{6,7},{7,4},{8,9},{9,10},{10,1... | collective-permute-start | bytes 24584 | tf_op jit(solution)/shard_map/ppermute | solution.py:298
  13.2 8.2 %copy-start.6 = (f32[2,1024]{1,0:T(2,128)}, f32[2,1024]{1,0:T(2,128)S(1)}, u32[]{:S(2)}) copy-start(f32[2,1024]{1,0:T(2,128)S(1)} %collective-permute-done.2.p3) | copy-start | bytes 24580
  16.1 5.2 %copy-start.7 = (f32[2,1024]{1,0:T(2,128)}, f32[2,1024]{1,0:T(2,128)S(1)}, u32[]{:S(2)}) copy-start(f32[2,1024]{1,0:T(2,128)S(1)} %collective-permute-done.1.p2) | copy-start | bytes 24580
  16.2 5.1 %copy-start.8 = (f32[2,1024]{1,0:T(2,128)}, f32[2,1024]{1,0:T(2,128)S(1)}, u32[]{:S(2)}) copy-start(f32[2,1024]{1,0:T(2,128)S(1)} %collective-permute-done.p1) | copy-start | bytes 24580
  18.5 0.8 copy-start.9
  19.3 18.4 %collective-permute-start.3 = (f32[128,1280]{1,0:T(8,128)}, f32[128,1280]{1,0:T(8,128)}, u32[]{:S(2)}, u32[]{:S(2)}) collective-permute-start(f32[128,1280]{1,0:T(8,128)} %get-tuple-element.47), channel_id=1, source_target_pairs={{0,1},{1,2},{2,3},{3,0},{4,7},{5,4},{6,5},{7,6},{8,9},{9,10},{10,1... | collective-permute-start | bytes 1966088 | tf_op jit(solution)/shard_map/ppermute | solution.py:313
  19.9 19.1 %collective-permute-start.4 = (f32[128,1280]{1,0:T(8,128)}, f32[128,1280]{1,0:T(8,128)S(1)}, u32[]{:S(2)}, u32[]{:S(2)}) collective-permute-start(f32[128,1280]{1,0:T(8,128)} %copy-done.9), channel_id=1, source_target_pairs={{0,1},{1,2},{2,3},{3,0},{4,7},{5,4},{6,5},{7,6},{8,9},{9,10},{10,1... | collective-permute-start | bytes 1966088 | tf_op jit(solution)/shard_map/ppermute | solution.py:313
  21.4 1.3 %copy-start.3 = (bf16[1024,640]{1,0:T(8,128)(2,1)S(1)}, bf16[1024,640]{1,0:T(8,128)(2,1)}, u32[]{:S(2)}) copy-start(bf16[1024,640]{1,0:T(8,128)(2,1)} %hidden_ref.3) | copy-start | bytes 3932164
  22.7 1.3 copy-start.4
  24.0 1.7 %copy-start.2 = (bf16[1024,1280]{1,0:T(8,128)(2,1)S(1)}, bf16[1024,1280]{1,0:T(8,128)(2,1)}, u32[]{:S(2)}) copy-start(bf16[1024,1280]{1,0:T(8,128)(2,1)} %memory_ref.5) | copy-start | bytes 7864324
  31.0 12.2 %collective-permute-start.6 = (f32[640,1280]{1,0:T(8,128)S(1)}, f32[640,1280]{1,0:T(8,128)S(1)}, u32[]{:S(2)}, u32[]{:S(2)}) collective-permute-start(f32[640,1280]{1,0:T(8,128)S(1)} %get-tuple-element.53), channel_id=1, source_target_pairs={{0,4},{1,5},{2,6},{3,7},{4,0},{5,1},{6,2},{7,3},{8,12},{9,13},{10,... | collective-permute-start | bytes 9830408 | tf_op jit(solution)/shard_map/ppermute | solution.py:307
  37.7 2.7 %copy-start.12 = (s32[1024,8]{0,1:T(8,128)S(1)}, s32[1024,8]{0,1:T(8,128)}, u32[]{:S(2)}) copy-start(s32[1024,8]{0,1:T(8,128)} %param.14) | copy-start | bytes 98308
  37.8 2.7 %copy-start.13 = (s32[1024,8]{0,1:T(8,128)S(1)}, s32[1024,8]{0,1:T(8,128)}, u32[]{:S(2)}) copy-start(s32[1024,8]{0,1:T(8,128)} %param.15) | copy-start | bytes 98308
  39.0 9.8 %collective-permute-start.9 = (f32[128,1280]{1,0:T(8,128)S(1)}, f32[128,1280]{1,0:T(8,128)S(1)}, u32[]{:S(2)}, u32[]{:S(2)}) collective-permute-start(f32[128,1280]{1,0:T(8,128)S(1)} %bitcast_add_fusion.5), channel_id=1, source_target_pairs={{0,1},{1,2},{2,3},{3,0},{4,7},{5,4},{6,5},{7,6},{8,9},{9,10},{10,1... | collective-permute-start | bytes 1966088 | tf_op jit(solution)/shard_map/ppermute | solution.py:313
  43.7 20.5 %collective-permute-start.8 = (f32[320,1280]{1,0:T(8,128)S(1)}, f32[320,1280]{1,0:T(8,128)S(1)}, u32[]{:S(2)}, u32[]{:S(2)}) collective-permute-start(f32[320,1280]{1,0:T(8,128)S(1)} %slice.50), channel_id=1, source_target_pairs={{0,32},{1,33},{2,34},{3,35},{4,12},{5,13},{6,14},{7,15},{8,40},{9,... | collective-permute-start | bytes 4915208 | tf_op jit(solution)/shard_map/ppermute | solution.py:307
  45.5 10.4 %collective-permute-start.5 = (f32[128,1280]{1,0:T(8,128)S(1)}, f32[128,1280]{1,0:T(8,128)S(1)}, u32[]{:S(2)}, u32[]{:S(2)}) collective-permute-start(f32[128,1280]{1,0:T(8,128)S(1)} %bitcast_add_fusion.4), channel_id=1, source_target_pairs={{0,1},{1,2},{2,3},{3,0},{4,7},{5,4},{6,5},{7,6},{8,9},{9,10},{10,1... | collective-permute-start | bytes 1966088 | tf_op jit(solution)/shard_map/ppermute | solution.py:313
  48.9 19.2 %collective-permute-start.10 = (f32[128,1280]{1,0:T(8,128)S(1)}, f32[128,1280]{1,0:T(8,128)S(1)}, u32[]{:S(2)}, u32[]{:S(2)}) collective-permute-start(f32[128,1280]{1,0:T(8,128)S(1)} %bitcast_add_fusion.1), channel_id=1, source_target_pairs={{0,1},{1,2},{2,3},{3,0},{4,7},{5,4},{6,5},{7,6},{8,9},{9,10},{10,1... | collective-permute-start | bytes 1966088 | tf_op jit(solution)/shard_map/ppermute | solution.py:313
  55.9 15.6 %collective-permute-start.7 = (f32[128,1280]{1,0:T(8,128)S(1)}, f32[128,1280]{1,0:T(8,128)S(1)}, u32[]{:S(2)}, u32[]{:S(2)}) collective-permute-start(f32[128,1280]{1,0:T(8,128)S(1)} %bitcast_add_fusion.3), channel_id=1, source_target_pairs={{0,1},{1,2},{2,3},{3,0},{4,7},{5,4},{6,5},{7,6},{8,9},{9,10},{10,1... | collective-permute-start | bytes 1966088 | tf_op jit(solution)/shard_map/ppermute | solution.py:313
  64.5 13.7 %collective-permute-start.11 = (f32[160,1280]{1,0:T(8,128)S(1)}, f32[160,1280]{1,0:T(8,128)S(1)}, u32[]{:S(2)}, u32[]{:S(2)}) collective-permute-start(f32[160,1280]{1,0:T(8,128)S(1)} %slice.55), channel_id=1, source_target_pairs={{0,96},{1,97},{2,98},{3,99},{4,28},{5,29},{6,30},{7,31},{8,104},{9... | collective-permute-start | bytes 2457608 | tf_op jit(solution)/shard_map/ppermute | solution.py:307
  79.1 48.6 %all-to-all-start = ((f32[128,1,5248]{2,1,0:T(1,128)}), f32[128,1,5248]{2,1,0:T(1,128)S(1)}, u32[]{:S(2)}, u32[]{:S(2)}) async-start(f32[128,1,5248]{2,1,0:T(1,128)} %bitcast.13), calls=%async_computation | async-start | bytes 5373952 | tf_op jit(solution)/shard_map/all_to_all | solution.py:486
  92.0 35.7 %collective-permute-start.14 = (f32[40,1280]{1,0:T(8,128)}, f32[40,1280]{1,0:T(8,128)}, u32[]{:S(2)}, u32[]{:S(2)}) collective-permute-start(f32[40,1280]{1,0:T(8,128)} %get-tuple-element.85), channel_id=1, source_target_pairs={{0,16},{1,17},{2,18},{3,19},{4,68},{5,69},{6,70},{7,71},{8,24},{9,... | collective-permute-start | bytes 614408 | tf_op jit(solution)/shard_map/ppermute | solution.py:307
  94.9 32.8 %collective-permute-start.13 = (f32[40,1280]{1,0:T(8,128)}, f32[40,1280]{1,0:T(8,128)}, u32[]{:S(2)}, u32[]{:S(2)}) collective-permute-start(f32[40,1280]{1,0:T(8,128)} %get-tuple-element.86), channel_id=1, source_target_pairs={{0,8},{1,9},{2,10},{3,11},{4,36},{5,37},{6,38},{7,39},{8,0},{9,1},... | collective-permute-start | bytes 614408 | tf_op jit(solution)/shard_map/ppermute | solution.py:307
  95.2 32.6 %copy-start.10 = (f32[512,160]{0,1:T(8,128)S(1)}, f32[512,160]{0,1:T(8,128)}, u32[]{:S(2)}) copy-start(f32[512,160]{0,1:T(8,128)} %param.16) | copy-start | bytes 983044
  95.2 32.6 %copy-start.11 = (f32[512,160]{0,1:T(8,128)S(1)}, f32[512,160]{0,1:T(8,128)}, u32[]{:S(2)}) copy-start(f32[512,160]{0,1:T(8,128)} %param.17) | copy-start | bytes 983044
  95.2 32.6 %collective-permute-start.12 = (f32[40,1280]{1,0:T(8,128)}, f32[40,1280]{1,0:T(8,128)}, u32[]{:S(2)}, u32[]{:S(2)}) collective-permute-start(f32[40,1280]{1,0:T(8,128)} %get-tuple-element.87), channel_id=1, source_target_pairs={{0,24},{1,25},{2,26},{3,27},{4,100},{5,101},{6,102},{7,103},{8,16}... | collective-permute-start | bytes 614408 | tf_op jit(solution)/shard_map/ppermute | solution.py:307

commit v7 on v6

--- a/solution.py
+++ b/solution.py
@@ -124,13 +124,13 @@
         at += out_ref.shape[0]
 
 
-def first_kernel(at_ref, p0, p1, p2, p3, first_ref, wk_ref, wv_ref, top_ref, low_ref):
+def first_kernel(at_ref, p0, p1, p2, p3, first_ref, wk_ref, wv_ref, out_ref):
     count, width = first_ref.shape[0], first_ref.shape[1] // 2
     tile = pl.ds(pl.multiple_of(at_ref[0] * count, count), count)
     gates, scores = gate_columns(summed_parts((p0, p1, p2, p3), tile), width)
     key_grad = (scores * first_ref[:, :width].astype(F32)).astype(BF16)
     value_grad = (gates * first_ref[:, width:].astype(F32)).astype(BF16)
-    memory_grad_tile(key_grad, value_grad, wk_ref, wv_ref, top_ref, low_ref)
+    memory_grad_tile(key_grad, value_grad, wk_ref, wv_ref, out_ref)
 
 
 def gate_kernel(p0, p1, p2, p3, hidden_ref, grad_ref, both_ref):
@@ -320,23 +320,20 @@
     top = 128
     low = quarter - top
 
-    first_top, first_low = pl.pallas_call(
+    first = pl.pallas_call(
         first_kernel,
         grid_spec=pltpu.PrefetchScalarGridSpec(
             num_scalar_prefetch=1,
             grid=(1,),
             in_specs=[part_whole] * 4 + [chunk] + weights,
-            out_specs=[whole((top, depth)), whole((low, depth))],
-        ),
-        out_shape=[
-            jax.ShapeDtypeStruct((top, depth), F32),
-            jax.ShapeDtypeStruct((low, depth), F32),
-        ],
+            out_specs=whole((quarter, depth)),
+        ),
+        out_shape=jax.ShapeDtypeStruct((quarter, depth), F32),
         compiler_params=params(20),
         cost_estimate=cost(4 * quarter * depth * width, 6 << 20),
         name="first",
     )(start, *parts, first_both, w_key, w_value)
-    parts, _ = lax.optimization_barrier((parts, first_low))
+    parts, _ = lax.optimization_barrier((parts, first))
 
     def by_rows(cols):
         return pl.BlockSpec((quarter, cols), lambda i: (i, 0))
@@ -398,8 +395,8 @@
         half = value.shape[0] // 2
         return value[:half] + swapped(value[half:], bits)
 
-    moved_top = turned(first_top) + rest_top[0]
-    moved_low = turned(first_low) + rest_low[0]
+    moved_top = turned(first[:top]) + rest_top[0]
+    moved_low = turned(first[top:]) + rest_low[0]
     moved_top, moved_low, owners, slots = lax.optimization_barrier(
         (moved_top, moved_low, row_owner.T, row_slot.T)
     )

time: 132 us -> 132 us (level)
    unnamed x28 -> x26, local copies, waits for them, and re-layouts: 4.37 us -> 3.53 us
where the time goes in v7:
time: 132 us; the launch traced here: 131 us
  waiting for transfers between devices  43.1 us (33%)
  Pallas kernels  40.6 us (31%)
  starting transfers between devices  36.6 us (28%)
  local copies, waits for them, and re-layouts  6.91 us (5%)
  other arithmetic  3.24 us (2%)
    all_to_all x1, waiting for transfers between devices, body(): lax.all_to_all(packed.reshape(128, 1, CHUNK * 128), ('dp', 'tensor'), spl...  26.1 us
    ppermute x6, starting transfers between devices, swapped(): lax.ppermute(value, ('dp', 'tensor'), [(i, goal(i)) for i in range(128)])  11.3 us
    all_to_all x1, starting transfers between devices, body(): lax.all_to_all(packed.reshape(128, 1, CHUNK * 128), ('dp', 'tensor'), spl...  10.8 us
    ppermute x6, starting transfers between devices, turned(): lax.ppermute(value, ('dp', 'tensor'), [(i, goal(i)) for i in range(128)])  9.87 us
    pallas_call x1, Pallas kernels, body(): pl.pallas_call(forward_kernel, grid_spec=pltpu.PrefetchScalarGridSpec(num...  7.81 us
    ppermute x6, waiting for transfers between devices, swapped(): lax.ppermute(value, ('dp', 'tensor'), [(i, goal(i)) for i in range(128)])  7.68 us
    ppermute x6, waiting for transfers between devices, turned(): lax.ppermute(value, ('dp', 'tensor'), [(i, goal(i)) for i in range(128)])  6.33 us
    pallas_call x1, Pallas kernels, body(): pl.pallas_call(hidden_grad_kernel, grid=(4,), in_specs=[total_spec] * 4 +...  5.84 us
  transfers between devices with their start and end apart: 16, of which 7 were waited for; matrix products, arithmetic and copies ran while one was open for 3% of the time, Pallas kernels for 21%

profile of v7, /device:TPU:1, one launch (start us, length us, event | category | flops | bytes accessed | tf_op | source)
XLA Modules:
  0.0 131.4 jit_solution(15469275967194298018)
XLA Ops:
  0.7 0.0 copy-start.1
  0.7 7.8 %forward.1 = (f32[2,1024]{1,0:T(2,128)S(1)}, bf16[256,1280]{1,0:T(8,128)(2,1)S(1)}) custom-call(s32[1]{0:T(128)} %bitcast.at_ref, bf16[1024,1280]{1,0:T(8,128)(2,1)} %memory_ref.5, bf16[1024,640]{1,0:T(8,128)(2,1)} %hidden_ref.3, bf16[1024,640]{1,0:T(8,128)(2,1)} %grad_ref.3, bf16[1280,640]{1,0:T(8,128)(2,1)} %wk_ref.7, bf16[1280,640]{1,0:T(8,128)(2,1)} %wv_ref.5), custom_call_target="tpu_custom_call" | custom-call | flops 3355443200 | bytes 12582912 | tf_op jit(solution)/shard_map/forward/pallas_call | solution.py:272
  8.5 0.0 copy-start.5
  8.5 3.6 %collective-permute-start.2 = (f32[2,1024]{1,0:T(2,128)S(1)}, f32[2,1024]{1,0:T(2,128)S(1)}, u32[]{:S(2)}, u32[]{:S(2)}) collective-permute-start(f32[2,1024]{1,0:T(2,128)S(1)} %get-tuple-element.70.p0), channel_id=1, source_target_pairs={{0,3},{1,0},{2,1},{3,2},{4,7},{5,4},{6,5},{7,6},{8,11},{9,8},{10,9... | collective-permute-start | bytes 24584 | tf_op jit(solution)/shard_map/ppermute | solution.py:298
  12.1 0.3 collective-permute-start.1
  12.5 0.7 collective-permute-start
  13.2 0.0 collective-permute-done.2.p3
  13.2 3.0 %collective-permute-done.1.p2 = f32[2,1024]{1,0:T(2,128)S(1)} collective-permute-done((f32[2,1024]{1,0:T(2,128)S(1)}, f32[2,1024]{1,0:T(2,128)S(1)}, u32[]{:S(2)}, u32[]{:S(2)}) %collective-permute-start.1) | collective-permute-done | bytes 8224 | tf_op jit(solution)/shard_map/ppermute | solution.py:298
  16.1 0.1 collective-permute-done.p1
  16.2 1.4 %first.1 = f32[256,1280]{1,0:T(8,128)S(1)} custom-call(s32[1]{0:T(128)} %bitcast.at_ref, f32[2,1024]{1,0:T(2,128)S(1)} %get-tuple-element.70.p0, f32[2,1024]{1,0:T(2,128)S(1)} %collective-permute-done.p1, f32[2,1024]{1,0:T(2,128)S(1)} %collective-permute-done.1.p2, f32[2,1024]{1,0:T(2,128)S(1)} %collective-permute-done.2.p3, ...), custom_call_target="tpu_custom_call" | custom-call | flops 838860800 | bytes 6291456 | tf_op jit(solution)/shard_map/first/pallas_call | solution.py:323
  17.6 1.2 fusion
  18.8 0.6 collective-permute-start.3
  19.4 1.4 %collective-permute-start.4 = (f32[128,1280]{1,0:T(8,128)}, f32[128,1280]{1,0:T(8,128)S(1)}, u32[]{:S(2)}, u32[]{:S(2)}) collective-permute-start(f32[128,1280]{1,0:T(8,128)} %get-tuple-element.81), channel_id=1, source_target_pairs={{0,1},{1,2},{2,3},{3,0},{4,7},{5,4},{6,5},{7,6},{8,9},{9,10},{10,1... | collective-permute-start | bytes 1966088 | tf_op jit(solution)/shard_map/ppermute | solution.py:313
  20.8 0.1 pad_add_fusion.1.at_ref
  20.9 0.0 copy-start.3
  20.9 1.3 copy-done.3
  22.2 1.3 %copy-done.4 = bf16[1024,640]{1,0:T(8,128)(2,1)S(1)} copy-done((bf16[1024,640]{1,0:T(8,128)(2,1)S(1)}, bf16[1024,640]{1,0:T(8,128)(2,1)}, u32[]{:S(2)}) %copy-start.4) | copy-done | bytes 1310744
  23.5 0.8 gate.1.both_ref
  24.3 0.1 pad_add_fusion.at_ref
  24.4 0.8 copy-done.2
  25.2 5.3 %weight_grad.1 = (f32[640,1280]{1,0:T(8,128)S(1)}, f32[640,1280]{1,0:T(8,128)S(1)}) custom-call(s32[3]{0:T(128)S(1)} %pad_add_fusion.1.at_ref, bf16[1024,1280]{1,0:T(8,128)(2,1)S(1)} %copy-done.2, bf16[1024,1280]{1,0:T(8,128)(2,1)S(1)} %gate.1.both_ref), custom_call_target="tpu_custom_call" | custom-call | flops 1 | bytes 1 | tf_op jit(solution)/shard_map/weight_grad/pallas_call | solution.py:354
  30.5 2.1 %collective-permute-start.6 = (f32[640,1280]{1,0:T(8,128)S(1)}, f32[640,1280]{1,0:T(8,128)S(1)}, u32[]{:S(2)}, u32[]{:S(2)}) collective-permute-start(f32[640,1280]{1,0:T(8,128)S(1)} %get-tuple-element.49), channel_id=1, source_target_pairs={{0,4},{1,5},{2,6},{3,7},{4,0},{5,1},{6,2},{7,3},{8,12},{9,13},{10,... | collective-permute-start | bytes 9830408 | tf_op jit(solution)/shard_map/ppermute | solution.py:307
  32.6 4.6 %rest.1 = (f32[3,128,1280]{2,1,0:T(8,128)S(1)}, f32[3,128,1280]{2,1,0:T(8,128)S(1)}) custom-call(s32[2]{0:T(128)S(1)} %pad_add_fusion.at_ref, bf16[1024,1280]{1,0:T(8,128)(2,1)S(1)} %gate.1.both_ref, bf16[1280,640]{1,0:T(8,128)(2,1)S(1)} %copy-done.1, bf16[1280,640]{1,0:T(8,128)(2,1)S(1)} %copy-done), custom_call_target="tpu_custom_call" | custom-call | flops 1 | bytes 1 | tf_op jit(solution)/shard_map/rest/pallas_call | solution.py:371
  37.2 0.0 collective-permute-done.3
  37.2 0.0 copy-start.11
  37.3 0.0 copy-start.12
  37.3 1.2 bitcast_add_fusion.5
  38.4 0.0 collective-permute-done.4
  38.4 0.1 bitcast_add_fusion.4
  38.5 1.4 %collective-permute-start.9 = (f32[128,1280]{1,0:T(8,128)S(1)}, f32[128,1280]{1,0:T(8,128)S(1)}, u32[]{:S(2)}, u32[]{:S(2)}) collective-permute-start(f32[128,1280]{1,0:T(8,128)S(1)} %bitcast_add_fusion.5), channel_id=1, source_target_pairs={{0,1},{1,2},{2,3},{3,0},{4,7},{5,4},{6,5},{7,6},{8,9},{9,10},{10,1... | collective-permute-start | bytes 1966088 | tf_op jit(solution)/shard_map/ppermute | solution.py:313
  39.9 2.7 %ranks.1 = (bf16[1024,2048]{1,0:T(8,128)(2,1)S(1)}, f32[2048,128]{1,0:T(8,128)S(1)}, f32[128,128]{1,0:T(8,128)S(1)}) custom-call(s32[2]{0:T(128)S(1)} %pad_add_fusion.at_ref, s32[8,1024]{1,0:T(8,128)S(1)} %bitcast.28, s32[8,1024]{1,0:T(8,128)S(1)} %bitcast.29), custom_call_target="tpu_custom_call" | custom-call | flops 68719476736 | bytes 134217728 | tf_op jit(solution)/shard_map/ranks/pallas_call | solution.py:405
  42.7 0.0 collective-permute-done.6
  42.7 0.4 add.38
  43.1 0.1 slice.58
  43.2 1.7 %collective-permute-start.8 = (f32[320,1280]{1,0:T(8,128)S(1)}, f32[320,1280]{1,0:T(8,128)S(1)}, u32[]{:S(2)}, u32[]{:S(2)}) collective-permute-start(f32[320,1280]{1,0:T(8,128)S(1)} %slice.58), channel_id=1, source_target_pairs={{0,32},{1,33},{2,34},{3,35},{4,12},{5,13},{6,14},{7,15},{8,40},{9,... | collective-permute-start | bytes 4915208 | tf_op jit(solution)/shard_map/ppermute | solution.py:307
  44.9 1.7 %collective-permute-start.5 = (f32[128,1280]{1,0:T(8,128)S(1)}, f32[128,1280]{1,0:T(8,128)S(1)}, u32[]{:S(2)}, u32[]{:S(2)}) collective-permute-start(f32[128,1280]{1,0:T(8,128)S(1)} %bitcast_add_fusion.4), channel_id=1, source_target_pairs={{0,1},{1,2},{2,3},{3,0},{4,7},{5,4},{6,5},{7,6},{8,9},{9,10},{10,1... | collective-permute-start | bytes 1966088 | tf_op jit(solution)/shard_map/ppermute | solution.py:313
  46.6 1.7 %collective-permute-done.9 = f32[128,1280]{1,0:T(8,128)S(1)} collective-permute-done((f32[128,1280]{1,0:T(8,128)S(1)}, f32[128,1280]{1,0:T(8,128)S(1)}, u32[]{:S(2)}, u32[]{:S(2)}) %collective-permute-start.9) | collective-permute-done | bytes 655392 | tf_op jit(solution)/shard_map/ppermute | solution.py:313
  48.3 0.1 bitcast_add_fusion.1
  48.4 2.3 %collective-permute-start.10 = (f32[128,1280]{1,0:T(8,128)S(1)}, f32[128,1280]{1,0:T(8,128)S(1)}, u32[]{:S(2)}, u32[]{:S(2)}) collective-permute-start(f32[128,1280]{1,0:T(8,128)S(1)} %bitcast_add_fusion.1), channel_id=1, source_target_pairs={{0,1},{1,2},{2,3},{3,0},{4,7},{5,4},{6,5},{7,6},{8,9},{9,10},{10,1... | collective-permute-start | bytes 1966088 | tf_op jit(solution)/shard_map/ppermute | solution.py:313
  50.7 4.6 %collective-permute-done.5 = f32[128,1280]{1,0:T(8,128)S(1)} collective-permute-done((f32[128,1280]{1,0:T(8,128)S(1)}, f32[128,1280]{1,0:T(8,128)S(1)}, u32[]{:S(2)}, u32[]{:S(2)}) %collective-permute-start.5) | collective-permute-done | bytes 655392 | tf_op jit(solution)/shard_map/ppermute | solution.py:313
  55.4 0.1 bitcast_add_fusion.3
  55.4 2.5 %collective-permute-start.7 = (f32[128,1280]{1,0:T(8,128)S(1)}, f32[128,1280]{1,0:T(8,128)S(1)}, u32[]{:S(2)}, u32[]{:S(2)}) collective-permute-start(f32[128,1280]{1,0:T(8,128)S(1)} %bitcast_add_fusion.3), channel_id=1, source_target_pairs={{0,1},{1,2},{2,3},{3,0},{4,7},{5,4},{6,5},{7,6},{8,9},{9,10},{10,1... | collective-permute-start | bytes 1966088 | tf_op jit(solution)/shard_map/ppermute | solution.py:313
  57.9 5.8 %collective-permute-done.8 = f32[320,1280]{1,0:T(8,128)S(1)} collective-permute-done((f32[320,1280]{1,0:T(8,128)S(1)}, f32[320,1280]{1,0:T(8,128)S(1)}, u32[]{:S(2)}, u32[]{:S(2)}) %collective-permute-start.8) | collective-permute-done | bytes 1638432 | tf_op jit(solution)/shard_map/ppermute | solution.py:307
  63.7 0.2 slice_add_fusion
  63.9 0.1 slice.63
  64.0 3.7 %collective-permute-start.11 = (f32[160,1280]{1,0:T(8,128)S(1)}, f32[160,1280]{1,0:T(8,128)S(1)}, u32[]{:S(2)}, u32[]{:S(2)}) collective-permute-start(f32[160,1280]{1,0:T(8,128)S(1)} %slice.63), channel_id=1, source_target_pairs={{0,96},{1,97},{2,98},{3,99},{4,28},{5,29},{6,30},{7,31},{8,104},{9... | collective-permute-start | bytes 2457608 | tf_op jit(solution)/shard_map/ppermute | solution.py:307
  67.6 0.0 collective-permute-done.10
  67.6 0.1 bitcast_add_fusion.sum_ref
  67.7 3.3 %pack_top.1.part_ref = f32[5,1024,128]{2,1,0:T(8,128)S(1)} custom-call(f32[128,1280]{1,0:T(8,128)S(1)} %bitcast_add_fusion.sum_ref, bf16[1024,2048]{1,0:T(8,128)(2,1)S(1)} %get-tuple-element.63.select_ref, f32[2048,128]{1,0:T(8,128)S(1)} %get-tuple-element.64.group_ref), custom_call_target="tpu_custom_call" | custom-call | flops 2684354560 | bytes 8388608 | tf_op jit(solution)/shard_map/pack_top/pallas_call | solution.py:446
  71.0 0.1 bitcast_add_fusion.2.sum_ref
  71.1 4.7 %pack_low.1 = f32[5248,128]{1,0:T(8,128)} custom-call(f32[128,1280]{1,0:T(8,128)S(1)} %bitcast_add_fusion.2.sum_ref, bf16[1024,2048]{1,0:T(8,128)(2,1)S(1)} %get-tuple-element.63.select_ref, f32[2048,128]{1,0:T(8,128)S(1)} %get-tuple-element.64.group_ref, f32[5,1024,128]{2,1,0:T(8,128)S(1)} %pack_top.1.part_ref, f32[128,128]{1,0:T(8,128)S(1)} %get-tuple-element.67.sent_ref), custom_call_target="tpu_custom_call" | custom-call | flops 2684354560 | bytes 12582912 | tf_op jit(solution)/shard_map/pack_low/pallas_call | solution.py:457
  75.8 1.9 %collective-permute-done.11 = f32[160,1280]{1,0:T(8,128)S(1)} collective-permute-done((f32[160,1280]{1,0:T(8,128)S(1)}, f32[160,1280]{1,0:T(8,128)S(1)}, u32[]{:S(2)}, u32[]{:S(2)}) %collective-permute-start.11) | collective-permute-done | bytes 819232 | tf_op jit(solution)/shard_map/ppermute | solution.py:307
  77.7 1.0 slice_add_fusion.1
  78.6 10.8 %all-to-all-start = ((f32[128,1,5248]{2,1,0:T(1,128)}), f32[128,1,5248]{2,1,0:T(1,128)S(1)}, u32[]{:S(2)}, u32[]{:S(2)}) async-start(f32[128,1,5248]{2,1,0:T(1,128)} %bitcast.13), calls=%async_computation | async-start | bytes 5373952 | tf_op jit(solution)/shard_map/all_to_all | solution.py:483
  89.4 2.1 %fusion.1 = (f32[40,1280]{1,0:T(8,128)}, f32[40,1280]{1,0:T(8,128)}, f32[40,1280]{1,0:T(8,128)}, f32[40,1280]{1,0:T(8,128)S(1)}) fusion(f32[160,1280]{1,0:T(8,128)} %slice_add_fusion.1), kind=kLoop, calls=%fused_computation.11 | loop fusion | bytes 1638400 | tf_op jit(solution)/shard_map/slice | solution.py:492
  91.5 2.9 %collective-permute-start.14 = (f32[40,1280]{1,0:T(8,128)}, f32[40,1280]{1,0:T(8,128)}, u32[]{:S(2)}, u32[]{:S(2)}) collective-permute-start(f32[40,1280]{1,0:T(8,128)} %get-tuple-element.83), channel_id=1, source_target_pairs={{0,16},{1,17},{2,18},{3,19},{4,68},{5,69},{6,70},{7,71},{8,24},{9,... | collective-permute-start | bytes 614408 | tf_op jit(solution)/shard_map/ppermute | solution.py:307
  94.4 0.3 collective-permute-start.13
  94.7 0.6 collective-permute-start.12
  95.3 5.8 %hidden_grad.1 = bf16[1024,640]{1,0:T(8,128)(2,1)} custom-call(f32[2,1024]{1,0:T(2,128)} %copy-done.5, f32[2,1024]{1,0:T(2,128)} %copy-done.8, f32[2,1024]{1,0:T(2,128)} %copy-done.7, f32[2,1024]{1,0:T(2,128)} %copy-done.6, bf16[1024,1280]{1,0:T(8,128)(2,1)} %memory_ref.5, bf16[1280,640]{1,0:T(8,128)(2,1)} %wk_ref.7), custom_call_target="tpu_custom_call" | custom-call | flops 1677721600 | bytes 6291456 | tf_op jit(solution)/shard_map/hidden_grad/pallas_call | solution.py:473
  101.1 26.1 %all-to-all-done = f32[128,1,5248]{2,1,0:T(1,128)S(1)} async-done(((f32[128,1,5248]{2,1,0:T(1,128)}), f32[128,1,5248]{2,1,0:T(1,128)S(1)}, u32[]{:S(2)}, u32[]{:S(2)}) %all-to-all-start) | async-done | bytes 2687008 | tf_op jit(solution)/shard_map/all_to_all | solution.py:483
  127.2 0.0 collective-permute-done.14.b3
  127.2 0.0 collective-permute-done.13.b2
  127.2 0.0 collective-permute-done.12.b1
  127.3 4.2 %update.1 = (f32[160,512]{1,0:T(8,128)}, f32[160,512]{1,0:T(8,128)}, f32[40,640]{1,0:T(8,128)}, f32[40,640]{1,0:T(8,128)}) custom-call(f32[5248,128]{1,0:T(8,128)S(1)} %bitcast.25, f32[160,512]{1,0:T(8,128)S(1)} %bitcast.26, f32[160,512]{1,0:T(8,128)S(1)} %bitcast.27, f32[40,1280]{1,0:T(8,128)S(1)} %get-tuple-element.86.b0, ...), custom_call_target="tpu_custom_call" | custom-call | flops 1342177280 | bytes 5242880 | tf_op jit(solution)/shard_map/update/pallas_call | solution.py:498
  (19 shorter events, 0.0 us)
Async XLA Ops:
  0.6 15.6 %copy-start = (bf16[1280,640]{1,0:T(8,128)(2,1)S(1)}, bf16[1280,640]{1,0:T(8,128)(2,1)}, u32[]{:S(2)}) copy-start(bf16[1280,640]{1,0:T(8,128)(2,1)} %wv_ref.5) | copy-start | bytes 4915204
  0.7 15.6 %copy-start.1 = (bf16[1280,640]{1,0:T(8,128)(2,1)S(1)}, bf16[1280,640]{1,0:T(8,128)(2,1)}, u32[]{:S(2)}) copy-start(bf16[1280,640]{1,0:T(8,128)(2,1)} %wk_ref.7) | copy-start | bytes 4915204
  8.5 12.3 %copy-start.5 = (f32[2,1024]{1,0:T(2,128)}, f32[2,1024]{1,0:T(2,128)S(1)}, u32[]{:S(2)}) copy-start(f32[2,1024]{1,0:T(2,128)S(1)} %get-tuple-element.70.p0) | copy-start | bytes 24580
  8.5 4.7 %collective-permute-start.2 = (f32[2,1024]{1,0:T(2,128)S(1)}, f32[2,1024]{1,0:T(2,128)S(1)}, u32[]{:S(2)}, u32[]{:S(2)}) collective-permute-start(f32[2,1024]{1,0:T(2,128)S(1)} %get-tuple-element.70.p0), channel_id=1, source_target_pairs={{0,3},{1,0},{2,1},{3,2},{4,7},{5,4},{6,5},{7,6},{8,11},{9,8},{10,9... | collective-permute-start | bytes 24584 | tf_op jit(solution)/shard_map/ppermute | solution.py:298
  12.1 4.0 %collective-permute-start.1 = (f32[2,1024]{1,0:T(2,128)S(1)}, f32[2,1024]{1,0:T(2,128)S(1)}, u32[]{:S(2)}, u32[]{:S(2)}) collective-permute-start(f32[2,1024]{1,0:T(2,128)S(1)} %get-tuple-element.70.p0), channel_id=1, source_target_pairs={{0,2},{1,3},{2,0},{3,1},{4,6},{5,7},{6,4},{7,5},{8,10},{9,11},{10,... | collective-permute-start | bytes 24584 | tf_op jit(solution)/shard_map/ppermute | solution.py:298
  12.5 3.7 %collective-permute-start = (f32[2,1024]{1,0:T(2,128)S(1)}, f32[2,1024]{1,0:T(2,128)S(1)}, u32[]{:S(2)}, u32[]{:S(2)}) collective-permute-start(f32[2,1024]{1,0:T(2,128)S(1)} %get-tuple-element.70.p0), channel_id=1, source_target_pairs={{0,1},{1,2},{2,3},{3,0},{4,5},{5,6},{6,7},{7,4},{8,9},{9,10},{10,1... | collective-permute-start | bytes 24584 | tf_op jit(solution)/shard_map/ppermute | solution.py:298
  13.2 7.7 %copy-start.6 = (f32[2,1024]{1,0:T(2,128)}, f32[2,1024]{1,0:T(2,128)S(1)}, u32[]{:S(2)}) copy-start(f32[2,1024]{1,0:T(2,128)S(1)} %collective-permute-done.2.p3) | copy-start | bytes 24580
  16.1 4.7 %copy-start.7 = (f32[2,1024]{1,0:T(2,128)}, f32[2,1024]{1,0:T(2,128)S(1)}, u32[]{:S(2)}) copy-start(f32[2,1024]{1,0:T(2,128)S(1)} %collective-permute-done.1.p2) | copy-start | bytes 24580
  16.2 4.6 %copy-start.8 = (f32[2,1024]{1,0:T(2,128)}, f32[2,1024]{1,0:T(2,128)S(1)}, u32[]{:S(2)}) copy-start(f32[2,1024]{1,0:T(2,128)S(1)} %collective-permute-done.p1) | copy-start | bytes 24580
  18.8 18.4 %collective-permute-start.3 = (f32[128,1280]{1,0:T(8,128)}, f32[128,1280]{1,0:T(8,128)}, u32[]{:S(2)}, u32[]{:S(2)}) collective-permute-start(f32[128,1280]{1,0:T(8,128)} %get-tuple-element.82), channel_id=1, source_target_pairs={{0,1},{1,2},{2,3},{3,0},{4,7},{5,4},{6,5},{7,6},{8,9},{9,10},{10,1... | collective-permute-start | bytes 1966088 | tf_op jit(solution)/shard_map/ppermute | solution.py:313
  19.4 19.1 %collective-permute-start.4 = (f32[128,1280]{1,0:T(8,128)}, f32[128,1280]{1,0:T(8,128)S(1)}, u32[]{:S(2)}, u32[]{:S(2)}) collective-permute-start(f32[128,1280]{1,0:T(8,128)} %get-tuple-element.81), channel_id=1, source_target_pairs={{0,1},{1,2},{2,3},{3,0},{4,7},{5,4},{6,5},{7,6},{8,9},{9,10},{10,1... | collective-permute-start | bytes 1966088 | tf_op jit(solution)/shard_map/ppermute | solution.py:313
  20.9 1.3 %copy-start.3 = (bf16[1024,640]{1,0:T(8,128)(2,1)S(1)}, bf16[1024,640]{1,0:T(8,128)(2,1)}, u32[]{:S(2)}) copy-start(bf16[1024,640]{1,0:T(8,128)(2,1)} %hidden_ref.3) | copy-start | bytes 3932164
  22.2 1.3 %copy-start.4 = (bf16[1024,640]{1,0:T(8,128)(2,1)S(1)}, bf16[1024,640]{1,0:T(8,128)(2,1)}, u32[]{:S(2)}) copy-start(bf16[1024,640]{1,0:T(8,128)(2,1)} %grad_ref.3) | copy-start | bytes 3932164
  23.5 1.7 %copy-start.2 = (bf16[1024,1280]{1,0:T(8,128)(2,1)S(1)}, bf16[1024,1280]{1,0:T(8,128)(2,1)}, u32[]{:S(2)}) copy-start(bf16[1024,1280]{1,0:T(8,128)(2,1)} %memory_ref.5) | copy-start | bytes 7864324
  30.5 12.2 %collective-permute-start.6 = (f32[640,1280]{1,0:T(8,128)S(1)}, f32[640,1280]{1,0:T(8,128)S(1)}, u32[]{:S(2)}, u32[]{:S(2)}) collective-permute-start(f32[640,1280]{1,0:T(8,128)S(1)} %get-tuple-element.49), channel_id=1, source_target_pairs={{0,4},{1,5},{2,6},{3,7},{4,0},{5,1},{6,2},{7,3},{8,12},{9,13},{10,... | collective-permute-start | bytes 9830408 | tf_op jit(solution)/shard_map/ppermute | solution.py:307
  37.2 2.7 %copy-start.11 = (s32[1024,8]{0,1:T(8,128)S(1)}, s32[1024,8]{0,1:T(8,128)}, u32[]{:S(2)}) copy-start(s32[1024,8]{0,1:T(8,128)} %param.14) | copy-start | bytes 98308
  37.3 2.7 %copy-start.12 = (s32[1024,8]{0,1:T(8,128)S(1)}, s32[1024,8]{0,1:T(8,128)}, u32[]{:S(2)}) copy-start(s32[1024,8]{0,1:T(8,128)} %param.15) | copy-start | bytes 98308
  38.5 9.8 %collective-permute-start.9 = (f32[128,1280]{1,0:T(8,128)S(1)}, f32[128,1280]{1,0:T(8,128)S(1)}, u32[]{:S(2)}, u32[]{:S(2)}) collective-permute-start(f32[128,1280]{1,0:T(8,128)S(1)} %bitcast_add_fusion.5), channel_id=1, source_target_pairs={{0,1},{1,2},{2,3},{3,0},{4,7},{5,4},{6,5},{7,6},{8,9},{9,10},{10,1... | collective-permute-start | bytes 1966088 | tf_op jit(solution)/shard_map/ppermute | solution.py:313
  43.2 20.5 %collective-permute-start.8 = (f32[320,1280]{1,0:T(8,128)S(1)}, f32[320,1280]{1,0:T(8,128)S(1)}, u32[]{:S(2)}, u32[]{:S(2)}) collective-permute-start(f32[320,1280]{1,0:T(8,128)S(1)} %slice.58), channel_id=1, source_target_pairs={{0,32},{1,33},{2,34},{3,35},{4,12},{5,13},{6,14},{7,15},{8,40},{9,... | collective-permute-start | bytes 4915208 | tf_op jit(solution)/shard_map/ppermute | solution.py:307
  44.9 10.4 %collective-permute-start.5 = (f32[128,1280]{1,0:T(8,128)S(1)}, f32[128,1280]{1,0:T(8,128)S(1)}, u32[]{:S(2)}, u32[]{:S(2)}) collective-permute-start(f32[128,1280]{1,0:T(8,128)S(1)} %bitcast_add_fusion.4), channel_id=1, source_target_pairs={{0,1},{1,2},{2,3},{3,0},{4,7},{5,4},{6,5},{7,6},{8,9},{9,10},{10,1... | collective-permute-start | bytes 1966088 | tf_op jit(solution)/shard_map/ppermute | solution.py:313
  48.4 19.2 %collective-permute-start.10 = (f32[128,1280]{1,0:T(8,128)S(1)}, f32[128,1280]{1,0:T(8,128)S(1)}, u32[]{:S(2)}, u32[]{:S(2)}) collective-permute-start(f32[128,1280]{1,0:T(8,128)S(1)} %bitcast_add_fusion.1), channel_id=1, source_target_pairs={{0,1},{1,2},{2,3},{3,0},{4,7},{5,4},{6,5},{7,6},{8,9},{9,10},{10,1... | collective-permute-start | bytes 1966088 | tf_op jit(solution)/shard_map/ppermute | solution.py:313
  55.4 15.6 %collective-permute-start.7 = (f32[128,1280]{1,0:T(8,128)S(1)}, f32[128,1280]{1,0:T(8,128)S(1)}, u32[]{:S(2)}, u32[]{:S(2)}) collective-permute-start(f32[128,1280]{1,0:T(8,128)S(1)} %bitcast_add_fusion.3), channel_id=1, source_target_pairs={{0,1},{1,2},{2,3},{3,0},{4,7},{5,4},{6,5},{7,6},{8,9},{9,10},{10,1... | collective-permute-start | bytes 1966088 | tf_op jit(solution)/shard_map/ppermute | solution.py:313
  64.0 13.7 %collective-permute-start.11 = (f32[160,1280]{1,0:T(8,128)S(1)}, f32[160,1280]{1,0:T(8,128)S(1)}, u32[]{:S(2)}, u32[]{:S(2)}) collective-permute-start(f32[160,1280]{1,0:T(8,128)S(1)} %slice.63), channel_id=1, source_target_pairs={{0,96},{1,97},{2,98},{3,99},{4,28},{5,29},{6,30},{7,31},{8,104},{9... | collective-permute-start | bytes 2457608 | tf_op jit(solution)/shard_map/ppermute | solution.py:307
  78.6 48.6 %all-to-all-start = ((f32[128,1,5248]{2,1,0:T(1,128)}), f32[128,1,5248]{2,1,0:T(1,128)S(1)}, u32[]{:S(2)}, u32[]{:S(2)}) async-start(f32[128,1,5248]{2,1,0:T(1,128)} %bitcast.13), calls=%async_computation | async-start | bytes 5373952 | tf_op jit(solution)/shard_map/all_to_all | solution.py:483
  91.5 35.7 %collective-permute-start.14 = (f32[40,1280]{1,0:T(8,128)}, f32[40,1280]{1,0:T(8,128)}, u32[]{:S(2)}, u32[]{:S(2)}) collective-permute-start(f32[40,1280]{1,0:T(8,128)} %get-tuple-element.83), channel_id=1, source_target_pairs={{0,16},{1,17},{2,18},{3,19},{4,68},{5,69},{6,70},{7,71},{8,24},{9,... | collective-permute-start | bytes 614408 | tf_op jit(solution)/shard_map/ppermute | solution.py:307
  94.4 32.8 %collective-permute-start.13 = (f32[40,1280]{1,0:T(8,128)}, f32[40,1280]{1,0:T(8,128)}, u32[]{:S(2)}, u32[]{:S(2)}) collective-permute-start(f32[40,1280]{1,0:T(8,128)} %get-tuple-element.84), channel_id=1, source_target_pairs={{0,8},{1,9},{2,10},{3,11},{4,36},{5,37},{6,38},{7,39},{8,0},{9,1},... | collective-permute-start | bytes 614408 | tf_op jit(solution)/shard_map/ppermute | solution.py:307
  94.7 32.6 %copy-start.9 = (f32[512,160]{0,1:T(8,128)S(1)}, f32[512,160]{0,1:T(8,128)}, u32[]{:S(2)}) copy-start(f32[512,160]{0,1:T(8,128)} %param.16) | copy-start | bytes 983044
  94.7 32.6 %copy-start.10 = (f32[512,160]{0,1:T(8,128)S(1)}, f32[512,160]{0,1:T(8,128)}, u32[]{:S(2)}) copy-start(f32[512,160]{0,1:T(8,128)} %param.17) | copy-start | bytes 983044
  94.7 32.5 %collective-permute-start.12 = (f32[40,1280]{1,0:T(8,128)}, f32[40,1280]{1,0:T(8,128)}, u32[]{:S(2)}, u32[]{:S(2)}) collective-permute-start(f32[40,1280]{1,0:T(8,128)} %get-tuple-element.85), channel_id=1, source_target_pairs={{0,24},{1,25},{2,26},{3,27},{4,100},{5,101},{6,102},{7,103},{8,16}... | collective-permute-start | bytes 614408 | tf_op jit(solution)/shard_map/ppermute | solution.py:307
